TPU v7x, 32 devices: a whole 2x2x4 slice. The times are simulated.
32 devices in a mesh: dp: 16 (over z, y, core), tensor: 2 (over x).
Axes of the slice: x: 2, y: 2, z: 4, core: 2. Of those that a mesh axis runs over, the one named last changes fastest.
Arguments:
- block_input: bfloat16 [16384, 1024], P(('dp', 'tensor'))
- positions: int32 [16384], P('dp'), may hold values from 0 to 1023, as said below
- expert_ids: int32 [16384, 8], P('dp'), may hold values from 0 to 31, all different within a row
- attn_gain: float32 [1024], replicated, may hold values from 0.1 to 1.9
- query_weight: bfloat16 [1024, 1024], P('dp', 'tensor'), may hold values from -2 to 2
- kv_weight: bfloat16 [1024, 8, 128], P('dp', 'tensor'), may hold values from -0.1875 to 0.1875
- out_weight: bfloat16 [1024, 1024], P('tensor', 'dp'), may hold values from -6 to 6
- ffn_gain: float32 [1024], replicated, may hold values from 0.1 to 1.9
- router_weight: bfloat16 [1024, 32], replicated, may hold values from -0.09375 to 0.09375
- gate_weight: bfloat16 [32, 1024, 512], P('tensor', 'dp'), may hold values from -0.1875 to 0.1875
- up_weight: bfloat16 [32, 1024, 512], P('tensor', 'dp'), may hold values from -0.1875 to 0.1875
- down_weight: bfloat16 [32, 512, 1024], P('tensor', 'dp'), may hold values from -4 to 4
- out_grad: bfloat16 [16384, 1024], P(('dp', 'tensor')), may hold values from -6 to 6
Outputs:
- block_output: bfloat16 [16384, 1024], P(('dp', 'tensor'))
- input_grad: bfloat16 [16384, 1024], P(('dp', 'tensor'))
- attn_gain_grad: float32 [1024], replicated
- query_grad: float32 [1024, 1024], P('dp', 'tensor')
- kv_grad: float32 [1024, 8, 128], P('dp', 'tensor')
- out_weight_grad: float32 [1024, 1024], P('tensor', 'dp')
- ffn_gain_grad: float32 [1024], replicated
- router_grad: float32 [1024, 32], replicated
- gate_grad: float32 [32, 1024, 512], P('tensor', 'dp')
- up_grad: float32 [32, 1024, 512], P('tensor', 'dp')
- down_grad: float32 [32, 512, 1024], P('tensor', 'dp')
Inputs may be any that keep to these rules, and one draw needn't show every extreme that they name: `expert_ids`: each row names 8 different experts. Within each sequence of 1024 tokens, positions count up by one from 0 at the first token of each packed document; every sequence's first token begins a document, and the first sequence is one whole document.
All inputs are finite; a program needn't handle non-finite values.
Results may differ from a plain program's by a relative error of at most 0.02.
Values may be sent and summed in bfloat16 or wider, within the bound.
No kernel may reach another device: no remote copies, remote signals or barrier semaphores. Data moves between devices by JAX's collectives and lax.ppermute only.
A program may use at most 320 MiB of HBM per device.

v0:
```python
import jax
import jax.numpy as jnp
from jax import lax
from jax.sharding import PartitionSpec as P

CAP = 320


norm_eps = 1e-06
attn_scale = 0.015625
residual_scale = 0.22
rope_base = 10000.0
masked_score = -1e30


def row_scale(values):
    return lax.rsqrt(jnp.mean(values * values, axis=-1, keepdims=True) + norm_eps)


def rotary(values, positions, direction):
    head_dim = values.shape[-1]
    half_dim = head_dim // 2
    frequency = rope_base ** (-(jnp.arange(half_dim, dtype=jnp.float32) * 2.0 / head_dim))
    angles = positions.astype(jnp.float32)[:, None] * frequency[None, :]
    cosine = jnp.concatenate([jnp.cos(angles), jnp.cos(angles)], axis=-1)[:, None, :]
    sine_table = jnp.concatenate([jnp.sin(angles), jnp.sin(angles)], axis=-1)[:, None, :]
    rotated = jnp.concatenate([-values[..., half_dim:], values[..., :half_dim]], axis=-1)
    return values * cosine + direction * rotated * sine_table


def contract(left, right, left_dim, right_dim):
    return lax.dot_general(
        left, right, (((left_dim,), (right_dim,)), ((), ())), preferred_element_type=jnp.float32
    )


def norm_backward(normed_grad, source, gain):
    scale_rows = row_scale(source)
    unit_rows = source * scale_rows
    scaled_grad = normed_grad * gain
    gain_grad = jnp.sum(normed_grad * unit_rows, axis=0)
    source_grad = scale_rows * (
        scaled_grad - unit_rows * jnp.mean(scaled_grad * unit_rows, axis=-1, keepdims=True)
    )
    return (source_grad, gain_grad)


def block_scores(q_block, keys, first_row):
    block_rows = q_block.shape[0]
    scores = (
        jnp.einsum("bgrd,sgd->grbs", q_block, keys, preferred_element_type=jnp.float32) * attn_scale
    )
    row_pos = first_row + jnp.arange(block_rows)
    key_pos = jnp.arange(keys.shape[0])
    return jnp.where(
        key_pos[None, None, None, :] <= row_pos[None, None, :, None], scores, masked_score
    )


def attention_forward(query, keys, values_in):
    seq_len = query.shape[0]
    block_rows = min(512, seq_len)

    def one_block(state_in, first_row):
        q_block = lax.dynamic_slice_in_dim(query, first_row, block_rows, 0)
        scores = block_scores(q_block, keys, first_row)
        top_score = jnp.max(scores, axis=-1, keepdims=True)
        log_total = top_score + jnp.log(
            jnp.sum(jnp.exp(scores - top_score), axis=-1, keepdims=True)
        )
        prob_vals = jnp.exp(scores - log_total).astype(jnp.bfloat16)
        blended = jnp.einsum(
            "grbs,sgd->bgrd", prob_vals, values_in, preferred_element_type=jnp.float32
        )
        return (state_in, (blended.astype(jnp.bfloat16), log_total))

    starts = jnp.arange(seq_len // block_rows) * block_rows
    _, (blended, log_totals) = lax.scan(one_block, 0, starts)
    return (blended.reshape(seq_len, -1), log_totals)


def attention_backward(query, keys, values_in, log_totals, mixed_grad):
    seq_len = query.shape[0]
    block_rows = min(512, seq_len)

    def one_block(state_in, step_items):
        key_grad, value_grad = state_in
        first_row, log_total = step_items
        q_block = lax.dynamic_slice_in_dim(query, first_row, block_rows, 0)
        g_block = lax.dynamic_slice_in_dim(mixed_grad, first_row, block_rows, 0)
        scores = block_scores(q_block, keys, first_row)
        prob_vals = jnp.exp(scores - log_total)
        prob_grad = jnp.einsum(
            "bgrd,sgd->grbs", g_block, values_in, preferred_element_type=jnp.float32
        )
        row_dot = jnp.sum(prob_vals * prob_grad, axis=-1, keepdims=True)
        score_grad = (prob_vals * (prob_grad - row_dot)).astype(jnp.bfloat16)
        query_grad = (
            jnp.einsum("grbs,sgd->bgrd", score_grad, keys, preferred_element_type=jnp.float32)
            * attn_scale
        )
        key_grad = (
            key_grad
            + jnp.einsum("grbs,bgrd->sgd", score_grad, q_block, preferred_element_type=jnp.float32)
            * attn_scale
        )
        value_grad = value_grad + jnp.einsum(
            "grbs,bgrd->sgd",
            prob_vals.astype(jnp.bfloat16),
            g_block,
            preferred_element_type=jnp.float32,
        )
        return ((key_grad, value_grad), query_grad)

    zero_keys = jnp.zeros(keys.shape, jnp.float32)
    starts = jnp.arange(seq_len // block_rows) * block_rows
    (key_grad, value_grad), query_grad = lax.scan(
        one_block, (zero_keys, zero_keys), (starts, log_totals)
    )
    return (query_grad.reshape(query.shape), key_grad, value_grad)


def slot_table(expert_ids, rank_local, expert_now, gate_vals):
    owner_hits = (expert_ids == expert_now) & (rank_local < CAP)
    slot_code = jnp.sum(jnp.where(owner_hits, rank_local + 1, 0), axis=1) - 1
    slot_match = jnp.arange(CAP)[:, None] == slot_code[None, :]
    token_gate = jnp.sum(jnp.where(owner_hits, gate_vals, 0.0), axis=1)
    slot_gate = jnp.sum(jnp.where(slot_match, token_gate[None, :], 0.0), axis=1)
    return (owner_hits, slot_match, slot_gate)


def shards(
    block_input,
    positions,
    expert_ids,
    attn_gain,
    query_weight,
    kv_weight,
    out_weight,
    ffn_gain,
    router_weight,
    gate_weight,
    up_weight,
    down_weight,
    out_grad,
):
    query_full, kv_full, out_full = (
        lax.all_gather(query_weight, "dp", axis=0, tiled=True),
        lax.all_gather(kv_weight, "dp", axis=0, tiled=True),
        lax.all_gather(out_weight, "dp", axis=1, tiled=True),
    )
    input_rows = block_input.astype(jnp.float32)
    attn_normed = (input_rows * row_scale(input_rows) * attn_gain).astype(jnp.bfloat16)
    attn_tokens = lax.all_gather(attn_normed, "tensor", axis=0, tiled=True)
    seq_len = attn_tokens.shape[0]
    kv_local = kv_full.shape[1]
    head_dim = kv_full.shape[2] // 2
    heads_local = query_full.shape[1] // head_dim
    query_pre = jnp.dot(attn_tokens, query_full, preferred_element_type=jnp.float32).reshape(
        seq_len, heads_local, head_dim
    )
    kv_pre = jnp.einsum("sd,dgk->sgk", attn_tokens, kv_full, preferred_element_type=jnp.float32)
    query_rot = (
        rotary(query_pre, positions, 1.0)
        .astype(jnp.bfloat16)
        .reshape(seq_len, kv_local, heads_local // kv_local, head_dim)
    )
    key_rot = rotary(kv_pre[..., :head_dim], positions, 1.0).astype(jnp.bfloat16)
    value_low = kv_pre[..., head_dim:].astype(jnp.bfloat16)
    attn_mixed, log_totals = attention_forward(query_rot, key_rot, value_low)
    attn_out = lax.psum_scatter(
        jnp.dot(attn_mixed, out_full, preferred_element_type=jnp.float32),
        "tensor",
        scatter_dimension=0,
        tiled=True,
    )
    hidden_state = input_rows + residual_scale * attn_out
    ffn_normed = (hidden_state * row_scale(hidden_state) * ffn_gain).astype(jnp.bfloat16)
    ffn_tokens = lax.all_gather(ffn_normed, "tensor", axis=0, tiled=True)
    gate_full, up_full, down_full = (
        lax.all_gather(gate_weight, "dp", axis=1, tiled=True),
        lax.all_gather(up_weight, "dp", axis=1, tiled=True),
        lax.all_gather(down_weight, "dp", axis=1, tiled=True),
    )
    expert_count = router_weight.shape[1]
    logits = jnp.dot(ffn_tokens, router_weight, preferred_element_type=jnp.float32)
    id_match = expert_ids[:, :, None] == jnp.arange(expert_count)[None, None, :]
    selected = jnp.sum(jnp.where(id_match, logits[:, None, :], 0.0), axis=2)
    top_logit = jnp.max(selected, axis=1, keepdims=True)
    raised = jnp.exp(selected - top_logit)
    gate_vals = raised / jnp.sum(raised, axis=1, keepdims=True)
    experts_local = gate_full.shape[0]
    expert_first = lax.axis_index("tensor") * experts_local
    local_ids = expert_first + jnp.arange(experts_local)
    flat_hits = (expert_ids.reshape(-1)[:, None] == local_ids[None, :]).astype(jnp.int32)
    rank_local = jnp.sum((jnp.cumsum(flat_hits, axis=0) - flat_hits) * flat_hits, axis=1).reshape(
        expert_ids.shape
    )

    def expert_forward(moe_total, step_items):
        expert_now, w_gate, w_up, w_down = step_items
        owner_hits, slot_match, slot_gate = slot_table(
            expert_ids, rank_local, expert_now, gate_vals
        )
        dispatch_low = slot_match.astype(jnp.bfloat16)
        expert_in = jnp.dot(dispatch_low, ffn_tokens, preferred_element_type=jnp.float32).astype(
            jnp.bfloat16
        )
        gate_pre = jnp.dot(expert_in, w_gate, preferred_element_type=jnp.float32)
        up_pre = jnp.dot(expert_in, w_up, preferred_element_type=jnp.float32)
        hidden_act = (jax.nn.silu(gate_pre) * up_pre).astype(jnp.bfloat16)
        expert_out = jnp.dot(hidden_act, w_down, preferred_element_type=jnp.float32)
        weighted = (slot_gate[:, None] * expert_out).astype(jnp.bfloat16)
        moe_total = moe_total + contract(dispatch_low, weighted, 0, 0)
        return (moe_total, (expert_in, gate_pre, up_pre, hidden_act, expert_out))

    moe_zero = jnp.zeros((seq_len, ffn_tokens.shape[1]), jnp.float32)
    moe_total, expert_saved = lax.scan(
        expert_forward, moe_zero, (local_ids, gate_full, up_full, down_full)
    )
    moe_out = lax.psum_scatter(
        moe_total.astype(jnp.bfloat16), "tensor", scatter_dimension=0, tiled=True
    ).astype(jnp.float32)
    block_output = (hidden_state + residual_scale * moe_out).astype(jnp.bfloat16)
    grad_rows = out_grad.astype(jnp.float32)
    moe_grad = lax.all_gather(
        (residual_scale * grad_rows).astype(jnp.bfloat16), "tensor", axis=0, tiled=True
    )
    gate_back, up_back, down_back = (
        lax.all_gather(gate_weight, "dp", axis=1, tiled=True),
        lax.all_gather(up_weight, "dp", axis=1, tiled=True),
        lax.all_gather(down_weight, "dp", axis=1, tiled=True),
    )

    def expert_backward(state_in, step_items):
        normed_grad, pair_grad = state_in
        expert_now, w_gate, w_up, w_down, expert_in, gate_pre, up_pre, hidden_act, expert_out = (
            step_items
        )
        owner_hits, slot_match, slot_gate = slot_table(
            expert_ids, rank_local, expert_now, gate_vals
        )
        dispatch_low = slot_match.astype(jnp.bfloat16)
        slot_grad = jnp.dot(dispatch_low, moe_grad, preferred_element_type=jnp.float32)
        slot_gate_grad = jnp.sum(slot_grad * expert_out, axis=1)
        out_slot_grad = (slot_gate[:, None] * slot_grad).astype(jnp.bfloat16)
        down_step = contract(hidden_act, out_slot_grad, 0, 0)
        hidden_grad = contract(out_slot_grad, w_down, 1, 1)
        sigmoid_gate = jax.nn.sigmoid(gate_pre)
        gate_pre_grad = (
            hidden_grad * up_pre * sigmoid_gate * (1.0 + gate_pre * (1.0 - sigmoid_gate))
        ).astype(jnp.bfloat16)
        up_pre_grad = (hidden_grad * gate_pre * sigmoid_gate).astype(jnp.bfloat16)
        gate_step = contract(expert_in, gate_pre_grad, 0, 0)
        up_step = contract(expert_in, up_pre_grad, 0, 0)
        in_grad = (
            contract(gate_pre_grad, w_gate, 1, 1) + contract(up_pre_grad, w_up, 1, 1)
        ).astype(jnp.bfloat16)
        normed_grad = normed_grad + contract(dispatch_low, in_grad, 0, 0)
        token_gate_grad = jnp.sum(jnp.where(slot_match, slot_gate_grad[:, None], 0.0), axis=0)
        pair_grad = pair_grad + jnp.where(owner_hits, token_gate_grad[:, None], 0.0)
        return ((normed_grad, pair_grad), (gate_step, up_step, down_step))

    pair_zero = jnp.zeros(gate_vals.shape, jnp.float32)
    (normed_grad, pair_grad), (gate_part, up_part, down_part) = lax.scan(
        expert_backward,
        (moe_zero, pair_zero),
        (local_ids, gate_back, up_back, down_back) + expert_saved,
    )
    sel_grad = gate_vals * (pair_grad - jnp.sum(gate_vals * pair_grad, axis=1, keepdims=True))
    logit_part = jnp.sum(jnp.where(id_match, sel_grad[:, :, None], 0.0), axis=1)
    normed_local, logit_local = (
        lax.psum_scatter(
            normed_grad.astype(jnp.bfloat16), "tensor", scatter_dimension=0, tiled=True
        ).astype(jnp.float32),
        lax.psum_scatter(
            logit_part.astype(jnp.bfloat16), "tensor", scatter_dimension=0, tiled=True
        ).astype(jnp.float32),
    )
    logit_low = logit_local.astype(jnp.bfloat16)
    normed_local = normed_local + contract(logit_low, router_weight, 1, 1)
    router_part = contract(ffn_normed, logit_low, 0, 0)
    state_grad, ffn_gain_part = norm_backward(normed_local, hidden_state, ffn_gain)
    state_grad = state_grad + grad_rows
    attn_grad_all = lax.all_gather(
        (residual_scale * state_grad).astype(jnp.bfloat16), "tensor", axis=0, tiled=True
    )
    query_back, kv_back, out_back = (
        lax.all_gather(query_weight, "dp", axis=0, tiled=True),
        lax.all_gather(kv_weight, "dp", axis=0, tiled=True),
        lax.all_gather(out_weight, "dp", axis=1, tiled=True),
    )
    out_part = contract(attn_mixed, attn_grad_all, 0, 0)
    mixed_grad = (
        contract(attn_grad_all, out_back, 1, 1).astype(jnp.bfloat16).reshape(query_rot.shape)
    )
    query_grad, key_grad, value_grad = attention_backward(
        query_rot, key_rot, value_low, log_totals, mixed_grad
    )
    query_pre_grad = (
        rotary(query_grad.reshape(seq_len, heads_local, head_dim), positions, -1.0)
        .astype(jnp.bfloat16)
        .reshape(seq_len, heads_local * head_dim)
    )
    kv_pre_grad = jnp.concatenate([rotary(key_grad, positions, -1.0), value_grad], axis=-1).astype(
        jnp.bfloat16
    )
    query_part = contract(attn_tokens, query_pre_grad, 0, 0)
    kv_part = jnp.einsum(
        "sd,sgk->dgk", attn_tokens, kv_pre_grad, preferred_element_type=jnp.float32
    )
    kv_flat_grad = kv_pre_grad.reshape(seq_len, -1)
    kv_flat_weight = kv_back.reshape(kv_back.shape[0], -1)
    attn_normed_grad = lax.psum_scatter(
        (
            contract(query_pre_grad, query_back, 1, 1)
            + contract(kv_flat_grad, kv_flat_weight, 1, 1)
        ).astype(jnp.bfloat16),
        "tensor",
        scatter_dimension=0,
        tiled=True,
    ).astype(jnp.float32)
    input_part, attn_gain_part = norm_backward(attn_normed_grad, input_rows, attn_gain)
    input_grad = (state_grad + input_part).astype(jnp.bfloat16)
    query_sum, kv_sum, out_sum, gate_sum, up_sum, down_sum = (
        lax.psum_scatter(
            query_part.astype(jnp.bfloat16), "dp", scatter_dimension=0, tiled=True
        ).astype(jnp.float32),
        lax.psum_scatter(
            kv_part.astype(jnp.bfloat16), "dp", scatter_dimension=0, tiled=True
        ).astype(jnp.float32),
        lax.psum_scatter(
            out_part.astype(jnp.bfloat16), "dp", scatter_dimension=1, tiled=True
        ).astype(jnp.float32),
        lax.psum_scatter(
            gate_part.astype(jnp.bfloat16), "dp", scatter_dimension=1, tiled=True
        ).astype(jnp.float32),
        lax.psum_scatter(
            up_part.astype(jnp.bfloat16), "dp", scatter_dimension=1, tiled=True
        ).astype(jnp.float32),
        lax.psum_scatter(
            down_part.astype(jnp.bfloat16), "dp", scatter_dimension=1, tiled=True
        ).astype(jnp.float32),
    )
    attn_gain_grad, ffn_gain_grad, router_grad = lax.psum(
        (attn_gain_part, ffn_gain_part, router_part), ("dp", "tensor")
    )
    return (
        block_output,
        input_grad,
        attn_gain_grad,
        query_sum,
        kv_sum,
        out_sum,
        ffn_gain_grad,
        router_grad,
        gate_sum,
        up_sum,
        down_sum,
    )


def solution(mesh):
    return jax.shard_map(
        shards,
        mesh=mesh,
        in_specs=(
            P(("dp", "tensor"), None),
            P("dp"),
            P("dp", None),
            P(),
            P("dp", "tensor"),
            P("dp", "tensor", None),
            P("tensor", "dp"),
            P(),
            P(),
            P("tensor", "dp", None),
            P("tensor", "dp", None),
            P("tensor", "dp", None),
            P(("dp", "tensor"), None),
        ),
        out_specs=(
            P(("dp", "tensor"), None),
            P(("dp", "tensor"), None),
            P(),
            P("dp", "tensor"),
            P("dp", "tensor", None),
            P("tensor", "dp"),
            P(),
            P(),
            P("tensor", "dp", None),
            P("tensor", "dp", None),
            P("tensor", "dp", None),
        ),
        check_vma=False,
    )
```

profile of v0, /device:TPU:0, one launch (start us, length us, event | category | flops | bytes accessed | tf_op | source)
XLA Modules:
  0.0 2575.0 jit_solution(12089318440555055701)
XLA Ops:
  16.2 35.2 %all-gather.15.cloned.1.call-done = bf16[1024,4,128]{2,0,1:T(8,128)(2,1)} async-done(((bf16[64,4,128]{2,0,1:T(8,128)(2,1)}), bf16[1024,4,128]{2,0,1:T(8,128)(2,1)}) %all-gather.15.cloned.1.call-update) | async-done | bytes 1048592 | tf_op jit(solution)/shard_map/all_gather | solution.py:149
  51.4 34.2 %all-gather.11.cloned.1.call-done = bf16[1024,1024]{1,0:T(8,128)(2,1)} async-done(((bf16[512,1024]{1,0:T(8,128)(2,1)}), bf16[1024,1024]{1,0:T(8,128)(2,1)}) %all-gather.11.cloned.1.call-update) | async-done | bytes 2097168 | tf_op jit(solution)/shard_map/all_gather | solution.py:154
  90.9 34.8 %all-gather.13.cloned.1.call-done = bf16[1024,512]{1,0:T(8,128)(2,1)} async-done(((bf16[64,512]{1,0:T(8,128)(2,1)}), bf16[1024,512]{1,0:T(8,128)(2,1)}) %all-gather.13.cloned.1.call-update) | async-done | bytes 1048592 | tf_op jit(solution)/shard_map/all_gather | solution.py:148
  131.3 33.3 %while.71 = (s32[]{:T(128)}, bf16[2,512,4,2,64]{1,4,3,2,0:T(8,128)(2,1)S(1)}, f32[2,4,2,512,1]{3,2,1,4,0:T(2,128)S(1)}, s32[2]{0:T(128)S(1)}, bf16[1024,4,2,64]{...) while((s32[]{:T(128)}, ...), condition=%wide.region_4.5_spmd, body=%wide.region_1.4_spmd.sunk | while | flops 1120662016 | bytes 54661280 | solution.py:78
  171.0 53.4 %reduce-scatter.12.cloned.1.call-done = f32[512,1024]{1,0:T(8,128)} async-done(((f32[1024,1024]{1,0:T(8,128)}), f32[512,1024]{1,0:T(8,128)}) %reduce-scatter.12.cloned.1.call-update) | async-done | bytes 2097168 | tf_op jit(solution)/shard_map/reduce_scatter | solution.py:171
  241.4 19.9 all-gather.19.cloned.1.call-done
  264.5 125.5 %all-gather.21.cloned.1.call-done = bf16[16,1024,512]{2,1,0:T(8,128)(2,1)} async-done(((bf16[16,64,512]{2,1,0:T(8,128)(2,1)}), bf16[16,1024,512]{2,1,0:T(8,128)(2,1)}) %all-gather.21.cloned.1.call-update) | async-done | bytes 16777232 | tf_op jit(solution)/shard_map/all_gather | solution.py:181
  390.0 126.8 %all-gather.23.cloned.1.call-done = bf16[16,1024,512]{2,1,0:T(8,128)(2,1)} async-done(((bf16[16,64,512]{2,1,0:T(8,128)(2,1)}), bf16[16,1024,512]{2,1,0:T(8,128)(2,1)}) %all-gather.23.cloned.1.call-update) | async-done | bytes 16777232 | tf_op jit(solution)/shard_map/all_gather | solution.py:182
  516.8 126.8 %all-gather.25.cloned.1.call-done = bf16[16,512,1024]{2,1,0:T(8,128)(2,1)} async-done(((bf16[16,32,1024]{2,1,0:T(8,128)(2,1)}), bf16[16,512,1024]{2,1,0:T(8,128)(2,1)}) %all-gather.25.cloned.1.call-update) | async-done | bytes 16777232 | tf_op jit(solution)/shard_map/all_gather | solution.py:183
  643.7 330.7 %while.72 = (s32[]{:T(128)}, f32[1024,1024]{1,0:T(8,128)}, bf16[16,320,1024]{2,1,0:T(8,128)(2,1)}, f32[16,320,512]{2,1,0:T(8,128)}, f32[16,320,512]{2,1,0:T(8,12...) while((s32[]{:T(128)}, f32[1024,1024]{1,0:T(8,128)}, ...), condition=%wide.region_17.18_spmd.clone, body=%wide.region_13.17_spmd.clone.sunk | while | flops 2354576128 | bytes 27908820 | solution.py:218
  974.4 420.2 %while.73 = (s32[]{:T(128)}, f32[1024,1024]{1,0:T(8,128)}, f32[1024,8]{0,1:T(8,128)}, bf16[16,1024,512]{2,1,0:T(8,128)(2,1)}, bf16[16,1024,512]{2,1,0:T(8,128)(2...) while((s32[]{:T(128)}, f32[1024,1024]{1,0:T(8,128)}, ...), condition=%wide.region_25.26_spmd.clone, body=%wide.region_19.25_spmd.clone.sunk | while | flops 3364673024 | bytes 34287096 | solution.py:265
  1405.3 34.6 %reduce-scatter.16.cloned.1.call-done = bf16[512,1024]{1,0:T(8,128)(2,1)} async-done(((bf16[1024,1024]{1,0:T(8,128)(2,1)}), bf16[512,1024]{1,0:T(8,128)(2,1)}) %reduce-scatter.16.cloned.1.call-update) | async-done | bytes 1048592 | tf_op jit(solution)/shard_map/reduce_scatter | solution.py:273
  1445.7 33.1 %all-gather.29.cloned.1.call-done = bf16[1024,1024]{1,0:T(8,128)(2,1)} async-done(((bf16[512,1024]{1,0:T(8,128)(2,1)}), bf16[1024,1024]{1,0:T(8,128)(2,1)}) %all-gather.29.cloned.1.call-update) | async-done | bytes 2097168 | tf_op jit(solution)/shard_map/all_gather | solution.py:285
  1483.0 159.3 %while.74 = (s32[]{:T(128)}, f32[1024,4,64]{0,2,1:T(8,128)}, f32[1024,4,64]{0,2,1:T(8,128)}, f32[2,512,4,2,64]{1,0,4,3,2:T(2,128)}, s32[2]{0:T(128)S(1)}, /*inde...) while((s32[]{:T(128)}, f32[1024,4,64]{0,2,1:T(8,128)}, ...), condition=%wide.region_33.34_spmd.clone, body=%wide.region_31.33_spmd.clone.sunk | while | flops 2724196864 | bytes 230248848 | solution.py:117
  1485.7 9.4 fusion.237
  1496.2 10.0 fusion.238
  1506.2 15.3 fusion.239
  1528.6 19.6 dynamic_update_slice.106
  1565.2 9.4 fusion.237
  1575.6 10.0 fusion.238
  1585.7 15.3 fusion.239
  1608.1 19.6 dynamic_update_slice.106
  1675.0 30.7 %reduce-scatter.24.cloned.1.call-done = bf16[64,4,128]{2,0,1:T(8,128)(2,1)} async-done(((bf16[1024,4,128]{2,0,1:T(8,128)(2,1)}), bf16[64,4,128]{2,0,1:T(8,128)(2,1)}) %reduce-scatter.24.cloned.1.call-update) | async-done | bytes 65552 | tf_op jit(solution)/shard_map/reduce_scatter | solution.py:329
  1707.2 58.5 %reduce-scatter.26.cloned.1.call-done = bf16[512,64]{0,1:T(8,128)(2,1)} async-done(((bf16[512,1024]{0,1:T(8,128)(2,1)}), bf16[512,64]{0,1:T(8,128)(2,1)}) %reduce-scatter.26.cloned.1.call-update) | async-done | bytes 65552 | tf_op jit(solution)/shard_map/reduce_scatter | solution.py:332
  1767.2 59.3 %reduce-scatter.22.cloned.1.call-done = bf16[64,512]{1,0:T(8,128)(2,1)} async-done(((bf16[1024,512]{1,0:T(8,128)(2,1)}), bf16[64,512]{1,0:T(8,128)(2,1)}) %reduce-scatter.22.cloned.1.call-update) | async-done | bytes 65552 | tf_op jit(solution)/shard_map/reduce_scatter | solution.py:326
  1828.0 32.1 %reduce-scatter.20.cloned.1.call-done = bf16[512,1024]{1,0:T(8,128)(2,1)} async-done(((bf16[1024,1024]{1,0:T(8,128)(2,1)}), bf16[512,1024]{1,0:T(8,128)(2,1)}) %reduce-scatter.20.cloned.1.call-update) | async-done | bytes 1048592 | tf_op jit(solution)/shard_map/reduce_scatter | solution.py:314
  1862.2 32.0 %reduce-scatter.14.cloned.1.call-done = bf16[512,1024]{1,0:T(8,128)(2,1)} async-done(((bf16[1024,1024]{1,0:T(8,128)(2,1)}), bf16[512,1024]{1,0:T(8,128)(2,1)}) %reduce-scatter.14.cloned.1.call-update) | async-done | bytes 1048592 | tf_op jit(solution)/shard_map/reduce_scatter | solution.py:221
  1898.3 39.5 %all-reduce = (f32[1024]{0:T(1024)}, f32[1024]{0:T(1024)}) all-reduce(f32[1024]{0:T(1024)S(1)} %get-tuple-element.792, f32[1024]{0:T(1024)S(1)} %copy-done.51), channel_id=1, replica_groups=mesh['dp'=16,'tensor'=2] {'dp','tensor'}, use_global_device_ids=true, to_apply=%region_37.38 | all-reduce | flops 2048 | bytes 16384 | tf_op jit(solution)/shard_map/psum | solution.py:345
  1937.8 137.8 %reduce-scatter.28.cloned.1.call-done = bf16[16,64,512]{2,1,0:T(8,128)(2,1)} async-done(((bf16[16,1024,512]{2,1,0:T(8,128)(2,1)}), bf16[16,64,512]{2,1,0:T(8,128)(2,1)}) %reduce-scatter.28.cloned.1.call-update) | async-done | bytes 1048592 | tf_op jit(solution)/shard_map/reduce_scatter | solution.py:335
  2078.4 177.6 %reduce-scatter.30.cloned.1.call-done = bf16[16,64,512]{2,1,0:T(8,128)(2,1)} async-done(((bf16[16,1024,512]{2,1,0:T(8,128)(2,1)}), bf16[16,64,512]{2,1,0:T(8,128)(2,1)}) %reduce-scatter.30.cloned.1.call-update) | async-done | bytes 1048592 | tf_op jit(solution)/shard_map/reduce_scatter | solution.py:338
  2258.9 177.7 %reduce-scatter.32.cloned.1.call-done = bf16[16,32,1024]{2,1,0:T(8,128)(2,1)} async-done(((bf16[16,512,1024]{2,1,0:T(8,128)(2,1)}), bf16[16,32,1024]{2,1,0:T(8,128)(2,1)}) %reduce-scatter.32.cloned.1.call-update) | async-done | bytes 1048592 | tf_op jit(solution)/shard_map/reduce_scatter | solution.py:341
  2439.4 127.0 %all-reduce.3.cloned.1.call-done = f32[1024,32]{0,1:T(8,128)} async-done(((f32[1024,32]{0,1:T(8,128)}), f32[1024,32]{0,1:T(8,128)}) %all-reduce.3.cloned.1.call-update) | async-done | bytes 131088 | tf_op jit(solution)/shard_map/psum | solution.py:345
  (739 shorter events, 944.5 us)
Async XLA Ops:
  7.2 254.1 %copy-start = (bf16[1024,32]{0,1:T(8,128)(2,1)S(1)}, bf16[1024,32]{0,1:T(8,128)(2,1)}, u32[]{:S(2)}) copy-start(bf16[1024,32]{0,1:T(8,128)(2,1)} %param.29) | copy-start | bytes 196612
  7.2 44.2 %all-gather.15.cloned.1.call-start = ((), (), s32[]{:S(2)}) async-start(), calls=%async_computation.13 | async-start | bytes 1114112 | tf_op jit(solution)/shard_map/all_gather | solution.py:149
  8.8 76.8 %all-gather.11.cloned.1.call-start = ((), (), s32[]{:S(2)}) async-start(), calls=%async_computation.11 | async-start | bytes 3145728 | tf_op jit(solution)/shard_map/all_gather | solution.py:154
  13.4 112.2 %all-gather.13.cloned.1.call-start = ((), (), s32[]{:S(2)}) async-start(), calls=%async_computation.12 | async-start | bytes 1114112 | tf_op jit(solution)/shard_map/all_gather | solution.py:148
  14.2 151.9 %all-gather.17.cloned.1.call-start = ((), (), s32[]{:S(2)}) async-start(), calls=%async_computation.14 | async-start | bytes 1114112 | tf_op jit(solution)/shard_map/all_gather | solution.py:150
  14.8 209.7 %reduce-scatter.12.cloned.1.call-start = ((), (), s32[]{:S(2)}) async-start(), calls=%async_computation.15 | async-start | bytes 6291456 | tf_op jit(solution)/shard_map/reduce_scatter | solution.py:171
  171.0 90.3 %all-gather.19.cloned.1.call-start = ((), (), s32[]{:S(2)}) async-start(), calls=%async_computation.16 | async-start | bytes 3145728 | tf_op jit(solution)/shard_map/all_gather | solution.py:179
  226.5 1216.1 %copy-start.5 = (f32[512,1024]{1,0:T(8,128)}, f32[512,1024]{1,0:T(8,128)S(1)}, u32[]{:S(2)}) copy-start(f32[512,1024]{1,0:T(8,128)S(1)} %get-tuple-element.907) | copy-start | bytes 6291460
  228.0 161.9 %all-gather.21.cloned.1.call-start = ((), (), s32[]{:S(2)}) async-start(), calls=%async_computation.17 | async-start | bytes 17825792 | tf_op jit(solution)/shard_map/all_gather | solution.py:181
  228.8 288.0 %all-gather.23.cloned.1.call-start = ((), (), s32[]{:S(2)}) async-start(), calls=%async_computation.18 | async-start | bytes 17825792 | tf_op jit(solution)/shard_map/all_gather | solution.py:182
  229.6 414.1 %all-gather.25.cloned.1.call-start = ((), (), s32[]{:S(2)}) async-start(), calls=%async_computation.19 | async-start | bytes 17825792 | tf_op jit(solution)/shard_map/all_gather | solution.py:183
  230.3 744.1 %all-gather.27.cloned.1.call-start = ((), (), s32[]{:S(2)}) async-start(), calls=%async_computation.21 | async-start | bytes 3145728 | tf_op jit(solution)/shard_map/all_gather | solution.py:226
  231.6 1173.8 %reduce-scatter.18.cloned.1.call-start = ((), (), s32[]{:S(2)}) async-start(), calls=%async_computation.23 | async-start | bytes 98304 | tf_op jit(solution)/shard_map/reduce_scatter | solution.py:276
  263.8 379.9 %copy-start.32 = (f32[1024,8]{0,1:T(8,128)}, f32[1024,8]{0,1:T(8,128)S(1)}, u32[]{:S(2)}) copy-start(f32[1024,8]{0,1:T(8,128)S(1)} %select_reduce_fusion.8) | copy-start | bytes 98308
  263.8 379.9 %copy-start.38 = (f32[1024]{0:T(1024)}, f32[1024]{0:T(1024)S(1)}, u32[]{:S(2)}) copy-start(f32[1024]{0:T(1024)S(1)} %reduce_max.18) | copy-start | bytes 12292
  263.8 379.8 %copy-start.42 = (f32[1024]{0:T(1024)}, f32[1024]{0:T(1024)S(1)}, u32[]{:S(2)}) copy-start(f32[1024]{0:T(1024)S(1)} %fusion.134) | copy-start | bytes 12292
  1397.0 43.0 %reduce-scatter.16.cloned.1.call-start = ((), (), s32[]{:S(2)}) async-start(), calls=%async_computation.22 | async-start | bytes 3145728 | tf_op jit(solution)/shard_map/reduce_scatter | solution.py:273
  1400.9 77.9 %all-gather.29.cloned.1.call-start = ((), (), s32[]{:S(2)}) async-start(), calls=%async_computation.24 | async-start | bytes 3145728 | tf_op jit(solution)/shard_map/all_gather | solution.py:285
  1445.6 260.0 %reduce-scatter.24.cloned.1.call-start = ((), (), s32[]{:S(2)}) async-start(), calls=%async_computation.27 | async-start | bytes 1114112 | tf_op jit(solution)/shard_map/reduce_scatter | solution.py:329
  1647.8 117.9 %reduce-scatter.26.cloned.1.call-start = ((), (), s32[]{:S(2)}) async-start(), calls=%async_computation.28 | async-start | bytes 1114112 | tf_op jit(solution)/shard_map/reduce_scatter | solution.py:332
  1652.3 174.3 %reduce-scatter.22.cloned.1.call-start = ((), (), s32[]{:S(2)}) async-start(), calls=%async_computation.26 | async-start | bytes 1114112 | tf_op jit(solution)/shard_map/reduce_scatter | solution.py:326
  1661.2 198.9 %reduce-scatter.20.cloned.1.call-start = ((), (), s32[]{:S(2)}) async-start(), calls=%async_computation.25 | async-start | bytes 3145728 | tf_op jit(solution)/shard_map/reduce_scatter | solution.py:314
  1666.6 227.6 %reduce-scatter.14.cloned.1.call-start = ((), (), s32[]{:S(2)}) async-start(), calls=%async_computation.20 | async-start | bytes 3145728 | tf_op jit(solution)/shard_map/reduce_scatter | solution.py:221
  1670.5 405.1 %reduce-scatter.28.cloned.1.call-start = ((), (), s32[]{:S(2)}) async-start(), calls=%async_computation.30 | async-start | bytes 17825792 | tf_op jit(solution)/shard_map/reduce_scatter | solution.py:335
  1671.2 584.8 %reduce-scatter.30.cloned.1.call-start = ((), (), s32[]{:S(2)}) async-start(), calls=%async_computation.31 | async-start | bytes 17825792 | tf_op jit(solution)/shard_map/reduce_scatter | solution.py:338
  1671.8 764.8 %reduce-scatter.32.cloned.1.call-start = ((), (), s32[]{:S(2)}) async-start(), calls=%async_computation.32 | async-start | bytes 17825792 | tf_op jit(solution)/shard_map/reduce_scatter | solution.py:341
  1672.5 221.6 %copy-start.6 = (f32[512,1024]{1,0:T(8,128)S(1)}, f32[512,1024]{1,0:T(8,128)}, u32[]{:S(2)}) copy-start(f32[512,1024]{1,0:T(8,128)} %copy-done.5) | copy-start | bytes 6291460
  1672.5 221.6 %copy-start.41 = (f32[1024]{0:T(1024)S(1)}, f32[1024]{0:T(1024)}, u32[]{:S(2)}) copy-start(f32[1024]{0:T(1024)} %param.28) | copy-start | bytes 12292
  1672.5 221.6 %copy-start.45 = (f32[512]{0:T(512)S(1)}, f32[512]{0:T(512)}, u32[]{:S(2)}) copy-start(f32[512]{0:T(512)} %copy-done.43) | copy-start | bytes 6148
  1672.6 221.6 %copy-start.50 = (f32[512]{0:T(512)S(1)}, f32[512]{0:T(512)}, u32[]{:S(2)}) copy-start(f32[512]{0:T(512)} %copy-done.49) | copy-start | bytes 6148
  1672.6 893.8 %all-reduce.3.cloned.1.call-start = ((), (), s32[]{:S(2)}) async-start(), calls=%async_computation.29 | async-start | bytes 262144 | tf_op jit(solution)/shard_map/psum | solution.py:345
  2256.0 311.9 %copy-start.1 = (bf16[1024,32]{0,1:T(8,128)(2,1)S(1)}, bf16[1024,32]{0,1:T(8,128)(2,1)}, u32[]{:S(2)}) copy-start(bf16[1024,32]{0,1:T(8,128)(2,1)} %param.29) | copy-start | bytes 196612
  (84 other events, 1428.0 us)
Sparse Core Ops, SparseCore 0:
  10.8 40.5 all-gather.14
  53.5 32.0 all-gather.10
  87.8 37.8 all-gather.12
  127.7 36.8 all-gather.16
  171.1 53.3 reduce-scatter.11
  228.2 33.0 all-gather.18
  263.5 126.4 all-gather.20
  392.2 124.6 all-gather.22
  519.0 124.6 all-gather.24
  645.6 31.2 all-gather.26
  1397.1 8.1 reduce-scatter.17
  1408.0 31.8 reduce-scatter.15
  1445.7 33.0 all-gather.28
  1648.0 57.6 reduce-scatter.23
  1709.1 56.5 reduce-scatter.25
  1769.8 56.7 reduce-scatter.21
  1829.2 30.8 reduce-scatter.19
  1862.2 31.8 reduce-scatter.13
  1898.3 177.2 reduce-scatter.27
  2079.6 176.4 reduce-scatter.29
  2260.2 176.3 reduce-scatter.31
  2442.7 123.5 all-reduce.2
where the time goes:
time: 2590 us; the launch traced here: 2570 us
  waiting for transfers between devices  1470 us (57%)
  matrix products  750 us (29%)
  other arithmetic  173 us (7%)
  local copies, waits for them, and re-layouts  120 us (5%)
  blocking collectives  39.5 us (2%)
    dot_general x119, matrix products, contract(): lax.dot_general(left, right, (((left_dim,), (right_dim,)), ((), ())), pre...  410 us
    reduce_scatter x1, waiting for transfers between devices, shards(): lax.psum_scatter(down_part.astype(jnp.bfloat16), 'dp', scatter_dimension=...  178 us
    reduce_scatter x1, waiting for transfers between devices, shards(): lax.psum_scatter(up_part.astype(jnp.bfloat16), 'dp', scatter_dimension=1,...  178 us
    reduce_scatter x1, waiting for transfers between devices, shards(): lax.psum_scatter(gate_part.astype(jnp.bfloat16), 'dp', scatter_dimension=...  138 us
    psum x1, waiting for transfers between devices, shards(): lax.psum((attn_gain_part, ffn_gain_part, router_part), ('dp', 'tensor'))  127 us
    all_gather x1, waiting for transfers between devices, shards(): lax.all_gather(down_weight, 'dp', axis=1, tiled=True)  127 us
    all_gather x1, waiting for transfers between devices, shards(): lax.all_gather(up_weight, 'dp', axis=1, tiled=True)  127 us
    all_gather x1, waiting for transfers between devices, shards(): lax.all_gather(gate_weight, 'dp', axis=1, tiled=True)  125 us
  transfers between devices with their start and end apart: 22, of which 20 were waited for; matrix products, arithmetic and copies ran while one was open for 17% of the time, Pallas kernels for 0%

commit v1 on v0

v1 whole, which is shorter than its diff:
```python
import functools

import jax
import jax.numpy as jnp
from jax import lax
from jax.sharding import Mesh, PartitionSpec as P

CAP = 320
norm_eps = 1e-06
attn_scale = 0.015625
residual_scale = 0.22
rope_base = 10000.0
masked_score = -1e30
f32 = jnp.float32
bf16 = jnp.bfloat16


def row_scale(values):
    return lax.rsqrt(jnp.mean(values * values, axis=-1, keepdims=True) + norm_eps)


def rope_tables(positions, head_dim):
    half_dim = head_dim // 2
    frequency = rope_base ** (-(jnp.arange(half_dim, dtype=f32) * 2.0 / head_dim))
    angles = positions.astype(f32)[:, None] * frequency[None, :]
    cosine, sine = jnp.cos(angles), jnp.sin(angles)
    return (
        jnp.concatenate([cosine, cosine], axis=-1)[:, None, :],
        jnp.concatenate([sine, sine], axis=-1)[:, None, :],
    )


def rotary(values, tables, direction):
    half_dim = values.shape[-1] // 2
    cosine, sine = tables
    rotated = jnp.concatenate([-values[..., half_dim:], values[..., :half_dim]], axis=-1)
    return values * cosine + direction * rotated * sine


def contract(left, right, left_dim, right_dim):
    return lax.dot_general(
        left, right, (((left_dim,), (right_dim,)), ((), ())), preferred_element_type=f32
    )


def ein(spec, *operands):
    return jnp.einsum(spec, *operands, preferred_element_type=f32)


def norm_backward(normed_grad, source, gain):
    scale_rows = row_scale(source)
    unit_rows = source * scale_rows
    scaled_grad = normed_grad * gain
    gain_grad = jnp.sum(normed_grad * unit_rows, axis=0)
    source_grad = scale_rows * (
        scaled_grad - unit_rows * jnp.mean(scaled_grad * unit_rows, axis=-1, keepdims=True)
    )
    return (source_grad, gain_grad)


def swap(values, axis):
    return lax.ppermute(values, axis, [(0, 1), (1, 0)])


def butterfly_sum(values, sizes):
    for axis, size in sizes:
        step = 1
        while step < size:
            values = values + lax.ppermute(values, axis, [(i, i ^ step) for i in range(size)])
            step *= 2
    return values


def in_order(mine, theirs, first):
    return jnp.concatenate(
        [jnp.where(first, mine, theirs), jnp.where(first, theirs, mine)], axis=0
    )


def gather_rows(rows, tensor_size):
    if tensor_size != 2:
        return lax.all_gather(rows, "tensor", axis=0, tiled=True)
    return in_order(rows, swap(rows, "tensor"), lax.axis_index("tensor") == 0)


def scatter_rows(values, tensor_size):
    if tensor_size != 2:
        return lax.psum_scatter(
            values.astype(bf16), "tensor", scatter_dimension=0, tiled=True
        ).astype(f32)
    half = values.shape[0] // 2
    me = lax.axis_index("tensor")
    give = lax.dynamic_slice_in_dim(values, (1 - me) * half, half, 0).astype(bf16)
    keep = lax.dynamic_slice_in_dim(values, me * half, half, 0)
    return keep.astype(f32) + swap(give, "tensor").astype(f32)


def gather_group(rows, tensor_size):
    if tensor_size != 2:
        own = gather_rows(rows, tensor_size)
        across = swap(own, "y")
    else:
        first = lax.axis_index("tensor") == 0
        half = rows.shape[0] // 2
        by_tensor, by_y = swap(rows, "tensor"), swap(rows, "y")
        corner = jnp.concatenate(
            [swap(by_y[:half], "tensor"), swap(by_tensor[half:], "y")], axis=0
        )
        own = in_order(rows, by_tensor, first)
        across = in_order(by_y, corner, first)
    return jnp.stack([own, across, swap(own, "core"), swap(across, "core")])


def scatter_group(parts, tensor_size):
    pair = [parts[i].astype(f32) + swap(parts[i + 2].astype(bf16), "core").astype(f32) for i in (0, 1)]
    own, across = pair
    if tensor_size != 2:
        own = own + swap(across.astype(bf16), "y").astype(f32)
        return scatter_rows(own, tensor_size)
    me = lax.axis_index("tensor")
    rows = own.shape[0] // 2
    half = rows // 2

    def take(values, which):
        return lax.dynamic_slice_in_dim(values, which * rows, rows, 0)

    mine, by_tensor = take(own, me), take(own, 1 - me)
    by_y, corner = take(across, me), take(across, 1 - me).astype(bf16)
    low, high = swap(corner[:half], "tensor"), swap(corner[half:], "y")
    by_y = jnp.concatenate([by_y[:half] + low.astype(f32), by_y[half:]], axis=0)
    by_tensor = jnp.concatenate([by_tensor[:half], by_tensor[half:] + high.astype(f32)], axis=0)
    return (
        mine
        + swap(by_tensor.astype(bf16), "tensor").astype(f32)
        + swap(by_y.astype(bf16), "y").astype(f32)
    )


def split_low(values, count):
    pieces = []
    for _ in range(count):
        piece = values.astype(bf16)
        pieces.append(piece)
        values = values - piece.astype(f32)
    return pieces


def attention_forward(query, keys, values_in):
    seq_len = query.shape[0]
    block = min(512, seq_len)
    mixed, log_totals = [], []
    for start in range(0, seq_len, block):
        stop = start + block
        scores = masked_scores(query[start:stop], keys[:stop], start)
        top_score = jnp.max(scores, axis=-1, keepdims=True)
        log_total = top_score + jnp.log(
            jnp.sum(jnp.exp(scores - top_score), axis=-1, keepdims=True)
        )
        prob_vals = jnp.exp(scores - log_total).astype(bf16)
        blended = ein("grbs,sgd->bgrd", prob_vals, values_in[:stop])
        mixed.append(blended.astype(bf16).reshape(block, -1))
        log_totals.append(log_total)
    return jnp.concatenate(mixed, axis=0), log_totals


def masked_scores(q_block, keys, start):
    scores = ein("bgrd,sgd->grbs", q_block, keys) * attn_scale
    row_pos = start + jnp.arange(q_block.shape[0])
    key_pos = jnp.arange(keys.shape[0])
    return jnp.where(
        key_pos[None, None, None, :] <= row_pos[None, None, :, None], scores, masked_score
    )


def attention_backward(query, keys, values_in, log_totals, mixed_grad):
    seq_len = query.shape[0]
    block = min(512, seq_len)
    query_grads = []
    key_grad = value_grad = None
    for index, start in reversed(list(enumerate(range(0, seq_len, block)))):
        stop = start + block
        q_block, g_block = query[start:stop], mixed_grad[start:stop]
        scores = masked_scores(q_block, keys[:stop], start)
        prob_vals = jnp.exp(scores - log_totals[index])
        prob_grad = ein("bgrd,sgd->grbs", g_block, values_in[:stop])
        row_dot = jnp.sum(prob_vals * prob_grad, axis=-1, keepdims=True)
        score_grad = (prob_vals * (prob_grad - row_dot)).astype(bf16)
        query_grads.append(ein("grbs,sgd->bgrd", score_grad, keys[:stop]) * attn_scale)
        key_step = ein("grbs,bgrd->sgd", score_grad, q_block) * attn_scale
        value_step = ein("grbs,bgrd->sgd", prob_vals.astype(bf16), g_block)
        if key_grad is None:
            key_grad, value_grad = key_step, value_step
        else:
            pad = ((0, seq_len - stop), (0, 0), (0, 0))
            key_grad = key_grad + jnp.pad(key_step, pad)
            value_grad = value_grad + jnp.pad(value_step, pad)
    return jnp.concatenate(query_grads[::-1], axis=0), key_grad, value_grad


def shards(
    sizes,
    block_input,
    positions,
    expert_ids,
    attn_gain,
    query_weight,
    kv_weight,
    out_weight,
    ffn_gain,
    router_weight,
    gate_weight,
    up_weight,
    down_weight,
    out_grad,
):
    tensor_size = sizes["tensor"]
    every_dp = ("z", "y", "core")
    seq_len = positions.shape[0]
    width = block_input.shape[1]
    kv_local = kv_weight.shape[1]
    head_dim = kv_weight.shape[2] // 2
    heads_local = query_weight.shape[1] // head_dim
    q_width, kv_width = heads_local * head_dim, kv_local * 2 * head_dim
    expert_count = router_weight.shape[1]
    experts_local = gate_weight.shape[0]
    owned = experts_local // 4
    hidden_width = gate_weight.shape[2]

    packed = jnp.concatenate(
        [query_weight, kv_weight.reshape(kv_weight.shape[0], -1), out_weight.T], axis=1
    )
    packed_full = lax.all_gather(packed, every_dp, axis=0, tiled=True)
    qkv_full = packed_full[:, : q_width + kv_width]
    out_full = packed_full[:, q_width + kv_width :]

    def to_owner(weight):
        return lax.all_to_all(weight, ("y", "core"), 0, 1, tiled=True)

    def from_owner(grad):
        return lax.all_to_all(grad, ("y", "core"), 1, 0, tiled=True)

    both = jnp.concatenate([to_owner(gate_weight), to_owner(up_weight)], axis=2)
    both_full = lax.all_gather(both, "z", axis=1, tiled=True)
    down_full = lax.all_gather(to_owner(down_weight), "z", axis=1, tiled=True)

    grad_rows = out_grad.astype(f32)
    moe_grad = gather_group((residual_scale * grad_rows).astype(bf16), tensor_size)

    ids_t = expert_ids.T
    hits = jnp.zeros((expert_count, seq_len), jnp.bool_)
    for k in range(ids_t.shape[0]):
        hits = hits | (ids_t[k][None, :] == jnp.arange(expert_count)[:, None])
    token_ids = jnp.arange(seq_len)
    earlier = (token_ids[:, None] < token_ids[None, :]).astype(bf16)
    rank = jnp.dot(hits.astype(bf16), earlier, preferred_element_type=f32)
    code = jnp.where(hits, jnp.where(rank < CAP, rank, -1.0), -2.0)
    code_y = swap(code, "y")
    codes = jnp.stack([code, code_y, swap(code, "core"), swap(code_y, "core")])

    input_rows = block_input.astype(f32)
    attn_normed = (input_rows * row_scale(input_rows) * attn_gain).astype(bf16)
    attn_tokens = gather_rows(attn_normed, tensor_size)
    tables = rope_tables(positions, head_dim)
    qkv_pre = jnp.dot(attn_tokens, qkv_full, preferred_element_type=f32)
    query_pre = qkv_pre[:, :q_width].reshape(seq_len, heads_local, head_dim)
    kv_pre = qkv_pre[:, q_width:].reshape(seq_len, kv_local, 2 * head_dim)
    query_rot = (
        rotary(query_pre, tables, 1.0)
        .astype(bf16)
        .reshape(seq_len, kv_local, heads_local // kv_local, head_dim)
    )
    key_rot = rotary(kv_pre[..., :head_dim], tables, 1.0).astype(bf16)
    value_low = kv_pre[..., head_dim:].astype(bf16)
    attn_mixed, log_totals = attention_forward(query_rot, key_rot, value_low)
    attn_out = scatter_rows(contract(attn_mixed, out_full, 1, 1), tensor_size)
    hidden_state = input_rows + residual_scale * attn_out
    ffn_normed = (hidden_state * row_scale(hidden_state) * ffn_gain).astype(bf16)

    tokens = gather_group(ffn_normed, tensor_size)
    logits = ein("dx,std->sxt", router_weight, tokens)
    chosen = codes > -1.5
    top_logit = jnp.max(jnp.where(chosen, logits, -jnp.inf), axis=1, keepdims=True)
    raised = jnp.where(chosen, jnp.exp(jnp.where(chosen, logits - top_logit, 0.0)), 0.0)
    gates = raised / jnp.sum(raised, axis=1, keepdims=True)
    expert_first = (
        lax.axis_index("tensor") * experts_local
        + (lax.axis_index("y") * 2 + lax.axis_index("core")) * owned
    )
    code_own = lax.dynamic_slice_in_dim(codes, expert_first, owned, 1)
    gate_own = lax.dynamic_slice_in_dim(gates, expert_first, owned, 1)
    slot_ids = jnp.arange(CAP, dtype=jnp.int32)
    dispatch = (code_own.astype(jnp.int32)[:, :, None, :] == slot_ids[:, None]).astype(bf16)

    gate_cols = jnp.stack(split_low(gate_own, 3), axis=-1)
    slot_gate = jnp.sum(ein("sect,setk->seck", dispatch, gate_cols), axis=-1)[..., None]
    expert_in = ein("sect,std->secd", dispatch, tokens).astype(bf16)
    both_pre = ein("secd,edf->secf", expert_in, both_full)
    gate_pre, up_pre = both_pre[..., :hidden_width], both_pre[..., hidden_width:]
    hidden_act = (jax.nn.silu(gate_pre) * up_pre).astype(bf16)
    expert_out = ein("secf,efd->secd", hidden_act, down_full)
    weighted = (slot_gate * expert_out).astype(bf16)
    moe_parts = ein("sect,secd->std", dispatch, weighted).astype(bf16)
    moe_out = scatter_group(moe_parts, tensor_size)
    block_output = (hidden_state + residual_scale * moe_out).astype(bf16)

    slot_grad = ein("sect,std->secd", dispatch, moe_grad)
    out_slot_grad = (slot_gate * slot_grad).astype(bf16)
    down_part = ein("secf,secd->efd", hidden_act, out_slot_grad).astype(bf16)
    raw_hidden_grad = ein("secd,efd->secf", slot_grad.astype(bf16), down_full)
    slot_gate_grad = jnp.sum(hidden_act.astype(f32) * raw_hidden_grad, axis=-1)
    hidden_grad = slot_gate * raw_hidden_grad
    sigmoid_gate = jax.nn.sigmoid(gate_pre)
    both_pre_grad = jnp.concatenate(
        [
            hidden_grad * up_pre * sigmoid_gate * (1.0 + gate_pre * (1.0 - sigmoid_gate)),
            hidden_grad * gate_pre * sigmoid_gate,
        ],
        axis=-1,
    ).astype(bf16)
    both_part = ein("secd,secf->edf", expert_in, both_pre_grad).astype(bf16)
    in_grad = ein("secf,edf->secd", both_pre_grad, both_full).astype(bf16)
    normed_parts = ein("sect,secd->std", dispatch, in_grad).astype(bf16)
    grad_cols = jnp.stack(split_low(slot_gate_grad, 3), axis=-1)
    pair_grad = jnp.sum(ein("sect,seck->setk", dispatch, grad_cols), axis=-1)
    gate_dot = jnp.sum(gate_own * pair_grad, axis=1, keepdims=True)
    pair_all = lax.dynamic_update_slice_in_dim(jnp.zeros_like(gates), pair_grad, expert_first, 1)
    logit_parts = jnp.swapaxes(gates * (pair_all - gate_dot), 1, 2).astype(bf16)
    normed_local = scatter_group(normed_parts, tensor_size)
    logit_low = scatter_group(logit_parts, tensor_size).astype(bf16)

    down_sum = from_owner(
        lax.psum_scatter(down_part, "z", scatter_dimension=1, tiled=True)
    ).astype(f32)
    both_sum = lax.psum_scatter(both_part, "z", scatter_dimension=1, tiled=True)
    gate_sum = from_owner(both_sum[..., :hidden_width]).astype(f32)
    up_sum = from_owner(both_sum[..., hidden_width:]).astype(f32)

    normed_local = normed_local + contract(logit_low, router_weight, 1, 1)
    router_part = contract(logit_low, ffn_normed, 0, 0)
    state_grad, ffn_gain_part = norm_backward(normed_local, hidden_state, ffn_gain)
    state_grad = state_grad + grad_rows
    steps = (
        ("core", 2),
        ("y", 2),
        ("tensor", tensor_size),
        ("z", sizes["z"]),
    )
    early_sum = butterfly_sum(
        jnp.concatenate([router_part, ffn_gain_part[None, :]], axis=0), steps
    )
    router_grad, ffn_gain_grad = early_sum[:expert_count].T, early_sum[expert_count]

    attn_grad_all = gather_rows((residual_scale * state_grad).astype(bf16), tensor_size)
    out_part = contract(attn_grad_all, attn_mixed, 0, 0).astype(bf16)
    out_sum = lax.psum_scatter(out_part, every_dp, scatter_dimension=0, tiled=True)
    mixed_grad = jnp.dot(attn_grad_all, out_full, preferred_element_type=f32)
    mixed_grad = mixed_grad.astype(bf16).reshape(query_rot.shape)
    query_grad, key_grad, value_grad = attention_backward(
        query_rot, key_rot, value_low, log_totals, mixed_grad
    )
    query_pre_grad = rotary(
        query_grad.reshape(seq_len, heads_local, head_dim), tables, -1.0
    ).astype(bf16)
    kv_pre_grad = jnp.concatenate(
        [rotary(key_grad, tables, -1.0), value_grad], axis=-1
    ).astype(bf16)
    qkv_pre_grad = jnp.concatenate(
        [query_pre_grad.reshape(seq_len, q_width), kv_pre_grad.reshape(seq_len, kv_width)], axis=1
    )
    qkv_part = contract(attn_tokens, qkv_pre_grad, 0, 0).astype(bf16)
    qkv_sum = lax.psum_scatter(qkv_part, every_dp, scatter_dimension=0, tiled=True)
    attn_normed_grad = scatter_rows(contract(qkv_pre_grad, qkv_full, 1, 1), tensor_size)
    input_part, attn_gain_part = norm_backward(attn_normed_grad, input_rows, attn_gain)
    input_grad = (state_grad + input_part).astype(bf16)
    attn_gain_grad = butterfly_sum(attn_gain_part[None, :], steps)[0]
    return (
        block_output,
        input_grad,
        attn_gain_grad,
        qkv_sum[:, :q_width].astype(f32),
        qkv_sum[:, q_width:].reshape(kv_weight.shape).astype(f32),
        out_sum.T.astype(f32),
        ffn_gain_grad,
        router_grad,
        gate_sum,
        up_sum,
        down_sum,
    )


def solution(mesh):
    dp, tensor = mesh.shape["dp"], mesh.shape["tensor"]
    fine = Mesh(mesh.devices.reshape(dp // 4, 2, 2, tensor), ("z", "y", "core", "tensor"))
    rows = ("z", "y", "core")
    every = rows + ("tensor",)
    experts = P("tensor", rows, None)
    return jax.shard_map(
        functools.partial(shards, dict(fine.shape)),
        mesh=fine,
        in_specs=(
            P(every, None),
            P(rows),
            P(rows, None),
            P(),
            P(rows, "tensor"),
            P(rows, "tensor", None),
            P("tensor", rows),
            P(),
            P(),
            experts,
            experts,
            experts,
            P(every, None),
        ),
        out_specs=(
            P(every, None),
            P(every, None),
            P(),
            P(rows, "tensor"),
            P(rows, "tensor", None),
            P("tensor", rows),
            P(),
            P(),
            experts,
            experts,
            experts,
        ),
        check_vma=False,
    )
```

time: 2590 us -> 778 us (0.30)
  waiting for transfers between devices: 1470 us -> 249 us
  matrix products: 750 us -> 275 us
  other arithmetic: 173 us -> 95.6 us
  starting transfers between devices: 0.89 us -> 78.2 us
  local copies, waits for them, and re-layouts: 120 us -> 53.2 us
  blocking collectives: 39.5 us -> 0 us
    reduce_scatter x11 -> x4, waiting for transfers between devices: 798 us -> 0.03 us  [the longest x1 0.02 us: shards(): lax.psum_scatter(qkv_part, every_dp, scatter_dimension=0, tiled=True)]
    all_gather x10 -> x3, waiting for transfers between devices: 536 us -> 10.5 us  [the longest x1 6.02 us: shards(): down_full = lax.all_gather(to_owner(down_weight), 'z', axis=1, tiled=True)]
    dot_general x119 -> x6, matrix products: 410 us -> 14.8 us  [contract(): lax.dot_general(left, right, (((left_dim,), (right_dim,)), ((), ())), pre...]
    ppermute x0 -> x47, waiting for transfers between devices: none -> 202 us  [the longest x37 145 us: swap(): return lax.ppermute(values, axis, [(0, 1), (1, 0)])]
    psum x1 -> x0, waiting for transfers between devices: 127 us -> none  [shards(): lax.psum((attn_gain_part, ffn_gain_part, router_part), ('dp', 'tensor'))]
    dot_general x99 -> x28, matrix products: 340 us -> 260 us  [the longest x25 252 us: ein(): return jnp.einsum(spec, *operands, preferred_element_type=f32)]
    reduce_sum x103 -> x3, other arithmetic: 67.6 us -> 9.92 us  [the longest x2 9.85 us: attention_forward(): jnp.sum(jnp.exp(scores - top_score), axis=-1, keepdims=True)]
    dynamic_update_slice x20 -> x0, local copies, waits for them, and re-layouts: 55.7 us -> none  [the longest x4 41.4 us: attention_backward(): lax.scan(one_block, (zero_keys, zero_keys), (starts, log_totals))]
  transfers between devices with their start and end apart: 22 -> 60, of which waited for: 20 -> 24; matrix products, arithmetic and copies ran while one was open for 17% -> 49% of each run, Pallas kernels for 0% -> 0%
where the time goes in v1:
time: 778 us; the launch traced here: 767 us
  matrix products  275 us (35%)
  waiting for transfers between devices  249 us (32%)
  other arithmetic  95.6 us (12%)
  starting transfers between devices  78.2 us (10%)
  local copies, waits for them, and re-layouts  53.2 us (7%)
  between operations  16.3 us (2%)
    dot_general x25, matrix products, ein(): return jnp.einsum(spec, *operands, preferred_element_type=f32)  252 us
    ppermute x37, waiting for transfers between devices, swap(): return lax.ppermute(values, axis, [(0, 1), (1, 0)])  145 us
    ppermute x10, waiting for transfers between devices, butterfly_sum(): lax.ppermute(values, axis, [(i, i ^ step) for i in range(size)])  57.8 us
    ppermute x37, starting transfers between devices, swap(): return lax.ppermute(values, axis, [(0, 1), (1, 0)])  32.2 us
    all_to_all x3, waiting for transfers between devices, to_owner(): return lax.all_to_all(weight, ('y', 'core'), 0, 1, tiled=True)  28.8 us
    all_to_all x3, starting transfers between devices, to_owner(): return lax.all_to_all(weight, ('y', 'core'), 0, 1, tiled=True)  22.5 us
  transfers between devices with their start and end apart: 60, of which 24 were waited for; matrix products, arithmetic and copies ran while one was open for 49% of the time, Pallas kernels for 0%

profile of v1, /device:TPU:0, one launch (start us, length us, event | category | flops | bytes accessed | tf_op | source)
XLA Modules:
  0.0 767.3 jit_solution(16090157803512232544)
XLA Ops:
  19.9 10.7 %all-to-all-done = bf16[16,64,512]{2,1,0:T(8,128)(2,1)S(1)} async-done(((bf16[16,64,512]{2,1,0:T(8,128)(2,1)}), bf16[16,64,512]{2,1,0:T(8,128)(2,1)S(1)}, u32[]{:S(2)}, u32[]{:S(2)}) %all-to-all-start) | async-done | bytes 1048608 | tf_op jit(solution)/shard_map/all_to_all | solution.py:237
  37.8 18.1 %all-to-all-done.1 = bf16[16,64,512]{2,1,0:T(8,128)(2,1)} async-done(((bf16[16,64,512]{2,1,0:T(8,128)(2,1)}), bf16[16,64,512]{2,1,0:T(8,128)(2,1)}, u32[]{:S(2)}, u32[]{:S(2)}) %all-to-all-start.1) | async-done | bytes 1048608 | tf_op jit(solution)/shard_map/all_to_all | solution.py:237
  78.9 7.5 fusion.195
  86.4 8.1 %exponential_reduce_fusion = f32[4,2,512]{2,1,0:T(2,128)S(1)} fusion(f32[4,2,512,1024]{2,3,1,0:T(8,128)} %get-tuple-element.103, f32[4,2,512]{2,1,0:T(2,128)S(1)} %get-tuple-element.102), kind=kLoop, calls=%fused_computation.21 | loop fusion | flops 8384512 | bytes 16809984 | tf_op jit(solution)/shard_map/reduce_sum | solution.py:157
  100.7 8.7 %fusion.107 = bf16[4,64,2,512]{3,1,2,0:T(8,128)(2,1)S(1)} fusion(f32[4,2,512,1024]{2,3,1,0:T(8,128)} %get-tuple-element.103, f32[4,2,512]{2,1,0:T(2,128)S(1)} %bitcast.376, bf16[1024,4,128]{0,2,1:T(8,128)(2,1)S(1)} %bitcast_convert_fusion.4), kind=kOutput, calls=%fused_computation.163 | convolution fusion | flops 545521664 | bytes 17842176 | tf_op jit(solution)/shard_map/grbs,sgd->bgrd/dot_general | solution.py:47
  117.1 22.6 %collective-permute-done.1 = bf16[512,1024]{1,0:T(8,128)(2,1)} collective-permute-done((bf16[512,1024]{1,0:T(8,128)(2,1)}, bf16[512,1024]{1,0:T(8,128)(2,1)}, u32[]{:S(2)}, u32[]{:S(2)}) %collective-permute-start.1) | collective-permute-done | bytes 1048608 | tf_op jit(solution)/shard_map/ppermute | solution.py:62
  147.0 15.1 %collective-permute-done.17 = bf16[512,1024]{1,0:T(8,128)(2,1)S(1)} collective-permute-done((bf16[512,1024]{1,0:T(8,128)(2,1)}, bf16[512,1024]{1,0:T(8,128)(2,1)S(1)}, u32[]{:S(2)}, u32[]{:S(2)}) %collective-permute-start.17) | collective-permute-done | bytes 1048608 | tf_op jit(solution)/shard_map/ppermute | solution.py:62
  162.7 32.4 %collective-permute-done.19 = bf16[256,1024]{1,0:T(8,128)(2,1)S(1)} collective-permute-done((bf16[256,1024]{1,0:T(8,128)(2,1)S(1)}, bf16[256,1024]{1,0:T(8,128)(2,1)S(1)}, u32[]{:S(2)}, u32[]{:S(2)}) %collective-permute-start.19) | collective-permute-done | bytes 524320 | tf_op jit(solution)/shard_map/ppermute | solution.py:62
  200.6 8.0 %collective-permute-done.7 = bf16[256,1024]{1,0:T(8,128)(2,1)S(1)} collective-permute-done((bf16[256,1024]{1,0:T(8,128)(2,1)S(1)}, bf16[256,1024]{1,0:T(8,128)(2,1)S(1)}, u32[]{:S(2)}, u32[]{:S(2)}) %collective-permute-start.7) | collective-permute-done | bytes 524320 | tf_op jit(solution)/shard_map/ppermute | solution.py:62
  214.1 13.9 %all-to-all-start.2 = ((bf16[16,32,1024]{2,1,0:T(8,128)(2,1)}), bf16[16,32,1024]{2,1,0:T(8,128)(2,1)}, u32[]{:S(2)}, u32[]{:S(2)}) async-start(bf16[16,32,1024]{2,1,0:T(8,128)(2,1)} %param.24), calls=%async_computation.2 | async-start | bytes 2097152 | tf_op jit(solution)/shard_map/all_to_all | solution.py:237
  230.6 14.7 %collective-permute-done.2 = f32[32,1024]{1,0:T(8,128)S(1)} collective-permute-done((f32[32,1024]{1,0:T(8,128)S(1)}, f32[32,1024]{1,0:T(8,128)S(1)}, u32[]{:S(2)}, u32[]{:S(2)}) %collective-permute-start.2) | collective-permute-done | bytes 131104 | tf_op jit(solution)/shard_map/ppermute | solution.py:62
  261.0 18.1 %fusion.57 = bf16[4,4,320,1024]{3,2,1,0:T(8,128)(2,1)} fusion(s32[4,4,1024]{2,1,0:T(4,128)S(1)} %dynamic-slice_convert_fusion.9, bf16[1,1024,1024]{2,1,0:T(8,128)(2,1)} %bitcast.35, bf16[1,1024,1024]{2,1,0:T(8,128)(2,1)} %bitcast.34, bf16[1,1024,1024]{2,1,0:T(8,128)(2,1)S(1)} %copy-done.35, bf16[1,1024,1024]{2,1,0:T(8,128)(2,1)S(1)} %copy-done.34), kind=kOutput, calls=%fused_computation.72 | convolution fusion | flops 10760486912 | bytes 18939904 | tf_op jit(solution)/shard_map/sect,std->secd/dot_general | solution.py:47
  283.4 20.9 %multiply_convert_fusion = (bf16[4,4,320,1024]{3,2,1,0:T(8,128)(2,1)}, bf16[4,4,320,1024]{3,2,1,0:T(8,128)(2,1)}) fusion(f32[4,4,320]{2,1,0:T(4,128)S(1)} %fusion.118, bf16[1,1024,1024]{2,1,0:T(8,128)(2,1)} %bitcast.66, bf16[1,1024,1024]{2,1,0:T(8,128)(2,1)} %bitcast.65, bf16[1,1024,1024]{2,1,0:T(8,128)(2,1)S(1)} %get-tuple-element.54, ...), kind=kOutput, calls=%fused_computation.3 | convolution fusion | flops 10770972672 | bytes 29446144 | tf_op jit(solution)/shard_map/sect,std->secd/dot_general | solution.py:47
  304.3 18.9 %fusion.45 = f32[4,4,320,1024]{3,2,0,1:T(8,128)} fusion(bf16[4,4,320,1024]{3,2,1,0:T(8,128)(2,1)} %fusion.57, bf16[4,1024,1024]{2,1,0:T(8,128)(2,1)} %all-gather.6.cloned.1.call-done), kind=kOutput, calls=%fused_computation.70 | convolution fusion | flops 10737418240 | bytes 39845888 | tf_op jit(solution)/shard_map/secd,edf->secf/dot_general | solution.py:47
  329.2 20.5 %multiply_convert_fusion.2 = (bf16[4,4,320,512]{3,2,0,1:T(8,128)(2,1)}, bf16[4,4,320,512]{3,2,0,1:T(8,128)(2,1)}, f32[4,4,320]{2,0,1:T(4,128)S(1)}, bf16[4,4,320,512]{3,2,0,1:T(8,128)(2,1)S(1)}) fusion(f32[4,4,320,1024]{3,2,0,1:T(8,128)} %fusion.45, f32[4,4,320]{2,0,1:T(4,128)S(1)} %copy.51, bf16[4,512,1024]{2,1,0:T(8,128)(2,1)} %all-gather.8.cloned.1.call-done, ...), kind=kOutput, calls=%fused_computation.36 | convolution fusion | flops 5421132800 | bytes 51421184 | tf_op jit(solution)/shard_map/secd,efd->secf/dot_general | solution.py:47
  352.0 11.2 %bitcast_convert_fusion.3 = bf16[4,512,1024]{2,1,0:T(8,128)(2,1)} fusion(bf16[4,4,320,512]{3,2,0,1:T(8,128)(2,1)S(1)} %get-tuple-element.23, bf16[4,4,320,1024]{3,2,1,0:T(8,128)(2,1)} %get-tuple-element.24), kind=kOutput, calls=%fused_computation.60 | convolution fusion | flops 5370806272 | bytes 19922944 | tf_op jit(solution)/shard_map/secf,secd->efd/dot_general | solution.py:47
  367.7 17.7 %fusion.31 = bf16[4,1024,4,320]{1,3,0,2:T(8,128)(2,1)} fusion(bf16[4,1024,1024]{2,1,0:T(8,128)(2,1)} %all-gather.6.cloned.1.call-done, bf16[4,4,320,512]{3,2,0,1:T(8,128)(2,1)} %get-tuple-element.21, bf16[4,4,320,512]{3,2,0,1:T(8,128)(2,1)} %get-tuple-element.20), kind=kOutput, calls=%fused_computation.48 | convolution fusion | flops 10758389760 | bytes 29360128 | tf_op jit(solution)/shard_map/secf,edf->secd/dot_general | solution.py:47
  385.4 15.8 %bitcast_convert_fusion.1 = bf16[4,1024,1024]{2,1,0:T(8,128)(2,1)S(1)} fusion(bf16[4,1024,4,320]{1,3,0,2:T(8,128)(2,1)} %fusion.31, s32[4,4,1024]{2,1,0:T(4,128)S(1)} %dynamic-slice_convert_fusion.9), kind=kOutput, calls=%fused_computation.17 | convolution fusion | flops 10746855424 | bytes 18939904 | tf_op jit(solution)/shard_map/sect,secd->std/dot_general | solution.py:47
  405.7 17.4 %bitcast_convert_fusion = bf16[4,1024,1024]{2,1,0:T(8,128)(2,1)} fusion(bf16[4,4,320,1024]{3,2,1,0:T(8,128)(2,1)} %fusion.57, bf16[4,4,320,512]{3,2,0,1:T(8,128)(2,1)} %get-tuple-element.21, bf16[4,4,320,512]{3,2,0,1:T(8,128)(2,1)} %get-tuple-element.20), kind=kOutput, calls=%fused_computation.11 | convolution fusion | flops 10762584064 | bytes 29360128 | tf_op jit(solution)/shard_map/secd,secf->edf/dot_general | solution.py:47
  423.2 13.2 %fusion.60 = f32[4,4,320,1024]{3,2,0,1:T(8,128)} fusion(bf16[4,4,320,512]{3,2,0,1:T(8,128)(2,1)} %copy-done.12, bf16[4,512,1024]{2,1,0:T(8,128)(2,1)} %all-gather.8.cloned.1.call-done), kind=kOutput, calls=%fused_computation.73 | convolution fusion | flops 5368709120 | bytes 30408704 | tf_op jit(solution)/shard_map/secf,efd->secd/dot_general | solution.py:47
  436.4 18.3 %bitcast_convert_fusion.2 = bf16[4,1024,1024]{2,1,0:T(8,128)(2,1)} fusion(f32[4,4,320,1024]{3,2,0,1:T(8,128)} %fusion.60, f32[4,4,320]{2,1,0:T(4,128)S(1)} %copy-done.65, s32[4,4,1024]{2,1,0:T(4,128)S(1)} %dynamic-slice_convert_fusion.9), kind=kOutput, calls=%fused_computation.18 | convolution fusion | flops 10757341184 | bytes 29446144 | tf_op jit(solution)/shard_map/sect,secd->std/dot_general | solution.py:47
  470.0 10.3 %collective-permute-done.25 = bf16[256,1024]{1,0:T(8,128)(2,1)S(1)} collective-permute-done((bf16[256,1024]{1,0:T(8,128)(2,1)S(1)}, bf16[256,1024]{1,0:T(8,128)(2,1)S(1)}, u32[]{:S(2)}, u32[]{:S(2)}) %collective-permute-start.25) | collective-permute-done | bytes 524320 | tf_op jit(solution)/shard_map/ppermute | solution.py:62
  486.1 20.9 %collective-permute-done.32 = bf16[512,32]{0,1:T(8,128)(2,1)S(1)} collective-permute-done((bf16[512,32]{0,1:T(8,128)(2,1)S(1)}, bf16[512,32]{0,1:T(8,128)(2,1)S(1)}, u32[]{:S(2)}, u32[]{:S(2)}) %collective-permute-start.32) | collective-permute-done | bytes 32800 | tf_op jit(solution)/shard_map/ppermute | solution.py:62
  525.2 15.4 %collective-permute-done.35 = bf16[512,1024]{1,0:T(8,128)(2,1)} collective-permute-done((bf16[512,1024]{1,0:T(8,128)(2,1)S(1)}, bf16[512,1024]{1,0:T(8,128)(2,1)}, u32[]{:S(2)}, u32[]{:S(2)}) %collective-permute-start.35) | collective-permute-done | bytes 1048608 | tf_op jit(solution)/shard_map/ppermute | solution.py:62
  546.4 6.6 fusion.41
  553.0 6.4 fusion.43
  563.4 10.6 %fusion.8 = (f32[4,2,512]{2,1,0:T(2,128)S(1)}, f32[4,1024,512,2]{2,1,3,0:T(8,128)}) fusion(f32[4,2,512,1024]{2,3,1,0:T(8,128)S(1)} %bitcast.344, f32[4,2,512]{2,1,0:T(2,128)S(1)} %bitcast.377, bf16[512,4,2,64]{0,3,2,1:T(8,128)(2,1)} %bitcast.358, bf16[1024,4,128]{0,2,1:T(8,128)(2,1)} %copy-done.22), kind=kOutput, calls=%fused_computation.14 | convolution fusion | flops 549449728 | bytes 34635776 | tf_op jit(solution)/shard_map/bgrd,sgd->grbs/dot_general | solution.py:47
  574.1 8.4 %fusion.10 = bf16[4,2,512,1024]{2,3,1,0:T(8,128)(2,1)S(1)} fusion(f32[4,1024,512,2]{2,1,3,0:T(8,128)} %get-tuple-element.110, f32[4,2,512,1024]{2,3,1,0:T(8,128)S(1)} %bitcast.344, f32[4,2,512]{2,1,0:T(2,128)S(1)} %get-tuple-element.109, f32[4,2,512]{2,1,0:T(2,128)S(1)} %bitcast.378), kind=kLoop, calls=%fused_computation.16 | loop fusion | flops 16777216 | bytes 41975808 | tf_op jit(solution)/shard_map/convert_element_type | solution.py:187
  607.7 8.9 %fusion.104 = bf16[1024,4,64]{0,2,1:T(8,128)(2,1)S(1)} fusion(bf16[512,4,2,64]{0,3,2,1:T(8,128)(2,1)S(1)} %bitcast.359, f32[4,2,512,1024]{2,3,1,0:T(8,128)} %get-tuple-element.103, f32[4,2,512]{2,1,0:T(2,128)S(1)} %bitcast.379, f32[512,4,64]{0,2,1:T(8,128)} %convolution_bitcast_fusion.1), kind=kOutput, calls=%fused_computation.162 | convolution fusion | flops 545783808 | bytes 18366464 | tf_op jit(solution)/shard_map/grbs,bgrd->sgd/dot_general | solution.py:47
  642.1 29.5 %collective-permute-done.44 = f32[33,1024]{1,0:T(8,128)S(1)} collective-permute-done((f32[33,1024]{1,0:T(8,128)S(1)}, f32[33,1024]{1,0:T(8,128)S(1)}, u32[]{:S(2)}, u32[]{:S(2)}) %collective-permute-start.44) | collective-permute-done | bytes 135200 | tf_op jit(solution)/shard_map/ppermute | solution.py:69
  692.5 14.9 %collective-permute-done.38 = f32[1,1024]{1,0:T(1,128)S(1)} collective-permute-done((f32[1,1024]{1,0:T(1,128)S(1)}, f32[1,1024]{1,0:T(1,128)S(1)}, u32[]{:S(2)}, u32[]{:S(2)}) %collective-permute-start.38) | collective-permute-done | bytes 4128 | tf_op jit(solution)/shard_map/ppermute | solution.py:69
  725.4 6.2 fusion.82
  (428 shorter events, 281.2 us)
Async XLA Ops:
  7.2 60.1 %all-gather.4.cloned.1.call-start = ((), (), s32[]{:S(2)}) async-start(), calls=%async_computation.10 | async-start | bytes 3342336 | tf_op jit(solution)/shard_map/all_gather | solution.py:232
  17.6 42.5 %collective-permute-start = (bf16[512,1024]{1,0:T(8,128)(2,1)}, bf16[512,1024]{1,0:T(8,128)(2,1)}, u32[]{:S(2)}, u32[]{:S(2)}) collective-permute-start(bf16[512,1024]{1,0:T(8,128)(2,1)} %fusion.77), channel_id=1, source_target_pairs={{0,1},{1,0},{2,3},{3,2},{4,5},{5,4},{6,7},{7,6},{8,9},{9,8},{10,11... | collective-permute-start | bytes 3145736 | tf_op jit(solution)/shard_map/ppermute | solution.py:62
  34.9 269.4 %all-gather.6.cloned.1.call-start = ((), (), s32[]{:S(2)}) async-start(), calls=%async_computation.11 | async-start | bytes 10485760 | tf_op jit(solution)/shard_map/all_gather | solution.py:243
  116.2 29.2 %collective-permute-start.18 = (bf16[512,1024]{1,0:T(8,128)(2,1)}, bf16[512,1024]{1,0:T(8,128)(2,1)}, u32[]{:S(2)}, u32[]{:S(2)}) collective-permute-start(bf16[512,1024]{1,0:T(8,128)(2,1)} %fusion.76), channel_id=1, source_target_pairs={{0,4},{4,0},{1,5},{5,1},{2,6},{6,2},{3,7},{7,3},{8,12},{12,8},{9,1... | collective-permute-start | bytes 3145736 | tf_op jit(solution)/shard_map/ppermute | solution.py:62
  116.6 45.5 %collective-permute-start.17 = (bf16[512,1024]{1,0:T(8,128)(2,1)}, bf16[512,1024]{1,0:T(8,128)(2,1)S(1)}, u32[]{:S(2)}, u32[]{:S(2)}) collective-permute-start(bf16[512,1024]{1,0:T(8,128)(2,1)} %fusion.76), channel_id=1, source_target_pairs={{0,1},{1,0},{2,3},{3,2},{4,5},{5,4},{6,7},{7,6},{8,9},{9,8},{10,11... | collective-permute-start | bytes 3145736 | tf_op jit(solution)/shard_map/ppermute | solution.py:62
  142.5 52.6 %collective-permute-start.6 = (bf16[512,1024]{1,0:T(8,128)(2,1)S(1)}, bf16[512,1024]{1,0:T(8,128)(2,1)S(1)}, u32[]{:S(2)}, u32[]{:S(2)}) collective-permute-start(bf16[512,1024]{1,0:T(8,128)(2,1)S(1)} %multiply_convert_fusion.5), channel_id=1, source_target_pairs={{0,4},{4,0},{1,5},{5,1},{2,6},{6,2},{3,7},{7,3},{8,12},{12,8},{9,1... | collective-permute-start | bytes 3145736 | tf_op jit(solution)/shard_map/ppermute | solution.py:62
  143.8 53.1 %collective-permute-start.5 = (bf16[512,1024]{1,0:T(8,128)(2,1)S(1)}, bf16[512,1024]{1,0:T(8,128)(2,1)S(1)}, u32[]{:S(2)}, u32[]{:S(2)}) collective-permute-start(bf16[512,1024]{1,0:T(8,128)(2,1)S(1)} %multiply_convert_fusion.5), channel_id=1, source_target_pairs={{0,1},{1,0},{2,3},{3,2},{4,5},{5,4},{6,7},{7,6},{8,9},{9,8},{10,11... | collective-permute-start | bytes 3145736 | tf_op jit(solution)/shard_map/ppermute | solution.py:62
  146.5 48.6 %collective-permute-start.19 = (bf16[256,1024]{1,0:T(8,128)(2,1)S(1)}, bf16[256,1024]{1,0:T(8,128)(2,1)S(1)}, u32[]{:S(2)}, u32[]{:S(2)}) collective-permute-start(bf16[256,1024]{1,0:T(8,128)(2,1)S(1)} %slice.343), channel_id=1, source_target_pairs={{0,1},{1,0},{2,3},{3,2},{4,5},{5,4},{6,7},{7,6},{8,9},{9,8},{10,11... | collective-permute-start | bytes 1572872 | tf_op jit(solution)/shard_map/ppermute | solution.py:62
  162.1 34.7 %collective-permute-start.20 = (bf16[256,1024]{1,0:T(8,128)(2,1)S(1)}, bf16[256,1024]{1,0:T(8,128)(2,1)S(1)}, u32[]{:S(2)}, u32[]{:S(2)}) collective-permute-start(bf16[256,1024]{1,0:T(8,128)(2,1)S(1)} %slice.344), channel_id=1, source_target_pairs={{0,4},{4,0},{1,5},{5,1},{2,6},{6,2},{3,7},{7,3},{8,12},{12,8},{9,1... | collective-permute-start | bytes 1572872 | tf_op jit(solution)/shard_map/ppermute | solution.py:62
  200.6 53.2 %collective-permute-start.9 = (bf16[1024,1024]{1,0:T(8,128)(2,1)}, bf16[1024,1024]{1,0:T(8,128)(2,1)}, u32[]{:S(2)}, u32[]{:S(2)}) collective-permute-start(bf16[1024,1024]{1,0:T(8,128)(2,1)} %get-tuple-element.45), channel_id=1, source_target_pairs={{0,2},{2,0},{1,3},{3,1},{4,6},{6,4},{5,7},{7,5},{8,10},{10,8},{9,1... | collective-permute-start | bytes 6291464 | tf_op jit(solution)/shard_map/ppermute | solution.py:62
  214.1 39.7 %collective-permute-start.10 = (bf16[1024,1024]{1,0:T(8,128)(2,1)}, bf16[1024,1024]{1,0:T(8,128)(2,1)}, u32[]{:S(2)}, u32[]{:S(2)}) collective-permute-start(bf16[1024,1024]{1,0:T(8,128)(2,1)} %get-tuple-element.47), channel_id=1, source_target_pairs={{0,2},{2,0},{1,3},{3,1},{4,6},{6,4},{5,7},{7,5},{8,10},{10,8},{9,1... | collective-permute-start | bytes 6291464 | tf_op jit(solution)/shard_map/ppermute | solution.py:62
  214.1 33.7 %all-to-all-start.2 = ((bf16[16,32,1024]{2,1,0:T(8,128)(2,1)}), bf16[16,32,1024]{2,1,0:T(8,128)(2,1)}, u32[]{:S(2)}, u32[]{:S(2)}) async-start(bf16[16,32,1024]{2,1,0:T(8,128)(2,1)} %param.24), calls=%async_computation.2 | async-start | bytes 2097152 | tf_op jit(solution)/shard_map/all_to_all | solution.py:237
  228.1 101.2 %all-gather.8.cloned.1.call-start = ((), (), s32[]{:S(2)}) async-start(), calls=%async_computation.12 | async-start | bytes 5242880 | tf_op jit(solution)/shard_map/all_gather | solution.py:244
  250.1 428.5 %reduce-scatter.11.cloned.1.call-start = ((), (), s32[]{:S(2)}) async-start(), calls=%async_computation.16 | async-start | bytes 5242880 | tf_op jit(solution)/shard_map/reduce_scatter | solution.py:332
  252.6 30.2 %collective-permute-start.21 = (bf16[1024,1024]{1,0:T(8,128)(2,1)S(1)}, bf16[1024,1024]{1,0:T(8,128)(2,1)}, u32[]{:S(2)}, u32[]{:S(2)}) collective-permute-start(bf16[1024,1024]{1,0:T(8,128)(2,1)S(1)} %get-tuple-element.53), channel_id=1, source_target_pairs={{0,2},{2,0},{1,3},{3,1},{4,6},{6,4},{5,7},{7,5},{8,10},{10,8},{9,1... | collective-permute-start | bytes 6291464 | tf_op jit(solution)/shard_map/ppermute | solution.py:62
  253.4 29.5 %collective-permute-start.22 = (bf16[1024,1024]{1,0:T(8,128)(2,1)S(1)}, bf16[1024,1024]{1,0:T(8,128)(2,1)}, u32[]{:S(2)}, u32[]{:S(2)}) collective-permute-start(bf16[1024,1024]{1,0:T(8,128)(2,1)S(1)} %get-tuple-element.55), channel_id=1, source_target_pairs={{0,2},{2,0},{1,3},{3,1},{4,6},{6,4},{5,7},{7,5},{8,10},{10,8},{9,1... | collective-permute-start | bytes 6291464 | tf_op jit(solution)/shard_map/ppermute | solution.py:62
  363.2 353.4 %reduce-scatter.9.cloned.1.call-start = ((), (), s32[]{:S(2)}) async-start(), calls=%async_computation.15 | async-start | bytes 10485760 | tf_op jit(solution)/shard_map/reduce_scatter | solution.py:334
  367.1 91.8 %collective-permute-start.29 = (bf16[1024,32]{0,1:T(8,128)(2,1)S(1)}, bf16[1024,32]{0,1:T(8,128)(2,1)}, u32[]{:S(2)}, u32[]{:S(2)}) collective-permute-start(bf16[1024,32]{0,1:T(8,128)(2,1)S(1)} %get-tuple-element.80), channel_id=1, source_target_pairs={{0,2},{2,0},{1,3},{3,1},{4,6},{6,4},{5,7},{7,5},{8,10},{10,8},{9,1... | collective-permute-start | bytes 196616 | tf_op jit(solution)/shard_map/ppermute | solution.py:62
  367.2 92.0 %collective-permute-start.30 = (bf16[1024,32]{0,1:T(8,128)(2,1)S(1)}, bf16[1024,32]{0,1:T(8,128)(2,1)}, u32[]{:S(2)}, u32[]{:S(2)}) collective-permute-start(bf16[1024,32]{0,1:T(8,128)(2,1)S(1)} %get-tuple-element.81), channel_id=1, source_target_pairs={{0,2},{2,0},{1,3},{3,1},{4,6},{6,4},{5,7},{7,5},{8,10},{10,8},{9,1... | collective-permute-start | bytes 196616 | tf_op jit(solution)/shard_map/ppermute | solution.py:62
  405.1 55.0 %collective-permute-start.23 = (bf16[1024,1024]{1,0:T(8,128)(2,1)}, bf16[1024,1024]{1,0:T(8,128)(2,1)}, u32[]{:S(2)}, u32[]{:S(2)}) collective-permute-start(bf16[1024,1024]{1,0:T(8,128)(2,1)} %get-tuple-element.28), channel_id=1, source_target_pairs={{0,2},{2,0},{1,3},{3,1},{4,6},{6,4},{5,7},{7,5},{8,10},{10,8},{9,1... | collective-permute-start | bytes 6291464 | tf_op jit(solution)/shard_map/ppermute | solution.py:62
  405.4 54.8 %collective-permute-start.24 = (bf16[1024,1024]{1,0:T(8,128)(2,1)S(1)}, bf16[1024,1024]{1,0:T(8,128)(2,1)}, u32[]{:S(2)}, u32[]{:S(2)}) collective-permute-start(bf16[1024,1024]{1,0:T(8,128)(2,1)S(1)} %get-tuple-element.29), channel_id=1, source_target_pairs={{0,2},{2,0},{1,3},{3,1},{4,6},{6,4},{5,7},{7,5},{8,10},{10,8},{9,1... | collective-permute-start | bytes 6291464 | tf_op jit(solution)/shard_map/ppermute | solution.py:62
  423.1 309.1 %reduce-scatter.7.cloned.1.call-start = ((), (), s32[]{:S(2)}) async-start(), calls=%async_computation.14 | async-start | bytes 1114112 | tf_op jit(solution)/shard_map/reduce_scatter | solution.py:355
  458.7 56.6 %collective-permute-start.11 = (bf16[1024,1024]{1,0:T(8,128)(2,1)}, bf16[1024,1024]{1,0:T(8,128)(2,1)}, u32[]{:S(2)}, u32[]{:S(2)}) collective-permute-start(bf16[1024,1024]{1,0:T(8,128)(2,1)} %get-tuple-element.32), channel_id=1, source_target_pairs={{0,2},{2,0},{1,3},{3,1},{4,6},{6,4},{5,7},{7,5},{8,10},{10,8},{9,1... | collective-permute-start | bytes 6291464 | tf_op jit(solution)/shard_map/ppermute | solution.py:62
  458.9 56.4 %collective-permute-start.12 = (bf16[1024,1024]{1,0:T(8,128)(2,1)S(1)}, bf16[1024,1024]{1,0:T(8,128)(2,1)}, u32[]{:S(2)}, u32[]{:S(2)}) collective-permute-start(bf16[1024,1024]{1,0:T(8,128)(2,1)S(1)} %get-tuple-element.33), channel_id=1, source_target_pairs={{0,2},{2,0},{1,3},{3,1},{4,6},{6,4},{5,7},{7,5},{8,10},{10,8},{9,1... | collective-permute-start | bytes 6291464 | tf_op jit(solution)/shard_map/ppermute | solution.py:62
  520.8 107.3 %collective-permute-start.13 = (bf16[256,1024]{1,0:T(8,128)(2,1)}, bf16[256,1024]{1,0:T(8,128)(2,1)}, u32[]{:S(2)}, u32[]{:S(2)}) collective-permute-start(bf16[256,1024]{1,0:T(8,128)(2,1)} %get-tuple-element.72), channel_id=1, source_target_pairs={{0,4},{4,0},{1,5},{5,1},{2,6},{6,2},{3,7},{7,3},{8,12},{12,8},{9,1... | collective-permute-start | bytes 1572872 | tf_op jit(solution)/shard_map/ppermute | solution.py:62
  522.3 118.2 %collective-permute-start.15 = (bf16[256,1024]{1,0:T(8,128)(2,1)}, bf16[256,1024]{1,0:T(8,128)(2,1)}, u32[]{:S(2)}, u32[]{:S(2)}) collective-permute-start(bf16[256,1024]{1,0:T(8,128)(2,1)} %get-tuple-element.73), channel_id=1, source_target_pairs={{0,1},{1,0},{2,3},{3,2},{4,5},{5,4},{6,7},{7,6},{8,9},{9,8},{10,11... | collective-permute-start | bytes 1572872 | tf_op jit(solution)/shard_map/ppermute | solution.py:62
  605.6 137.8 %reduce-scatter.5.cloned.1.call-start = ((), (), s32[]{:S(2)}) async-start(), calls=%async_computation.13 | async-start | bytes 2228224 | tf_op jit(solution)/shard_map/reduce_scatter | solution.py:371
  627.3 58.9 %collective-permute-start.36 = (bf16[512,1024]{1,0:T(8,128)(2,1)}, bf16[512,1024]{1,0:T(8,128)(2,1)}, u32[]{:S(2)}, u32[]{:S(2)}) collective-permute-start(bf16[512,1024]{1,0:T(8,128)(2,1)} %dynamic-slice_convert_fusion), channel_id=1, source_target_pairs={{0,1},{1,0},{2,3},{3,2},{4,5},{5,4},{6,7},{7,6},{8,9},{9,8},{10,11... | collective-permute-start | bytes 3145736 | tf_op jit(solution)/shard_map/ppermute | solution.py:62
  632.3 93.1 %collective-permute-start.14 = (bf16[512,1024]{1,0:T(8,128)(2,1)}, bf16[512,1024]{1,0:T(8,128)(2,1)}, u32[]{:S(2)}, u32[]{:S(2)}) collective-permute-start(bf16[512,1024]{1,0:T(8,128)(2,1)} %pad_maximum_fusion.22), channel_id=1, source_target_pairs={{0,1},{1,0},{2,3},{3,2},{4,5},{5,4},{6,7},{7,6},{8,9},{9,8},{10,11... | collective-permute-start | bytes 3145736 | tf_op jit(solution)/shard_map/ppermute | solution.py:62
  639.1 32.4 %collective-permute-start.44 = (f32[33,1024]{1,0:T(8,128)S(1)}, f32[33,1024]{1,0:T(8,128)S(1)}, u32[]{:S(2)}, u32[]{:S(2)}) collective-permute-start(f32[33,1024]{1,0:T(8,128)S(1)} %add.266), channel_id=1, source_target_pairs={{0,1},{1,0},{2,3},{3,2},{4,5},{5,4},{6,7},{7,6},{8,9},{9,8},{10,11... | collective-permute-start | bytes 405512 | tf_op jit(solution)/shard_map/ppermute | solution.py:69
  672.7 52.6 %collective-permute-start.16 = (bf16[512,1024]{1,0:T(8,128)(2,1)}, bf16[512,1024]{1,0:T(8,128)(2,1)}, u32[]{:S(2)}, u32[]{:S(2)}) collective-permute-start(bf16[512,1024]{1,0:T(8,128)(2,1)} %pad_maximum_fusion.23), channel_id=1, source_target_pairs={{0,4},{4,0},{1,5},{5,1},{2,6},{6,2},{3,7},{7,3},{8,12},{12,8},{9,1... | collective-permute-start | bytes 3145736 | tf_op jit(solution)/shard_map/ppermute | solution.py:62
  681.6 39.4 %all-to-all-start.5 = ((bf16[4,128,1024]{2,0,1:T(4,128)(2,1)}), bf16[4,128,1024]{2,0,1:T(4,128)(2,1)}, u32[]{:S(2)}, u32[]{:S(2)}) async-start(bf16[4,128,1024]{2,0,1:T(4,128)(2,1)} %copy.66), calls=%async_computation.9 | async-start | bytes 2097152 | tf_op jit(solution)/shard_map/all_to_all | solution.py:240
  (107 other events, 1705.0 us)
Sparse Core Ops, SparseCore 0:
  10.9 56.4 all-gather.3
  69.5 148.6 all-gather.5
  250.2 78.9 all-gather.7
  363.3 75.2 reduce-scatter.10
  440.8 145.2 reduce-scatter.8
  605.7 57.4 reduce-scatter.6
  667.5 64.4 reduce-scatter.4

commit v2 on v1

v2 whole, which is shorter than its diff:
```python
import functools

import jax
import jax.numpy as jnp
from jax import lax
from jax.experimental import pallas as pl
from jax.experimental.pallas import tpu as pltpu
from jax.sharding import Mesh, PartitionSpec as P

CAP = 320
HEAD = 64
HALF = HEAD // 2
LANES = 2 * HEAD
BLOCK = 256
norm_eps = 1e-06
attn_scale = 0.015625
residual_scale = 0.22
rope_base = 10000.0
masked_score = -1e30
f32 = jnp.float32
bf16 = jnp.bfloat16


def row_scale(values):
    return lax.rsqrt(jnp.mean(values * values, axis=-1, keepdims=True) + norm_eps)


def contract(left, right, left_dim, right_dim):
    return lax.dot_general(
        left, right, (((left_dim,), (right_dim,)), ((), ())), preferred_element_type=f32
    )


def ein(spec, *operands):
    return jnp.einsum(spec, *operands, preferred_element_type=f32)


def norm_backward(normed_grad, source, gain):
    scale_rows = row_scale(source)
    unit_rows = source * scale_rows
    scaled_grad = normed_grad * gain
    gain_grad = jnp.sum(normed_grad * unit_rows, axis=0)
    source_grad = scale_rows * (
        scaled_grad - unit_rows * jnp.mean(scaled_grad * unit_rows, axis=-1, keepdims=True)
    )
    return (source_grad, gain_grad)


def swap(values, axis):
    return lax.ppermute(values, axis, [(0, 1), (1, 0)])


def butterfly_sum(values, sizes):
    for axis, size in sizes:
        step = 1
        while step < size:
            values = values + lax.ppermute(values, axis, [(i, i ^ step) for i in range(size)])
            step *= 2
    return values


def in_order(mine, theirs, first):
    return jnp.concatenate(
        [jnp.where(first, mine, theirs), jnp.where(first, theirs, mine)], axis=0
    )


def gather_rows(rows, tensor_size):
    if tensor_size != 2:
        return lax.all_gather(rows, "tensor", axis=0, tiled=True)
    return in_order(rows, swap(rows, "tensor"), lax.axis_index("tensor") == 0)


def scatter_rows(values, tensor_size):
    if tensor_size != 2:
        return lax.psum_scatter(
            values.astype(bf16), "tensor", scatter_dimension=0, tiled=True
        ).astype(f32)
    half = values.shape[0] // 2
    me = lax.axis_index("tensor")
    give = lax.dynamic_slice_in_dim(values, (1 - me) * half, half, 0).astype(bf16)
    keep = lax.dynamic_slice_in_dim(values, me * half, half, 0)
    return keep.astype(f32) + swap(give, "tensor").astype(f32)


def gather_group(rows, tensor_size):
    if tensor_size != 2:
        own = gather_rows(rows, tensor_size)
        across = swap(own, "y")
    else:
        first = lax.axis_index("tensor") == 0
        half = rows.shape[0] // 2
        by_tensor, by_y = swap(rows, "tensor"), swap(rows, "y")
        corner = jnp.concatenate(
            [swap(by_y[:half], "tensor"), swap(by_tensor[half:], "y")], axis=0
        )
        own = in_order(rows, by_tensor, first)
        across = in_order(by_y, corner, first)
    return jnp.stack([own, across, swap(own, "core"), swap(across, "core")])


def scatter_group(parts, tensor_size):
    pair = [parts[i].astype(f32) + swap(parts[i + 2].astype(bf16), "core").astype(f32) for i in (0, 1)]
    own, across = pair
    if tensor_size != 2:
        own = own + swap(across.astype(bf16), "y").astype(f32)
        return scatter_rows(own, tensor_size)
    me = lax.axis_index("tensor")
    rows = own.shape[0] // 2
    half = rows // 2

    def take(values, which):
        return lax.dynamic_slice_in_dim(values, which * rows, rows, 0)

    mine, by_tensor = take(own, me), take(own, 1 - me)
    by_y, corner = take(across, me), take(across, 1 - me).astype(bf16)
    low, high = swap(corner[:half], "tensor"), swap(corner[half:], "y")
    by_y = jnp.concatenate([by_y[:half] + low.astype(f32), by_y[half:]], axis=0)
    by_tensor = jnp.concatenate([by_tensor[:half], by_tensor[half:] + high.astype(f32)], axis=0)
    return (
        mine
        + swap(by_tensor.astype(bf16), "tensor").astype(f32)
        + swap(by_y.astype(bf16), "y").astype(f32)
    )


def rope_lanes(values, cosine, sine, first, direction):
    lanes = values.shape[1]
    turned = jnp.where(
        first, pltpu.roll(values, lanes - HALF, 1), pltpu.roll(values, HALF, 1)
    )
    return values * cosine + direction * (turned * sine)


def lane_ids(rows):
    return lax.broadcasted_iota(jnp.int32, (rows, LANES), 1)


def attention_forward_kernel(pre_ref, cos_ref, sin_ref, mixed_ref, rot_ref, lse_ref):
    seq_len = pre_ref.shape[0]
    lane = lane_ids(seq_len)
    first = (lane & (2 * HALF - 1)) < HALF
    low = lane < HEAD
    cosine, sine = cos_ref[...], sin_ref[...]
    query = rope_lanes(pre_ref[:, :LANES], cosine, sine, first, 1.0).astype(bf16)
    kv = pre_ref[:, LANES:]
    kv = jnp.where(low, rope_lanes(kv, cosine, sine, first, 1.0), kv)
    rot_ref[:, :LANES] = query
    rot_ref[:, LANES:] = kv.astype(bf16)
    keys, values_in = head_pairs(kv, low)
    block = min(BLOCK, seq_len)
    for start in range(0, seq_len, block):
        stop = start + block
        allowed = causal(block, stop, start)
        total = jnp.zeros((block, LANES), f32)
        lses = []
        for head in (0, 1):
            scores = (
                contract(query[start:stop], keys[head][:stop], 1, 1) * attn_scale
            )
            scores = jnp.where(allowed, scores, masked_score)
            top = jnp.max(scores, axis=1, keepdims=True)
            raised = jnp.exp(scores - top)
            summed = jnp.sum(raised, axis=1, keepdims=True)
            prob = (raised * (1.0 / summed)).astype(bf16)
            total = total + jnp.dot(prob, values_in[head][:stop], preferred_element_type=f32)
            lses.append(top + jnp.log(summed))
        mixed_ref[start:stop, :] = total.astype(bf16)
        lse_ref[start:stop, :] = jnp.where(lane_ids(block) < HEAD, lses[0], lses[1])


def head_pairs(kv, low):
    kv = kv.astype(f32)
    turned = pltpu.roll(kv, HEAD, 1)
    zero = jnp.zeros_like(kv)
    keys = [jnp.where(low, kv, zero).astype(bf16), jnp.where(low, zero, turned).astype(bf16)]
    values_in = [jnp.where(low, turned, zero).astype(bf16), jnp.where(low, zero, kv).astype(bf16)]
    return keys, values_in


def causal(rows, columns, start):
    return lax.broadcasted_iota(jnp.int32, (rows, columns), 1) <= start + lax.broadcasted_iota(
        jnp.int32, (rows, columns), 0
    )


def attention_backward_kernel(
    rot_ref, grad_ref, lse_ref, cos_ref, sin_ref, out_ref, key_acc, value_acc
):
    seq_len = rot_ref.shape[0]
    lane = lane_ids(seq_len)
    first = (lane & (2 * HALF - 1)) < HALF
    low = lane < HEAD
    cosine, sine = cos_ref[...], sin_ref[...]
    keys, values_in = head_pairs(rot_ref[:, LANES:], low)
    key_acc[...] = jnp.zeros_like(key_acc)
    value_acc[...] = jnp.zeros_like(value_acc)
    block = min(BLOCK, seq_len)
    for start in range(0, seq_len, block):
        stop = start + block
        allowed = causal(block, stop, start)
        query = rot_ref[start:stop, :LANES]
        grad = grad_ref[start:stop, :]
        query_grad = jnp.zeros((block, LANES), f32)
        for head in (0, 1):
            scores = contract(query, keys[head][:stop], 1, 1) * attn_scale
            log_total = lse_ref[start:stop, head * HEAD : head * HEAD + 1]
            prob = jnp.where(allowed, jnp.exp(jnp.where(allowed, scores - log_total, 0.0)), 0.0)
            prob_grad = contract(grad, values_in[head][:stop], 1, 1)
            row_dot = jnp.sum(prob * prob_grad, axis=1, keepdims=True)
            score_grad = (prob * (prob_grad - row_dot)).astype(bf16)
            query_grad = query_grad + jnp.dot(
                score_grad, keys[head][:stop], preferred_element_type=f32
            )
            key_acc[head, :stop, :] += contract(score_grad, query, 0, 0)
            value_acc[head, :stop, :] += contract(prob.astype(bf16), grad, 0, 0)
        lane_block = (lane_ids(block) & (2 * HALF - 1)) < HALF
        out_ref[start:stop, :LANES] = rope_lanes(
            query_grad * attn_scale, cosine[start:stop], sine[start:stop], lane_block, -1.0
        ).astype(bf16)
    key_grad = (key_acc[0] + pltpu.roll(key_acc[1], HEAD, 1)) * attn_scale
    key_grad = rope_lanes(jnp.where(low, key_grad, 0.0), cosine, sine, first, -1.0)
    value_grad = pltpu.roll(value_acc[0], HEAD, 1) + value_acc[1]
    out_ref[:, LANES:] = jnp.where(low, key_grad, value_grad).astype(bf16)


def by_head(width):
    return lambda seq_len: pl.BlockSpec((seq_len, width), lambda g: (0, g))


def attention_forward(pre, cosine, sine):
    seq_len, width = pre.shape
    groups = width // (2 * LANES)
    whole = pl.BlockSpec((seq_len, LANES), lambda g: (0, 0))
    wide, narrow = by_head(2 * LANES)(seq_len), by_head(LANES)(seq_len)
    return pl.pallas_call(
        attention_forward_kernel,
        grid=(groups,),
        in_specs=[wide, whole, whole],
        out_specs=[narrow, wide, narrow],
        out_shape=[
            jax.ShapeDtypeStruct((seq_len, width // 2), bf16),
            jax.ShapeDtypeStruct((seq_len, width), bf16),
            jax.ShapeDtypeStruct((seq_len, width // 2), f32),
        ],
        cost_estimate=pl.CostEstimate(
            flops=6 * groups * seq_len * seq_len * LANES,
            bytes_accessed=10 * seq_len * width,
            transcendentals=groups * seq_len * seq_len,
        ),
        name="attention_forward",
    )(pre, cosine, sine)


def attention_backward(rot, grad, lse, cosine, sine):
    seq_len, width = rot.shape
    groups = width // (2 * LANES)
    whole = pl.BlockSpec((seq_len, LANES), lambda g: (0, 0))
    wide, narrow = by_head(2 * LANES)(seq_len), by_head(LANES)(seq_len)
    return pl.pallas_call(
        attention_backward_kernel,
        grid=(groups,),
        in_specs=[wide, narrow, narrow, whole, whole],
        out_specs=wide,
        out_shape=jax.ShapeDtypeStruct((seq_len, width), bf16),
        scratch_shapes=[pltpu.VMEM((2, seq_len, LANES), f32)] * 2,
        cost_estimate=pl.CostEstimate(
            flops=16 * groups * seq_len * seq_len * LANES,
            bytes_accessed=10 * seq_len * width,
            transcendentals=groups * seq_len * seq_len,
        ),
        name="attention_backward",
    )(rot, grad, lse, cosine, sine)


def expert_kernel(carried, member_ref, tokens_ref, grad_ref, code_ref, gate_ref, weight_ref, *refs):
    if carried:
        moe_in, normed_in, *refs = refs
    moe_ref, normed_ref, pair_ref, part_ref, both, down, both_acc, down_acc = refs
    step = pl.program_id(0)
    shards_z, members, rows = weight_ref.shape[:3]
    hidden = down.shape[0]
    both_rows = both.shape[0] // (shards_z * members)
    down_rows = hidden // (shards_z * members)

    def places():
        for z in range(shards_z):
            for rel in range(members):
                at = z * members + (member_ref[0] ^ rel)
                yield (
                    z,
                    rel,
                    pl.ds(pl.multiple_of(at * both_rows, both_rows), both_rows),
                    pl.ds(pl.multiple_of(at * down_rows, down_rows), down_rows),
                )

    @pl.when(step == 0)
    def _():
        for z, rel, both_at, down_at in places():
            both[both_at, :] = weight_ref[z, rel, :both_rows, :]
            down[down_at, :] = weight_ref[z, rel, both_rows:, :]
        both_acc[...] = jnp.zeros_like(both_acc)
        down_acc[...] = jnp.zeros_like(down_acc)

    seq_len = tokens_ref.shape[1]
    slot = lax.broadcasted_iota(jnp.int32, (CAP, seq_len), 0)
    match = code_ref[0] == slot
    dispatch = jnp.where(match, 1.0, 0.0).astype(bf16)
    slot_gate = jnp.sum(jnp.where(match, gate_ref[0], 0.0), axis=1, keepdims=True)
    expert_in = jnp.dot(dispatch, tokens_ref[0], preferred_element_type=f32).astype(bf16)
    gate_pre = jnp.dot(expert_in, both[:, :hidden], preferred_element_type=f32)
    up_pre = jnp.dot(expert_in, both[:, hidden:], preferred_element_type=f32)
    sigmoid = 1.0 / (1.0 + jnp.exp(-gate_pre))
    silu = gate_pre * sigmoid
    hidden_act = (silu * up_pre).astype(bf16)
    expert_out = jnp.dot(hidden_act, down[...], preferred_element_type=f32)
    weighted = (slot_gate * expert_out).astype(bf16)
    moe = contract(dispatch, weighted, 0, 0)
    if carried:
        moe = moe + moe_in[0].astype(f32)
    moe_ref[0] = moe.astype(bf16)

    slot_grad = jnp.dot(dispatch, grad_ref[0], preferred_element_type=f32)
    raw_grad = contract(slot_grad.astype(bf16), down[...], 1, 1)
    slot_gate_grad = jnp.sum(hidden_act.astype(f32) * raw_grad, axis=1, keepdims=True)
    pair_ref[0] = jnp.sum(jnp.where(match, slot_gate_grad, 0.0), axis=0, keepdims=True)
    hidden_grad = slot_gate * raw_grad
    gate_grad = (
        hidden_grad * up_pre * sigmoid * (1.0 + gate_pre * (1.0 - sigmoid))
    ).astype(bf16)
    up_grad = (hidden_grad * silu).astype(bf16)
    down_acc[...] += contract(hidden_act, (slot_gate * slot_grad).astype(bf16), 0, 0)
    both_acc[:, :hidden] += contract(expert_in, gate_grad, 0, 0)
    both_acc[:, hidden:] += contract(expert_in, up_grad, 0, 0)
    in_grad = (
        contract(gate_grad, both[:, :hidden], 1, 1) + contract(up_grad, both[:, hidden:], 1, 1)
    ).astype(bf16)
    normed = contract(dispatch, in_grad, 0, 0)
    if carried:
        normed = normed + normed_in[0].astype(f32)
    normed_ref[0] = normed.astype(bf16)

    @pl.when(step == pl.num_programs(0) - 1)
    def _():
        for z, rel, both_at, down_at in places():
            part_ref[z, rel, :both_rows, :] = both_acc[both_at, :].astype(bf16)
            part_ref[z, rel, both_rows:, :] = down_acc[down_at, :].astype(bf16)


def run_expert(member, tokens, grads, code, gate, weight, carry):
    sequences, seq_len, width = tokens.shape
    shards_z, members, rows, both_width = weight.shape
    hidden = both_width // 2
    per_seq = pl.BlockSpec((1, seq_len, width), lambda s: (s, 0, 0))
    per_row = pl.BlockSpec((1, 1, seq_len), lambda s: (s, 0, 0))
    every = pl.BlockSpec(weight.shape, lambda s: (0, 0, 0, 0), pipeline_mode=pl.Buffered(1))
    part = pl.BlockSpec(weight.shape, lambda s: (0, 0, 0, 0))
    slots = sequences * CAP
    return pl.pallas_call(
        functools.partial(expert_kernel, bool(carry)),
        grid=(sequences,),
        in_specs=[
            pl.BlockSpec(memory_space=pltpu.SMEM),
            per_seq,
            per_seq,
            per_row,
            per_row,
            every,
        ]
        + [per_seq] * len(carry),
        out_specs=[per_seq, per_seq, per_row, part],
        out_shape=[
            jax.ShapeDtypeStruct(tokens.shape, bf16),
            jax.ShapeDtypeStruct(tokens.shape, bf16),
            jax.ShapeDtypeStruct((sequences, 1, seq_len), f32),
            jax.ShapeDtypeStruct(weight.shape, bf16),
        ],
        scratch_shapes=[
            pltpu.VMEM((width, both_width), bf16),
            pltpu.VMEM((hidden, width), bf16),
            pltpu.VMEM((width, both_width), f32),
            pltpu.VMEM((hidden, width), f32),
        ],
        compiler_params=pltpu.CompilerParams(vmem_limit_bytes=66_000_000),
        cost_estimate=pl.CostEstimate(
            flops=2 * slots * width * (4 * seq_len + 9 * hidden),
            bytes_accessed=12 * sequences * seq_len * width + 4 * weight.size,
            transcendentals=slots * hidden,
        ),
        name="expert",
    )(member, tokens, grads, code, gate, weight, *carry)


def shards(
    sizes,
    block_input,
    positions,
    expert_ids,
    attn_gain,
    query_weight,
    kv_weight,
    out_weight,
    ffn_gain,
    router_weight,
    gate_weight,
    up_weight,
    down_weight,
    out_grad,
):
    tensor_size, z_size = sizes["tensor"], sizes["z"]
    seq_len = positions.shape[0]
    width = block_input.shape[1]
    shard_rows, groups = kv_weight.shape[:2]
    q_width = query_weight.shape[1]
    wide = 2 * q_width
    expert_count = router_weight.shape[1]
    experts_local = gate_weight.shape[0]
    owned = experts_local // 4
    hidden = gate_weight.shape[2]
    my_y, my_core = lax.axis_index("y"), lax.axis_index("core")
    my_tensor = lax.axis_index("tensor")
    y_first, core_first, tensor_first = my_y == 0, my_core == 0, my_tensor == 0

    def at(values, index):
        return lax.dynamic_index_in_dim(values, index, 0, keepdims=False)

    packed = jnp.concatenate(
        [
            jnp.concatenate([query_weight.reshape(shard_rows, groups, -1), kv_weight], axis=2)
            .reshape(shard_rows, wide),
            out_weight.T,
        ],
        axis=1,
    )
    by_z = lax.all_gather(packed, "z", axis=0, tiled=False)

    experts = jnp.concatenate(
        [jnp.concatenate([gate_weight, up_weight], axis=2), down_weight], axis=1
    )
    rows, both_width = experts.shape[1:]
    grouped = experts.reshape(2, 2, owned, rows, both_width)
    own_y, from_y = at(grouped, my_y), swap(at(grouped, 1 - my_y), "y")
    pieces = [
        at(own_y, my_core),
        swap(at(own_y, 1 - my_core), "core"),
        at(from_y, my_core),
        swap(at(from_y, 1 - my_core), "core"),
    ]
    weights = [
        lax.all_gather(jnp.stack([piece[e] for piece in pieces]), "z", axis=0, tiled=False)
        for e in range(owned)
    ]

    def stacked(mine, theirs, is_first):
        return jnp.stack([jnp.where(is_first, mine, theirs), jnp.where(is_first, theirs, mine)], 1)

    by_y = stacked(by_z, swap(by_z, "y"), y_first)
    other = swap(by_y, "core")
    packed_full = jnp.stack(
        [jnp.where(core_first, by_y, other), jnp.where(core_first, other, by_y)], 2
    ).reshape(width, -1)
    qkv_full, out_full = packed_full[:, :wide], packed_full[:, wide:]

    ids_t = expert_ids.T
    hits = jnp.zeros((expert_count, seq_len), jnp.bool_)
    for k in range(ids_t.shape[0]):
        hits = hits | (ids_t[k][None, :] == jnp.arange(expert_count)[:, None])
    token_ids = jnp.arange(seq_len)
    earlier = (token_ids[:, None] < token_ids[None, :]).astype(bf16)
    rank = jnp.dot(hits.astype(bf16), earlier, preferred_element_type=f32)
    code = jnp.where(hits, jnp.where(rank < CAP, rank, -1.0), -2.0)
    code_y = swap(code, "y")
    codes = jnp.stack([code, code_y, swap(code, "core"), swap(code_y, "core")])

    half_dim = HEAD // 2
    frequency = rope_base ** (-(jnp.arange(half_dim, dtype=f32) * 2.0 / HEAD))
    angles = positions.astype(f32)[:, None] * frequency[None, :]
    cosine = jnp.tile(jnp.cos(angles), (1, 4))
    sine = jnp.tile(jnp.concatenate([-jnp.sin(angles), jnp.sin(angles)], axis=1), (1, 2))

    input_rows = block_input.astype(f32)
    attn_normed = (input_rows * row_scale(input_rows) * attn_gain).astype(bf16)
    attn_tokens = gather_rows(attn_normed, tensor_size)
    grad_rows = out_grad.astype(f32)
    moe_rows = (residual_scale * grad_rows).astype(bf16)
    qkv_full, moe_rows, codes = lax.optimization_barrier((qkv_full, moe_rows, codes))
    moe_grad = gather_group(moe_rows, tensor_size)
    qkv_pre = jnp.dot(attn_tokens, qkv_full, preferred_element_type=f32)
    attn_mixed, qkv_rot, log_totals = attention_forward(qkv_pre, cosine, sine)
    attn_mixed, moe_grad = lax.optimization_barrier((attn_mixed, moe_grad))
    attn_out = scatter_rows(contract(attn_mixed, out_full, 1, 1), tensor_size)
    hidden_state = input_rows + residual_scale * attn_out
    ffn_normed = (hidden_state * row_scale(hidden_state) * ffn_gain).astype(bf16)

    tokens = gather_group(ffn_normed, tensor_size)
    logits = ein("dx,std->sxt", router_weight, tokens)
    chosen = codes > -1.5
    top_logit = jnp.max(jnp.where(chosen, logits, -jnp.inf), axis=1, keepdims=True)
    raised = jnp.where(chosen, jnp.exp(jnp.where(chosen, logits - top_logit, 0.0)), 0.0)
    gates = raised / jnp.sum(raised, axis=1, keepdims=True)
    member = my_y * 2 + my_core
    expert_first = my_tensor * experts_local + member * owned
    code_own = lax.dynamic_slice_in_dim(codes, expert_first, owned, 1).astype(jnp.int32)
    gate_own = lax.dynamic_slice_in_dim(gates, expert_first, owned, 1)

    carry, pairs, parts = (), [], []
    for e in range(owned):
        *carry, pair, part = run_expert(
            member.reshape(1).astype(jnp.int32),
            tokens,
            moe_grad,
            code_own[:, e : e + 1],
            gate_own[:, e : e + 1],
            weights[e],
            carry,
        )
        pairs.append(pair)
        parts.append(lax.psum_scatter(part, "z", scatter_dimension=0, tiled=False))
    moe_parts, normed_parts = carry

    pair_grad = jnp.concatenate(pairs, axis=1)
    pair_core = stacked(pair_grad[:2], swap(pair_grad[2:], "core"), core_first)
    pair_y = in_order(pair_core[0], swap(pair_core[1], "y"), y_first)
    pair_y = pair_y.reshape(experts_local, seq_len)
    if tensor_size == 2:
        local = seq_len // 2
        give = lax.dynamic_slice_in_dim(pair_y, (1 - my_tensor) * local, local, 1)
        keep = lax.dynamic_slice_in_dim(pair_y, my_tensor * local, local, 1)
        pair_all = in_order(keep, swap(give, "tensor"), tensor_first)
    else:
        local = seq_len // tensor_size
        pair_all = lax.all_gather(pair_y, "tensor", axis=0, tiled=True)
        pair_all = lax.dynamic_slice_in_dim(pair_all, my_tensor * local, local, 1)
    gates_local = lax.dynamic_slice_in_dim(gates[0], my_tensor * local, local, 1)
    gate_dot = jnp.sum(gates_local * pair_all, axis=0, keepdims=True)
    logit_low = (gates_local * (pair_all - gate_dot)).astype(bf16)

    normed_local = scatter_group(normed_parts, tensor_size)
    normed_local, moe_parts = lax.optimization_barrier((normed_local, moe_parts))
    normed_local = normed_local + contract(logit_low, router_weight, 0, 1)
    router_part = jnp.dot(logit_low, ffn_normed, preferred_element_type=f32)
    state_grad, ffn_gain_part = norm_backward(normed_local, hidden_state, ffn_gain)
    state_grad = state_grad + grad_rows
    steps = (("core", 2), ("y", 2), ("tensor", tensor_size), ("z", z_size))
    attn_grad_all = gather_rows((residual_scale * state_grad).astype(bf16), tensor_size)
    moe_out = scatter_group(moe_parts, tensor_size)
    block_output = (hidden_state + residual_scale * moe_out).astype(bf16)

    def scatter_dp(part):
        part = part.reshape(z_size, 2, 2, shard_rows, part.shape[1])
        part = jnp.take(part, my_core, axis=2), jnp.take(part, 1 - my_core, axis=2)
        part = part[0].astype(f32) + swap(part[1].astype(bf16), "core").astype(f32)
        part = jnp.take(part, my_y, axis=1), jnp.take(part, 1 - my_y, axis=1)
        part = part[0] + swap(part[1].astype(bf16), "y").astype(f32)
        return lax.psum_scatter(part.astype(bf16), "z", scatter_dimension=0, tiled=False)

    out_sum = scatter_dp(contract(attn_grad_all, attn_mixed, 0, 0))
    mixed_grad = jnp.dot(attn_grad_all, out_full, preferred_element_type=f32).astype(bf16)
    qkv_pre_grad = attention_backward(qkv_rot, mixed_grad, log_totals, cosine, sine)
    qkv_pre_grad, block_output = lax.optimization_barrier((qkv_pre_grad, block_output))
    attn_normed_grad = scatter_rows(contract(qkv_pre_grad, qkv_full, 1, 1), tensor_size)
    qkv_sum = scatter_dp(contract(attn_tokens, qkv_pre_grad, 0, 0))
    input_part, attn_gain_part = norm_backward(attn_normed_grad, input_rows, attn_gain)
    input_grad = (state_grad + input_part).astype(bf16)
    small = jnp.concatenate(
        [router_part, ffn_gain_part[None, :], attn_gain_part[None, :]], axis=0
    )
    small = butterfly_sum(small, steps)

    owners = []
    for part in parts:
        near = stacked(part[0::2], swap(part[1::2], "core"), core_first)
        owners.append(in_order(near[0], swap(near[1], "y"), y_first))
    summed = jnp.stack(owners, axis=1).reshape(experts_local, rows, both_width)
    both_rows = gate_weight.shape[1]
    qkv_sum = qkv_sum.reshape(shard_rows, groups, -1)
    return (
        block_output,
        input_grad,
        small[expert_count + 1],
        qkv_sum[:, :, : 2 * HEAD].reshape(query_weight.shape).astype(f32),
        qkv_sum[:, :, 2 * HEAD :].astype(f32),
        out_sum.T.astype(f32),
        small[expert_count],
        small[:expert_count].T,
        summed[:, :both_rows, :hidden].astype(f32),
        summed[:, :both_rows, hidden:].astype(f32),
        summed[:, both_rows:].astype(f32),
    )


def solution(mesh):
    dp, tensor = mesh.shape["dp"], mesh.shape["tensor"]
    fine = Mesh(mesh.devices.reshape(dp // 4, 2, 2, tensor), ("z", "y", "core", "tensor"))
    rows = ("z", "y", "core")
    every = rows + ("tensor",)
    experts = P("tensor", rows, None)
    return jax.shard_map(
        functools.partial(shards, dict(fine.shape)),
        mesh=fine,
        in_specs=(
            P(every, None),
            P(rows),
            P(rows, None),
            P(),
            P(rows, "tensor"),
            P(rows, "tensor", None),
            P("tensor", rows),
            P(),
            P(),
            experts,
            experts,
            experts,
            P(every, None),
        ),
        out_specs=(
            P(every, None),
            P(every, None),
            P(),
            P(rows, "tensor"),
            P(rows, "tensor", None),
            P("tensor", rows),
            P(),
            P(),
            experts,
            experts,
            experts,
        ),
        check_vma=False,
    )
```

time: 778 us -> 786 us (1.010)
  matrix products: 275 us -> 23.9 us
  Pallas kernels: 0 us -> 206 us
  waiting for transfers between devices: 249 us -> 318 us
  starting transfers between devices: 78.2 us -> 48.6 us
  blocking collectives: 0 us -> 20.3 us
    dot_general x25 -> x1, matrix products: 252 us -> 2.55 us  [ein(): return jnp.einsum(spec, *operands, preferred_element_type=f32)]
    pallas_call x0 -> x6, Pallas kernels: none -> 206 us  [the longest x4 162 us: run_expert(): pl.pallas_call(functools.partial(expert_kernel, bool(carry)), grid=(seque...]
    ppermute x37 -> x51, waiting for transfers between devices: 145 us -> 235 us  [swap(): return lax.ppermute(values, axis, [(0, 1), (1, 0)])]
    reduce_scatter x4 -> x6, waiting for transfers between devices: 0.03 us -> 52.4 us  [the longest x4 52.4 us: shards(): parts.append(lax.psum_scatter(part, 'z', scatter_dimension=0, tiled=False))]
    all_to_all x6 -> x0, waiting for transfers between devices: 36.1 us -> none  [the longest x3 28.8 us: to_owner(): return lax.all_to_all(weight, ('y', 'core'), 0, 1, tiled=True)]
    all_to_all x6 -> x0, starting transfers between devices: 34.8 us -> none  [the longest x3 22.5 us: to_owner(): return lax.all_to_all(weight, ('y', 'core'), 0, 1, tiled=True)]
    ppermute x10 -> x5, waiting for transfers between devices: 57.8 us -> 30.8 us  [butterfly_sum(): lax.ppermute(values, axis, [(i, i ^ step) for i in range(size)])]
    all_gather x0 -> x1, blocking collectives: none -> 20.3 us  [shards(): by_z = lax.all_gather(packed, 'z', axis=0, tiled=False)]
  transfers between devices with their start and end apart: 60 -> 66, of which waited for: 24 -> 33; matrix products, arithmetic and copies ran while one was open for 49% -> 19% of each run, Pallas kernels for 0% -> 26%
where the time goes in v2:
time: 786 us; the launch traced here: 780 us
  waiting for transfers between devices  318 us (40%)
  Pallas kernels  206 us (26%)
  other arithmetic  89.1 us (11%)
  local copies, waits for them, and re-layouts  58.4 us (7%)
  starting transfers between devices  48.6 us (6%)
  matrix products  23.9 us (3%)
  blocking collectives  20.3 us (3%)
  between operations  15.9 us (2%)
    ppermute x51, waiting for transfers between devices, swap(): return lax.ppermute(values, axis, [(0, 1), (1, 0)])  235 us
    pallas_call x4, Pallas kernels, run_expert(): pl.pallas_call(functools.partial(expert_kernel, bool(carry)), grid=(seque...  162 us
    reduce_scatter x4, waiting for transfers between devices, shards(): parts.append(lax.psum_scatter(part, 'z', scatter_dimension=0, tiled=False))  52.4 us
    ppermute x51, starting transfers between devices, swap(): return lax.ppermute(values, axis, [(0, 1), (1, 0)])  43.7 us
    ppermute x5, waiting for transfers between devices, butterfly_sum(): lax.ppermute(values, axis, [(i, i ^ step) for i in range(size)])  30.8 us
    pallas_call x1, Pallas kernels, attention_backward(): pl.pallas_call(attention_backward_kernel, grid=(groups,), in_specs=[wide,...  26.7 us
    all_gather x1, blocking collectives, shards(): by_z = lax.all_gather(packed, 'z', axis=0, tiled=False)  20.3 us
    another operation x6, other arithmetic, gather_group(): return jnp.stack([own, across, swap(own, 'core'), swap(across, 'core')])  19.5 us
  transfers between devices with their start and end apart: 66, of which 33 were waited for; matrix products, arithmetic and copies ran while one was open for 19% of the time, Pallas kernels for 26%

profile of v2, /device:TPU:0, one launch (start us, length us, event | category | flops | bytes accessed | tf_op | source)
XLA Modules:
  0.0 780.1 jit_solution(7286063229999318054)
XLA Ops:
  13.9 20.3 %all-gather = bf16[256,1536]{1,0:T(8,128)(2,1)} all-gather(bf16[64,1536]{1,0:T(8,128)(2,1)S(1)} %pad_maximum_fusion.30), channel_id=2, replica_groups=mesh['z'=4,'y'=2,'core'=2,'tensor'=2] {'z'}, dimensions={0}, use_global_device_ids=true | all-gather | bytes 983040 | tf_op jit(solution)/shard_map/all_gather | solution.py:435
  36.4 12.8 %collective-permute-done.20 = bf16[2,4,96,1024]{3,2,1,0:T(8,128)(2,1)} collective-permute-done((bf16[2,4,96,1024]{3,2,1,0:T(8,128)(2,1)}, bf16[2,4,96,1024]{3,2,1,0:T(8,128)(2,1)}, u32[]{:S(2)}, u32[]{:S(2)}) %collective-permute-start.20) | collective-permute-done | bytes 1572896 | tf_op jit(solution)/shard_map/ppermute | solution.py:50
  50.5 14.7 %collective-permute-done.1 = bf16[4,64,1536]{2,1,0:T(8,128)(2,1)} collective-permute-done((bf16[4,64,1536]{2,1,0:T(8,128)(2,1)}, bf16[4,64,1536]{2,1,0:T(8,128)(2,1)}, u32[]{:S(2)}, u32[]{:S(2)}) %collective-permute-start.1) | collective-permute-done | bytes 786464 | tf_op jit(solution)/shard_map/ppermute | solution.py:50
  90.9 21.9 %collective-permute-done.7 = bf16[512,1024]{1,0:T(8,128)(2,1)S(1)} collective-permute-done((bf16[512,1024]{1,0:T(8,128)(2,1)S(1)}, bf16[512,1024]{1,0:T(8,128)(2,1)S(1)}, u32[]{:S(2)}, u32[]{:S(2)}) %collective-permute-start.7) | collective-permute-done | bytes 1048608 | tf_op jit(solution)/shard_map/ppermute | solution.py:50
  121.7 8.0 %collective-permute-done.8 = bf16[256,1024]{1,0:T(8,128)(2,1)} collective-permute-done((bf16[256,1024]{1,0:T(8,128)(2,1)}, bf16[256,1024]{1,0:T(8,128)(2,1)}, u32[]{:S(2)}, u32[]{:S(2)}) %collective-permute-start.8) | collective-permute-done | bytes 524320 | tf_op jit(solution)/shard_map/ppermute | solution.py:50
  141.8 9.0 %collective-permute-done = bf16[512,1024]{1,0:T(8,128)(2,1)} collective-permute-done((bf16[512,1024]{1,0:T(8,128)(2,1)}, bf16[512,1024]{1,0:T(8,128)(2,1)}, u32[]{:S(2)}, u32[]{:S(2)}) %collective-permute-start) | collective-permute-done | bytes 1048608 | tf_op jit(solution)/shard_map/ppermute | solution.py:50
  153.9 4.4 fusion.19.pre_ref
  158.2 17.4 %attention_forward.1 = (bf16[1024,512]{1,0:T(8,128)(2,1)}, bf16[1024,1024]{1,0:T(8,128)(2,1)}, f32[1024,512]{1,0:T(8,128)}) custom-call(f32[1024,1024]{1,0:T(8,128)} %fusion.19.pre_ref, f32[1024,128]{1,0:T(8,128)} %copy.51.cos_ref, f32[1024,128]{1,0:T(8,128)} %copy.52.sin_ref), custom_call_target="tpu_custom_call" | custom-call | flops 3221225472 | bytes 10485760 | tf_op jit(solution)/shard_map/attention_forward/pallas_call | solution.py:236
  175.7 6.8 pad_maximum_fusion.grad_ref
  191.3 19.9 %collective-permute-done.12 = bf16[512,1024]{1,0:T(8,128)(2,1)S(1)} collective-permute-done((bf16[512,1024]{1,0:T(8,128)(2,1)S(1)}, bf16[512,1024]{1,0:T(8,128)(2,1)S(1)}, u32[]{:S(2)}, u32[]{:S(2)}) %collective-permute-start.12) | collective-permute-done | bytes 1048608 | tf_op jit(solution)/shard_map/ppermute | solution.py:50
  216.9 19.9 %collective-permute-done.14 = bf16[512,1024]{1,0:T(8,128)(2,1)S(1)} collective-permute-done((bf16[512,1024]{1,0:T(8,128)(2,1)S(1)}, bf16[512,1024]{1,0:T(8,128)(2,1)S(1)}, u32[]{:S(2)}, u32[]{:S(2)}) %collective-permute-start.14) | collective-permute-done | bytes 1048608 | tf_op jit(solution)/shard_map/ppermute | solution.py:50
  243.2 6.2 collective-permute-done.15
  266.8 39.8 %expert.4 = (bf16[4,1024,1024]{2,1,0:T(8,128)(2,1)}, bf16[4,1024,1024]{2,1,0:T(8,128)(2,1)}, f32[4,1,1024]{2,1,0:T(1,128)}, bf16[4,4,96,1024]{3,2,1,0:T(8,128)(2,1)}) custom-call(s32[1]{0:T(128)} %bitcast.28.member_ref, bf16[4,1024,1024]{2,1,0:T(8,128)(2,1)} %copy-done.5, bf16[4,1024,1024]{2,1,0:T(8,128)(2,1)} %pad_maximum_fusion.grad_ref, ...), custom_call_target="tpu_custom_call" | custom-call | flops 22817013760 | bytes 56623104 | tf_op jit(solution)/shard_map/expert/pallas_call | solution.py:359
  306.9 40.6 %expert.5 = (bf16[4,1024,1024]{2,1,0:T(8,128)(2,1)}, bf16[4,1024,1024]{2,1,0:T(8,128)(2,1)}, f32[4,1,1024]{2,1,0:T(1,128)}, bf16[4,4,96,1024]{3,2,1,0:T(8,128)(2,1)}) custom-call(s32[1]{0:T(128)} %bitcast.28.member_ref, bf16[4,1024,1024]{2,1,0:T(8,128)(2,1)} %copy-done.5, bf16[4,1024,1024]{2,1,0:T(8,128)(2,1)} %pad_maximum_fusion.grad_ref, ...), custom_call_target="tpu_custom_call" | custom-call | flops 22817013760 | bytes 56623104 | tf_op jit(solution)/shard_map/expert/pallas_call | solution.py:359
  347.9 40.7 %expert.6 = (bf16[4,1024,1024]{2,1,0:T(8,128)(2,1)}, bf16[4,1024,1024]{2,1,0:T(8,128)(2,1)}, f32[4,1,1024]{2,1,0:T(1,128)}, bf16[4,4,96,1024]{3,2,1,0:T(8,128)(2,1)}) custom-call(s32[1]{0:T(128)} %bitcast.28.member_ref, bf16[4,1024,1024]{2,1,0:T(8,128)(2,1)} %copy-done.5, bf16[4,1024,1024]{2,1,0:T(8,128)(2,1)} %pad_maximum_fusion.grad_ref, ...), custom_call_target="tpu_custom_call" | custom-call | flops 22817013760 | bytes 56623104 | tf_op jit(solution)/shard_map/expert/pallas_call | solution.py:359
  389.1 40.6 %expert.7 = (bf16[4,1024,1024]{2,1,0:T(8,128)(2,1)}, bf16[4,1024,1024]{2,1,0:T(8,128)(2,1)}, f32[4,1,1024]{2,1,0:T(1,128)}, bf16[4,4,96,1024]{3,2,1,0:T(8,128)(2,1)}) custom-call(s32[1]{0:T(128)} %bitcast.28.member_ref, bf16[4,1024,1024]{2,1,0:T(8,128)(2,1)} %copy-done.5, bf16[4,1024,1024]{2,1,0:T(8,128)(2,1)} %pad_maximum_fusion.grad_ref, ...), custom_call_target="tpu_custom_call" | custom-call | flops 22817013760 | bytes 56623104 | tf_op jit(solution)/shard_map/expert/pallas_call | solution.py:359
  451.7 8.2 %collective-permute-done.24 = bf16[256,1024]{1,0:T(8,128)(2,1)S(1)} collective-permute-done((bf16[256,1024]{1,0:T(8,128)(2,1)S(1)}, bf16[256,1024]{1,0:T(8,128)(2,1)S(1)}, u32[]{:S(2)}, u32[]{:S(2)}) %collective-permute-start.24) | collective-permute-done | bytes 524320 | tf_op jit(solution)/shard_map/ppermute | solution.py:50
  466.1 19.6 %collective-permute-done.25 = bf16[512,1024]{1,0:T(8,128)(2,1)S(1)} collective-permute-done((bf16[512,1024]{1,0:T(8,128)(2,1)S(1)}, bf16[512,1024]{1,0:T(8,128)(2,1)S(1)}, u32[]{:S(2)}, u32[]{:S(2)}) %collective-permute-start.25) | collective-permute-done | bytes 1048608 | tf_op jit(solution)/shard_map/ppermute | solution.py:50
  489.6 4.8 slice_bitcast_fusion.1
  495.1 6.8 collective-permute-done.28
  510.4 5.5 convert_add_fusion.1
  526.8 52.3 %reduce-scatter.17.cloned.1.call-done = bf16[1,4,96,1024]{3,2,1,0:T(8,128)(2,1)} async-done(((bf16[4,4,96,1024]{3,2,1,0:T(8,128)(2,1)}), bf16[1,4,96,1024]{3,2,1,0:T(8,128)(2,1)}) %reduce-scatter.17.cloned.1.call-update) | async-done | bytes 786448 | tf_op jit(solution)/shard_map/reduce_scatter | solution.py:518
  593.0 26.6 %collective-permute-done.49 = bf16[2,96,1024]{2,1,0:T(8,128)(2,1)S(1)} collective-permute-done((bf16[2,96,1024]{2,1,0:T(8,128)(2,1)S(1)}, bf16[2,96,1024]{2,1,0:T(8,128)(2,1)S(1)}, u32[]{:S(2)}, u32[]{:S(2)}) %collective-permute-start.49) | collective-permute-done | bytes 393248 | tf_op jit(solution)/shard_map/ppermute | solution.py:50
  621.0 7.0 collective-permute-done.51
  636.4 7.7 collective-permute-done.55
  647.2 9.0 %collective-permute-done.31 = bf16[512,1024]{1,0:T(8,128)(2,1)S(1)} collective-permute-done((bf16[512,1024]{1,0:T(8,128)(2,1)S(1)}, bf16[512,1024]{1,0:T(8,128)(2,1)S(1)}, u32[]{:S(2)}, u32[]{:S(2)}) %collective-permute-start.31) | collective-permute-done | bytes 1048608 | tf_op jit(solution)/shard_map/ppermute | solution.py:50
  662.8 26.7 %attention_backward.1 = bf16[1024,1024]{1,0:T(8,128)(2,1)} custom-call(bf16[1024,1024]{1,0:T(8,128)(2,1)} %get-tuple-element.44.rot_ref, bf16[1024,512]{1,0:T(8,128)(2,1)} %convolution_convert_fusion.grad_ref, f32[1024,512]{1,0:T(8,128)} %get-tuple-element.63.lse_ref, f32[1024,128]{1,0:T(8,128)} %copy.51.cos_ref, f32[1024,128]{1,0:T(8,128)} %copy.52.sin_ref), custom_call_target="tpu_custom_call" | custom-call | flops 8589934592 | bytes 10485760 | tf_op jit(solution)/shard_map/attention_backward/pallas_call | solution.py:260
  707.7 4.6 collective-permute-done.47
  713.2 7.3 collective-permute-done.38
  730.2 12.9 %collective-permute-done.40 = f32[34,1024]{1,0:T(8,128)S(1)} collective-permute-done((f32[34,1024]{1,0:T(8,128)S(1)}, f32[34,1024]{1,0:T(8,128)S(1)}, u32[]{:S(2)}, u32[]{:S(2)}) %collective-permute-start.40) | collective-permute-done | bytes 139296 | tf_op jit(solution)/shard_map/ppermute | solution.py:57
  753.6 6.4 collective-permute-done.42
  762.0 7.3 collective-permute-done.43
  (405 shorter events, 228.6 us)
Async XLA Ops:
  7.2 259.6 %all-gather.16.cloned.1.call-start = ((), (), s32[]{:S(2)}) async-start(), calls=%async_computation.15 | async-start | bytes 3932160 | tf_op jit(solution)/shard_map/all_gather | solution.py:450
  10.7 38.6 %collective-permute-start.20 = (bf16[2,4,96,1024]{3,2,1,0:T(8,128)(2,1)}, bf16[2,4,96,1024]{3,2,1,0:T(8,128)(2,1)}, u32[]{:S(2)}, u32[]{:S(2)}) collective-permute-start(bf16[2,4,96,1024]{3,2,1,0:T(8,128)(2,1)} %dynamic-slice_bitcast_fusion), channel_id=1, source_target_pairs={{0,4},{4,0},{1,5},{5,1},{2,6},{6,2},{3,7},{7,3},{8,12},{12,8},{9,1... | collective-permute-start | bytes 4718600 | tf_op jit(solution)/shard_map/ppermute | solution.py:50
  34.1 31.1 %collective-permute-start.1 = (bf16[4,64,1536]{2,1,0:T(8,128)(2,1)}, bf16[4,64,1536]{2,1,0:T(8,128)(2,1)}, u32[]{:S(2)}, u32[]{:S(2)}) collective-permute-start(bf16[4,64,1536]{2,1,0:T(8,128)(2,1)} %bitcast.1), channel_id=1, source_target_pairs={{0,4},{4,0},{1,5},{5,1},{2,6},{6,2},{3,7},{7,3},{8,12},{12,8},{9,1... | collective-permute-start | bytes 2359304 | tf_op jit(solution)/shard_map/ppermute | solution.py:50
  35.6 32.5 %collective-permute-start.19 = (bf16[4,96,1024]{2,1,0:T(8,128)(2,1)}, bf16[4,96,1024]{2,1,0:T(8,128)(2,1)}, u32[]{:S(2)}, u32[]{:S(2)}) collective-permute-start(bf16[4,96,1024]{2,1,0:T(8,128)(2,1)} %dynamic-slice_bitcast_fusion.2), channel_id=1, source_target_pairs={{0,2},{2,0},{1,3},{3,1},{4,6},{6,4},{5,7},{7,5},{8,10},{10,8},{9,1... | collective-permute-start | bytes 2359304 | tf_op jit(solution)/shard_map/ppermute | solution.py:50
  74.0 232.9 %all-gather.14.cloned.1.call-start = ((), (), s32[]{:S(2)}) async-start(), calls=%async_computation.14 | async-start | bytes 3932160 | tf_op jit(solution)/shard_map/all_gather | solution.py:450
  87.3 25.4 %collective-permute-start.7 = (bf16[512,1024]{1,0:T(8,128)(2,1)S(1)}, bf16[512,1024]{1,0:T(8,128)(2,1)S(1)}, u32[]{:S(2)}, u32[]{:S(2)}) collective-permute-start(bf16[512,1024]{1,0:T(8,128)(2,1)S(1)} %copy-done.19), channel_id=1, source_target_pairs={{0,4},{4,0},{1,5},{5,1},{2,6},{6,2},{3,7},{7,3},{8,12},{12,8},{9,1... | collective-permute-start | bytes 3145736 | tf_op jit(solution)/shard_map/ppermute | solution.py:50
  89.1 28.8 %collective-permute-start.6 = (bf16[512,1024]{1,0:T(8,128)(2,1)S(1)}, bf16[512,1024]{1,0:T(8,128)(2,1)S(1)}, u32[]{:S(2)}, u32[]{:S(2)}) collective-permute-start(bf16[512,1024]{1,0:T(8,128)(2,1)S(1)} %copy-done.19), channel_id=1, source_target_pairs={{0,1},{1,0},{2,3},{3,2},{4,5},{5,4},{6,7},{7,6},{8,9},{9,8},{10,11... | collective-permute-start | bytes 3145736 | tf_op jit(solution)/shard_map/ppermute | solution.py:50
  117.5 33.2 %collective-permute-start = (bf16[512,1024]{1,0:T(8,128)(2,1)}, bf16[512,1024]{1,0:T(8,128)(2,1)}, u32[]{:S(2)}, u32[]{:S(2)}) collective-permute-start(bf16[512,1024]{1,0:T(8,128)(2,1)} %fusion.7), channel_id=1, source_target_pairs={{0,1},{1,0},{2,3},{3,2},{4,5},{5,4},{6,7},{7,6},{8,9},{9,8},{10,11... | collective-permute-start | bytes 3145736 | tf_op jit(solution)/shard_map/ppermute | solution.py:50
  121.7 54.0 %collective-permute-start.10 = (bf16[1024,1024]{1,0:T(8,128)(2,1)}, bf16[1024,1024]{1,0:T(8,128)(2,1)}, u32[]{:S(2)}, u32[]{:S(2)}) collective-permute-start(bf16[1024,1024]{1,0:T(8,128)(2,1)} %get-tuple-element.151), channel_id=1, source_target_pairs={{0,2},{2,0},{1,3},{3,1},{4,6},{6,4},{5,7},{7,5},{8,10},{10,8},{9,1... | collective-permute-start | bytes 6291464 | tf_op jit(solution)/shard_map/ppermute | solution.py:50
  133.7 42.0 %collective-permute-start.11 = (bf16[1024,1024]{1,0:T(8,128)(2,1)}, bf16[1024,1024]{1,0:T(8,128)(2,1)}, u32[]{:S(2)}, u32[]{:S(2)}) collective-permute-start(bf16[1024,1024]{1,0:T(8,128)(2,1)} %get-tuple-element.153), channel_id=1, source_target_pairs={{0,2},{2,0},{1,3},{3,1},{4,6},{6,4},{5,7},{7,5},{8,10},{10,8},{9,1... | collective-permute-start | bytes 6291464 | tf_op jit(solution)/shard_map/ppermute | solution.py:50
  134.7 213.1 %all-gather.12.cloned.1.call-start = ((), (), s32[]{:S(2)}) async-start(), calls=%async_computation.13 | async-start | bytes 3932160 | tf_op jit(solution)/shard_map/all_gather | solution.py:450
  191.2 197.9 %all-gather.10.cloned.1.call-start = ((), (), s32[]{:S(2)}) async-start(), calls=%async_computation.12 | async-start | bytes 3932160 | tf_op jit(solution)/shard_map/all_gather | solution.py:450
  253.3 267.6 %reduce-scatter.11.cloned.1.call-start = ((), (), s32[]{:S(2)}) async-start(), calls=%async_computation.8 | async-start | bytes 3932160 | tf_op jit(solution)/shard_map/reduce_scatter | solution.py:518
  306.6 216.1 %reduce-scatter.13.cloned.1.call-start = ((), (), s32[]{:S(2)}) async-start(), calls=%async_computation.9 | async-start | bytes 3932160 | tf_op jit(solution)/shard_map/reduce_scatter | solution.py:518
  347.6 177.4 %reduce-scatter.15.cloned.1.call-start = ((), (), s32[]{:S(2)}) async-start(), calls=%async_computation.10 | async-start | bytes 3932160 | tf_op jit(solution)/shard_map/reduce_scatter | solution.py:518
  388.6 190.6 %reduce-scatter.17.cloned.1.call-start = ((), (), s32[]{:S(2)}) async-start(), calls=%async_computation.11 | async-start | bytes 3932160 | tf_op jit(solution)/shard_map/reduce_scatter | solution.py:518
  447.3 313.2 %reduce-scatter.9.cloned.1.call-start = ((), (), s32[]{:S(2)}) async-start(), calls=%async_computation.7 | async-start | bytes 327680 | tf_op jit(solution)/shard_map/reduce_scatter | solution.py:555
  464.5 24.5 %collective-permute-start.27 = (bf16[512,1024]{1,0:T(8,128)(2,1)S(1)}, bf16[512,1024]{1,0:T(8,128)(2,1)S(1)}, u32[]{:S(2)}, u32[]{:S(2)}) collective-permute-start(bf16[512,1024]{1,0:T(8,128)(2,1)S(1)} %pad_maximum_fusion.17), channel_id=1, source_target_pairs={{0,4},{4,0},{1,5},{5,1},{2,6},{6,2},{3,7},{7,3},{8,12},{12,8},{9,1... | collective-permute-start | bytes 3145736 | tf_op jit(solution)/shard_map/ppermute | solution.py:50
  517.3 62.8 %collective-permute-start.34 = (bf16[256,1024]{1,0:T(8,128)(2,1)}, bf16[256,1024]{1,0:T(8,128)(2,1)}, u32[]{:S(2)}, u32[]{:S(2)}) collective-permute-start(bf16[256,1024]{1,0:T(8,128)(2,1)} %get-tuple-element.182), channel_id=1, source_target_pairs={{0,4},{4,0},{1,5},{5,1},{2,6},{6,2},{3,7},{7,3},{8,12},{12,8},{9,1... | collective-permute-start | bytes 1572872 | tf_op jit(solution)/shard_map/ppermute | solution.py:50
  520.5 61.4 %collective-permute-start.36 = (bf16[256,1024]{1,0:T(8,128)(2,1)}, bf16[256,1024]{1,0:T(8,128)(2,1)}, u32[]{:S(2)}, u32[]{:S(2)}) collective-permute-start(bf16[256,1024]{1,0:T(8,128)(2,1)} %get-tuple-element.183), channel_id=1, source_target_pairs={{0,1},{1,0},{2,3},{3,2},{4,5},{5,4},{6,7},{7,6},{8,9},{9,8},{10,11... | collective-permute-start | bytes 1572872 | tf_op jit(solution)/shard_map/ppermute | solution.py:50
  522.7 62.3 %collective-permute-start.48 = (bf16[2,96,1024]{2,1,0:T(8,128)(2,1)}, bf16[2,96,1024]{2,1,0:T(8,128)(2,1)}, u32[]{:S(2)}, u32[]{:S(2)}) collective-permute-start(bf16[2,96,1024]{2,1,0:T(8,128)(2,1)} %slice.366), channel_id=1, source_target_pairs={{0,2},{2,0},{1,3},{3,1},{4,6},{6,4},{5,7},{7,5},{8,10},{10,8},{9,1... | collective-permute-start | bytes 1179656 | tf_op jit(solution)/shard_map/ppermute | solution.py:50
  524.5 63.2 %collective-permute-start.50 = (bf16[2,96,1024]{2,1,0:T(8,128)(2,1)}, bf16[2,96,1024]{2,1,0:T(8,128)(2,1)}, u32[]{:S(2)}, u32[]{:S(2)}) collective-permute-start(bf16[2,96,1024]{2,1,0:T(8,128)(2,1)} %slice.370), channel_id=1, source_target_pairs={{0,2},{2,0},{1,3},{3,1},{4,6},{6,4},{5,7},{7,5},{8,10},{10,8},{9,1... | collective-permute-start | bytes 1179656 | tf_op jit(solution)/shard_map/ppermute | solution.py:50
  526.8 62.7 %collective-permute-start.52 = (bf16[2,96,1024]{2,1,0:T(8,128)(2,1)}, bf16[2,96,1024]{2,1,0:T(8,128)(2,1)}, u32[]{:S(2)}, u32[]{:S(2)}) collective-permute-start(bf16[2,96,1024]{2,1,0:T(8,128)(2,1)} %slice.374), channel_id=1, source_target_pairs={{0,2},{2,0},{1,3},{3,1},{4,6},{6,4},{5,7},{7,5},{8,10},{10,8},{9,1... | collective-permute-start | bytes 1179656 | tf_op jit(solution)/shard_map/ppermute | solution.py:50
  581.9 46.2 %collective-permute-start.35 = (bf16[512,1024]{1,0:T(8,128)(2,1)S(1)}, bf16[512,1024]{1,0:T(8,128)(2,1)S(1)}, u32[]{:S(2)}, u32[]{:S(2)}) collective-permute-start(bf16[512,1024]{1,0:T(8,128)(2,1)S(1)} %pad_maximum_fusion.18), channel_id=1, source_target_pairs={{0,1},{1,0},{2,3},{3,2},{4,5},{5,4},{6,7},{7,6},{8,9},{9,8},{10,11... | collective-permute-start | bytes 3145736 | tf_op jit(solution)/shard_map/ppermute | solution.py:50
  585.0 43.1 %collective-permute-start.37 = (bf16[512,1024]{1,0:T(8,128)(2,1)S(1)}, bf16[512,1024]{1,0:T(8,128)(2,1)S(1)}, u32[]{:S(2)}, u32[]{:S(2)}) collective-permute-start(bf16[512,1024]{1,0:T(8,128)(2,1)S(1)} %pad_maximum_fusion.19), channel_id=1, source_target_pairs={{0,4},{4,0},{1,5},{5,1},{2,6},{6,2},{3,7},{7,3},{8,12},{12,8},{9,1... | collective-permute-start | bytes 3145736 | tf_op jit(solution)/shard_map/ppermute | solution.py:50
  587.7 31.9 %collective-permute-start.49 = (bf16[2,96,1024]{2,1,0:T(8,128)(2,1)S(1)}, bf16[2,96,1024]{2,1,0:T(8,128)(2,1)S(1)}, u32[]{:S(2)}, u32[]{:S(2)}) collective-permute-start(bf16[2,96,1024]{2,1,0:T(8,128)(2,1)S(1)} %fusion.51), channel_id=1, source_target_pairs={{0,4},{4,0},{1,5},{5,1},{2,6},{6,2},{3,7},{7,3},{8,12},{12,8},{9,1... | collective-permute-start | bytes 1179656 | tf_op jit(solution)/shard_map/ppermute | solution.py:50
  589.4 38.5 %collective-permute-start.51 = (bf16[2,96,1024]{2,1,0:T(8,128)(2,1)S(1)}, bf16[2,96,1024]{2,1,0:T(8,128)(2,1)S(1)}, u32[]{:S(2)}, u32[]{:S(2)}) collective-permute-start(bf16[2,96,1024]{2,1,0:T(8,128)(2,1)S(1)} %fusion.50), channel_id=1, source_target_pairs={{0,4},{4,0},{1,5},{5,1},{2,6},{6,2},{3,7},{7,3},{8,12},{12,8},{9,1... | collective-permute-start | bytes 1179656 | tf_op jit(solution)/shard_map/ppermute | solution.py:50
  592.2 44.2 %collective-permute-start.53 = (bf16[2,96,1024]{2,1,0:T(8,128)(2,1)S(1)}, bf16[2,96,1024]{2,1,0:T(8,128)(2,1)S(1)}, u32[]{:S(2)}, u32[]{:S(2)}) collective-permute-start(bf16[2,96,1024]{2,1,0:T(8,128)(2,1)S(1)} %fusion.49), channel_id=1, source_target_pairs={{0,4},{4,0},{1,5},{5,1},{2,6},{6,2},{3,7},{7,3},{8,12},{12,8},{9,1... | collective-permute-start | bytes 1179656 | tf_op jit(solution)/shard_map/ppermute | solution.py:50
  619.6 24.5 %collective-permute-start.55 = (bf16[2,96,1024]{2,1,0:T(8,128)(2,1)S(1)}, bf16[2,96,1024]{2,1,0:T(8,128)(2,1)S(1)}, u32[]{:S(2)}, u32[]{:S(2)}) collective-permute-start(bf16[2,96,1024]{2,1,0:T(8,128)(2,1)S(1)} %fusion.48), channel_id=1, source_target_pairs={{0,4},{4,0},{1,5},{5,1},{2,6},{6,2},{3,7},{7,3},{8,12},{12,8},{9,1... | collective-permute-start | bytes 1179656 | tf_op jit(solution)/shard_map/ppermute | solution.py:50
  662.8 37.2 %collective-permute-start.46 = (bf16[4,2,64,512]{3,2,0,1:T(8,128)(2,1)}, bf16[4,2,64,512]{3,2,0,1:T(8,128)(2,1)}, u32[]{:S(2)}, u32[]{:S(2)}) collective-permute-start(bf16[4,2,64,512]{3,2,0,1:T(8,128)(2,1)} %fusion.32), channel_id=1, source_target_pairs={{0,2},{2,0},{1,3},{3,1},{4,6},{6,4},{5,7},{7,5},{8,10},{10,8},{9,1... | collective-permute-start | bytes 1572872 | tf_op jit(solution)/shard_map/ppermute | solution.py:50
  694.8 25.8 %collective-permute-start.38 = (bf16[512,1024]{1,0:T(8,128)(2,1)}, bf16[512,1024]{1,0:T(8,128)(2,1)S(1)}, u32[]{:S(2)}, u32[]{:S(2)}) collective-permute-start(bf16[512,1024]{1,0:T(8,128)(2,1)} %dynamic-slice_convert_fusion), channel_id=1, source_target_pairs={{0,1},{1,0},{2,3},{3,2},{4,5},{5,4},{6,7},{7,6},{8,9},{9,8},{10,11... | collective-permute-start | bytes 3145736 | tf_op jit(solution)/shard_map/ppermute | solution.py:50
  713.2 57.5 %reduce-scatter.7.cloned.1.call-start = ((), (), s32[]{:S(2)}) async-start(), calls=%async_computation.6 | async-start | bytes 655360 | tf_op jit(solution)/shard_map/reduce_scatter | solution.py:555
  (100 other events, 1284.8 us)
Sparse Core Ops, SparseCore 0:
  74.1 65.0 all-gather.15
  140.8 62.0 all-gather.13
  204.5 62.0 all-gather.11
  268.0 62.0 all-gather.9
  332.3 59.0 reduce-scatter.10
  393.5 60.3 reduce-scatter.12
  456.2 60.3 reduce-scatter.14
  518.8 60.3 reduce-scatter.16
  713.3 18.9 reduce-scatter.8
  744.9 23.8 reduce-scatter.6

commit v3 on v2

--- a/solution.py
+++ b/solution.py
@@ -46,6 +46,14 @@
     return (source_grad, gain_grad)
 
 
+def together(*values):
+    return lax.optimization_barrier(values)
+
+
+def after(values, *earlier):
+    return lax.optimization_barrier((values,) + earlier)[0]
+
+
 def swap(values, axis):
     return lax.ppermute(values, axis, [(0, 1), (1, 0)])
 
@@ -83,25 +91,31 @@
     return keep.astype(f32) + swap(give, "tensor").astype(f32)
 
 
-def gather_group(rows, tensor_size):
+def gather_group(rows, tensor_size, earlier):
     if tensor_size != 2:
         own = gather_rows(rows, tensor_size)
         across = swap(own, "y")
     else:
         first = lax.axis_index("tensor") == 0
         half = rows.shape[0] // 2
-        by_tensor, by_y = swap(rows, "tensor"), swap(rows, "y")
-        corner = jnp.concatenate(
-            [swap(by_y[:half], "tensor"), swap(by_tensor[half:], "y")], axis=0
+        by_tensor, by_y, _ = together(swap(rows, "tensor"), swap(rows, "y"), earlier)
+        own = in_order(rows, by_tensor, first)
+        low, high, own_core = together(
+            swap(by_y[:half], "tensor"), swap(by_tensor[half:], "y"), swap(own, "core")
         )
-        own = in_order(rows, by_tensor, first)
+        corner = jnp.concatenate([low, high], axis=0)
         across = in_order(by_y, corner, first)
+        return jnp.stack([own, across, own_core, swap(across, "core")])
     return jnp.stack([own, across, swap(own, "core"), swap(across, "core")])
 
 
-def scatter_group(parts, tensor_size):
-    pair = [parts[i].astype(f32) + swap(parts[i + 2].astype(bf16), "core").astype(f32) for i in (0, 1)]
-    own, across = pair
+def add_core(parts):
+    given = swap(parts[2:], "core")
+    return (parts[:2].astype(f32) + given.astype(f32)).astype(bf16)
+
+
+def scatter_group(pair, tensor_size):
+    own, across = pair[0].astype(f32), pair[1].astype(f32)
     if tensor_size != 2:
         own = own + swap(across.astype(bf16), "y").astype(f32)
         return scatter_rows(own, tensor_size)
@@ -114,14 +128,13 @@
 
     mine, by_tensor = take(own, me), take(own, 1 - me)
     by_y, corner = take(across, me), take(across, 1 - me).astype(bf16)
-    low, high = swap(corner[:half], "tensor"), swap(corner[half:], "y")
+    low, high = together(swap(corner[:half], "tensor"), swap(corner[half:], "y"))
     by_y = jnp.concatenate([by_y[:half] + low.astype(f32), by_y[half:]], axis=0)
     by_tensor = jnp.concatenate([by_tensor[:half], by_tensor[half:] + high.astype(f32)], axis=0)
-    return (
-        mine
-        + swap(by_tensor.astype(bf16), "tensor").astype(f32)
-        + swap(by_y.astype(bf16), "y").astype(f32)
-    )
+    from_tensor, from_y = together(
+        swap(by_tensor.astype(bf16), "tensor"), swap(by_y.astype(bf16), "y")
+    )
+    return mine + from_tensor.astype(f32) + from_y.astype(f32)
 
 
 def rope_lanes(values, cosine, sine, first, direction):
@@ -273,12 +286,16 @@
     )(rot, grad, lse, cosine, sine)
 
 
-def expert_kernel(carried, member_ref, tokens_ref, grad_ref, code_ref, gate_ref, weight_ref, *refs):
+def expert_kernel(
+    carried, shared, member_ref, tokens_ref, grad_ref, code_ref, gate_ref, weight_ref, *refs
+):
     if carried:
         moe_in, normed_in, *refs = refs
+    if shared:
+        refs = refs[1:]
     moe_ref, normed_ref, pair_ref, part_ref, both, down, both_acc, down_acc = refs
     step = pl.program_id(0)
-    shards_z, members, rows = weight_ref.shape[:3]
+    shards_z, members, rows = weight_ref.shape[0], weight_ref.shape[2], weight_ref.shape[3]
     hidden = down.shape[0]
     both_rows = both.shape[0] // (shards_z * members)
     down_rows = hidden // (shards_z * members)
@@ -297,8 +314,8 @@
     @pl.when(step == 0)
     def _():
         for z, rel, both_at, down_at in places():
-            both[both_at, :] = weight_ref[z, rel, :both_rows, :]
-            down[down_at, :] = weight_ref[z, rel, both_rows:, :]
+            both[both_at, :] = weight_ref[z, 0, rel, :both_rows, :]
+            down[down_at, :] = weight_ref[z, 0, rel, both_rows:, :]
         both_acc[...] = jnp.zeros_like(both_acc)
         down_acc[...] = jnp.zeros_like(down_acc)
 
@@ -343,21 +360,22 @@
     @pl.when(step == pl.num_programs(0) - 1)
     def _():
         for z, rel, both_at, down_at in places():
-            part_ref[z, rel, :both_rows, :] = both_acc[both_at, :].astype(bf16)
-            part_ref[z, rel, both_rows:, :] = down_acc[down_at, :].astype(bf16)
-
-
-def run_expert(member, tokens, grads, code, gate, weight, carry):
+            part_ref[z, 0, rel, :both_rows, :] = both_acc[both_at, :].astype(bf16)
+            part_ref[z, 0, rel, both_rows:, :] = down_acc[down_at, :].astype(bf16)
+
+
+def run_expert(member, tokens, grads, code, gate, weight, place, carry, shared):
     sequences, seq_len, width = tokens.shape
-    shards_z, members, rows, both_width = weight.shape
+    shards_z, bunch, members, rows, both_width = weight.shape
     hidden = both_width // 2
     per_seq = pl.BlockSpec((1, seq_len, width), lambda s: (s, 0, 0))
     per_row = pl.BlockSpec((1, 1, seq_len), lambda s: (s, 0, 0))
-    every = pl.BlockSpec(weight.shape, lambda s: (0, 0, 0, 0), pipeline_mode=pl.Buffered(1))
-    part = pl.BlockSpec(weight.shape, lambda s: (0, 0, 0, 0))
+    one = (shards_z, 1, members, rows, both_width)
+    every = pl.BlockSpec(one, lambda s: (0, place, 0, 0, 0), pipeline_mode=pl.Buffered(1))
+    part = pl.BlockSpec(one, lambda s: (0, place, 0, 0, 0))
     slots = sequences * CAP
     return pl.pallas_call(
-        functools.partial(expert_kernel, bool(carry)),
+        functools.partial(expert_kernel, bool(carry), bool(shared)),
         grid=(sequences,),
         in_specs=[
             pl.BlockSpec(memory_space=pltpu.SMEM),
@@ -367,7 +385,8 @@
             per_row,
             every,
         ]
-        + [per_seq] * len(carry),
+        + [per_seq] * len(carry)
+        + [pl.BlockSpec(memory_space=pl.ANY)] * len(shared),
         out_specs=[per_seq, per_seq, per_row, part],
         out_shape=[
             jax.ShapeDtypeStruct(tokens.shape, bf16),
@@ -384,11 +403,12 @@
         compiler_params=pltpu.CompilerParams(vmem_limit_bytes=66_000_000),
         cost_estimate=pl.CostEstimate(
             flops=2 * slots * width * (4 * seq_len + 9 * hidden),
-            bytes_accessed=12 * sequences * seq_len * width + 4 * weight.size,
+            bytes_accessed=12 * sequences * seq_len * width + 4 * (weight.size // bunch),
             transcendentals=slots * hidden,
         ),
         name="expert",
-    )(member, tokens, grads, code, gate, weight, *carry)
+        input_output_aliases={6 + len(carry): 3} if shared else {},
+    )(member, tokens, grads, code, gate, weight, *carry, *shared)
 
 
 def shards(
@@ -417,12 +437,16 @@
     experts_local = gate_weight.shape[0]
     owned = experts_local // 4
     hidden = gate_weight.shape[2]
-    my_y, my_core = lax.axis_index("y"), lax.axis_index("core")
+    my_z, my_y, my_core = lax.axis_index("z"), lax.axis_index("y"), lax.axis_index("core")
     my_tensor = lax.axis_index("tensor")
     y_first, core_first, tensor_first = my_y == 0, my_core == 0, my_tensor == 0
 
     def at(values, index):
         return lax.dynamic_index_in_dim(values, index, 0, keepdims=False)
+
+    def stacked(mine, theirs, is_first, axis=1):
+        ordered = [jnp.where(is_first, mine, theirs), jnp.where(is_first, theirs, mine)]
+        return jnp.stack(ordered, axis)
 
     packed = jnp.concatenate(
         [
@@ -432,34 +456,43 @@
         ],
         axis=1,
     )
-    by_z = lax.all_gather(packed, "z", axis=0, tiled=False)
+    packed_full = lax.all_gather(packed, ("z", "y", "core"), axis=0, tiled=True)
+
+    input_rows = block_input.astype(f32)
+    attn_normed = (input_rows * row_scale(input_rows) * attn_gain).astype(bf16)
+    attn_tokens = gather_rows(attn_normed, tensor_size)
+    grad_rows = out_grad.astype(f32)
+    moe_rows = after((residual_scale * grad_rows).astype(bf16), attn_tokens)
 
     experts = jnp.concatenate(
         [jnp.concatenate([gate_weight, up_weight], axis=2), down_weight], axis=1
     )
     rows, both_width = experts.shape[1:]
     grouped = experts.reshape(2, 2, owned, rows, both_width)
-    own_y, from_y = at(grouped, my_y), swap(at(grouped, 1 - my_y), "y")
-    pieces = [
-        at(own_y, my_core),
-        swap(at(own_y, 1 - my_core), "core"),
-        at(from_y, my_core),
-        swap(at(from_y, 1 - my_core), "core"),
-    ]
-    weights = [
-        lax.all_gather(jnp.stack([piece[e] for piece in pieces]), "z", axis=0, tiled=False)
-        for e in range(owned)
-    ]
-
-    def stacked(mine, theirs, is_first):
-        return jnp.stack([jnp.where(is_first, mine, theirs), jnp.where(is_first, theirs, mine)], 1)
-
-    by_y = stacked(by_z, swap(by_z, "y"), y_first)
-    other = swap(by_y, "core")
-    packed_full = jnp.stack(
-        [jnp.where(core_first, by_y, other), jnp.where(core_first, other, by_y)], 2
-    ).reshape(width, -1)
+    own_y, give_y = at(grouped, my_y), at(grouped, 1 - my_y)
+    from_y = swap(give_y, "y")
+    members = jnp.stack(
+        [
+            at(own_y, my_core),
+            swap(at(own_y, 1 - my_core), "core"),
+            at(from_y, my_core),
+            swap(at(from_y, 1 - my_core), "core"),
+        ],
+        axis=1,
+    )
+    moe_own = gather_rows(moe_rows, tensor_size)
+    packed_full, attn_tokens, moe_own, members = together(
+        packed_full, attn_tokens, moe_own, members
+    )
     qkv_full, out_full = packed_full[:, :wide], packed_full[:, wide:]
+    bunch = min(2, owned)
+    weights = []
+    for e in range(0, owned, bunch):
+        item = members[e : e + bunch]
+        if weights:
+            item = after(item, launched)
+        launched = item
+        weights.append(lax.all_gather(item, "z", axis=0, tiled=False))
 
     ids_t = expert_ids.T
     hits = jnp.zeros((expert_count, seq_len), jnp.bool_)
@@ -478,21 +511,17 @@
     cosine = jnp.tile(jnp.cos(angles), (1, 4))
     sine = jnp.tile(jnp.concatenate([-jnp.sin(angles), jnp.sin(angles)], axis=1), (1, 2))
 
-    input_rows = block_input.astype(f32)
-    attn_normed = (input_rows * row_scale(input_rows) * attn_gain).astype(bf16)
-    attn_tokens = gather_rows(attn_normed, tensor_size)
-    grad_rows = out_grad.astype(f32)
-    moe_rows = (residual_scale * grad_rows).astype(bf16)
-    qkv_full, moe_rows, codes = lax.optimization_barrier((qkv_full, moe_rows, codes))
-    moe_grad = gather_group(moe_rows, tensor_size)
     qkv_pre = jnp.dot(attn_tokens, qkv_full, preferred_element_type=f32)
+    qkv_pre, moe_own, codes = together(qkv_pre, moe_own, codes)
+    moe_across = swap(moe_own, "y")
     attn_mixed, qkv_rot, log_totals = attention_forward(qkv_pre, cosine, sine)
-    attn_mixed, moe_grad = lax.optimization_barrier((attn_mixed, moe_grad))
     attn_out = scatter_rows(contract(attn_mixed, out_full, 1, 1), tensor_size)
+    attn_out, moe_across = lax.optimization_barrier((attn_out, moe_across))
+    moe_grad = jnp.stack([moe_own, moe_across, swap(moe_own, "core"), swap(moe_across, "core")])
     hidden_state = input_rows + residual_scale * attn_out
     ffn_normed = (hidden_state * row_scale(hidden_state) * ffn_gain).astype(bf16)
 
-    tokens = gather_group(ffn_normed, tensor_size)
+    tokens = gather_group(ffn_normed, tensor_size, moe_grad)
     logits = ein("dx,std->sxt", router_weight, tokens)
     chosen = codes > -1.5
     top_logit = jnp.max(jnp.where(chosen, logits, -jnp.inf), axis=1, keepdims=True)
@@ -503,7 +532,7 @@
     code_own = lax.dynamic_slice_in_dim(codes, expert_first, owned, 1).astype(jnp.int32)
     gate_own = lax.dynamic_slice_in_dim(gates, expert_first, owned, 1)
 
-    carry, pairs, parts = (), [], []
+    carry, pairs, parts, shared = (), [], [], ()
     for e in range(owned):
         *carry, pair, part = run_expert(
             member.reshape(1).astype(jnp.int32),
@@ -511,11 +540,16 @@
             moe_grad,
             code_own[:, e : e + 1],
             gate_own[:, e : e + 1],
-            weights[e],
+            weights[e // bunch],
+            e % bunch,
             carry,
+            shared,
         )
         pairs.append(pair)
-        parts.append(lax.psum_scatter(part, "z", scatter_dimension=0, tiled=False))
+        shared = (part,)
+        if (e + 1) % bunch == 0:
+            parts.append(lax.psum_scatter(part, "z", scatter_dimension=0, tiled=False))
+            shared = ()
     moe_parts, normed_parts = carry
 
     pair_grad = jnp.concatenate(pairs, axis=1)
@@ -531,47 +565,100 @@
         local = seq_len // tensor_size
         pair_all = lax.all_gather(pair_y, "tensor", axis=0, tiled=True)
         pair_all = lax.dynamic_slice_in_dim(pair_all, my_tensor * local, local, 1)
+    normed_pair, pair_all = together(add_core(normed_parts), pair_all)
+    normed_local = scatter_group(normed_pair, tensor_size)
+
+    def core_owners(part):
+        part = jnp.moveaxis(part.reshape(bunch, 2, 2, rows, both_width), 2, 0)
+        return stacked(part[0], swap(part[1], "core"), core_first, 0)
+
+    def y_owners(part):
+        keep, give = part[:, :, 0], part[:, :, 1]
+        return stacked(keep, swap(give, "y"), y_first, 0)
+
+    early = parts[:-1]
+    normed_local, *early = together(normed_local, *[core_owners(part) for part in early])
     gates_local = lax.dynamic_slice_in_dim(gates[0], my_tensor * local, local, 1)
     gate_dot = jnp.sum(gates_local * pair_all, axis=0, keepdims=True)
     logit_low = (gates_local * (pair_all - gate_dot)).astype(bf16)
 
-    normed_local = scatter_group(normed_parts, tensor_size)
-    normed_local, moe_parts = lax.optimization_barrier((normed_local, moe_parts))
     normed_local = normed_local + contract(logit_low, router_weight, 0, 1)
     router_part = jnp.dot(logit_low, ffn_normed, preferred_element_type=f32)
     state_grad, ffn_gain_part = norm_backward(normed_local, hidden_state, ffn_gain)
     state_grad = state_grad + grad_rows
-    steps = (("core", 2), ("y", 2), ("tensor", tensor_size), ("z", z_size))
     attn_grad_all = gather_rows((residual_scale * state_grad).astype(bf16), tensor_size)
-    moe_out = scatter_group(moe_parts, tensor_size)
-    block_output = (hidden_state + residual_scale * moe_out).astype(bf16)
-
-    def scatter_dp(part):
-        part = part.reshape(z_size, 2, 2, shard_rows, part.shape[1])
-        part = jnp.take(part, my_core, axis=2), jnp.take(part, 1 - my_core, axis=2)
-        part = part[0].astype(f32) + swap(part[1].astype(bf16), "core").astype(f32)
-        part = jnp.take(part, my_y, axis=1), jnp.take(part, 1 - my_y, axis=1)
-        part = part[0] + swap(part[1].astype(bf16), "y").astype(f32)
-        return lax.psum_scatter(part.astype(bf16), "z", scatter_dimension=0, tiled=False)
-
-    out_sum = scatter_dp(contract(attn_grad_all, attn_mixed, 0, 0))
+    moe_pair = add_core(after(moe_parts, normed_pair))
+    owners = [y_owners(part) for part in early]
+    attn_grad_all, moe_pair, *owners = together(attn_grad_all, moe_pair, *owners)
+    if tensor_size == 2:
+        local = seq_len // 2
+        moe_far = lax.dynamic_slice_in_dim(moe_pair[1], (1 - my_tensor) * local, local, 0)
+        moe_near = lax.dynamic_slice_in_dim(moe_pair[1], my_tensor * local, local, 0)
+    else:
+        moe_far, moe_near = moe_pair[1], jnp.zeros((1, width), bf16)
+    moe_far = swap(moe_far, "y")
+
+    def halves(part, mine):
+        return at(part, mine), at(part, 1 - mine).astype(bf16)
+
+    def by_dp(part):
+        return part.reshape(z_size, 2, 2, shard_rows, part.shape[1])
+
+    def add(keep, given):
+        return keep.astype(f32) + given.astype(f32)
+
+    out_part = contract(attn_grad_all, attn_mixed, 0, 0)
+    out_keep, out_give = halves(jnp.moveaxis(by_dp(out_part), 2, 0), my_core)
+    out_given = swap(out_give, "core")
     mixed_grad = jnp.dot(attn_grad_all, out_full, preferred_element_type=f32).astype(bf16)
     qkv_pre_grad = attention_backward(qkv_rot, mixed_grad, log_totals, cosine, sine)
-    qkv_pre_grad, block_output = lax.optimization_barrier((qkv_pre_grad, block_output))
-    attn_normed_grad = scatter_rows(contract(qkv_pre_grad, qkv_full, 1, 1), tensor_size)
-    qkv_sum = scatter_dp(contract(attn_tokens, qkv_pre_grad, 0, 0))
+    qkv_pre_grad, moe_far, out_given = together(qkv_pre_grad, moe_far, out_given)
+
+    out_keep, out_give = halves(jnp.moveaxis(add(out_keep, out_given), 1, 0), my_y)
+    attn_part = contract(qkv_pre_grad, qkv_full, 1, 1)
+    attn_scattered = scatter_rows(attn_part, tensor_size)
+    qkv_part = contract(attn_tokens, qkv_pre_grad, 0, 0)
+    qkv_keep, qkv_give = halves(jnp.moveaxis(by_dp(qkv_part), 2, 0), my_core)
+    attn_normed_grad, moe_near, qkv_given = together(
+        attn_scattered, swap(moe_near, "y"), swap(qkv_give, "core")
+    )
     input_part, attn_gain_part = norm_backward(attn_normed_grad, input_rows, attn_gain)
     input_grad = (state_grad + input_part).astype(bf16)
     small = jnp.concatenate(
         [router_part, ffn_gain_part[None, :], attn_gain_part[None, :]], axis=0
     )
-    small = butterfly_sum(small, steps)
-
-    owners = []
-    for part in parts:
-        near = stacked(part[0::2], swap(part[1::2], "core"), core_first)
-        owners.append(in_order(near[0], swap(near[1], "y"), y_first))
-    summed = jnp.stack(owners, axis=1).reshape(experts_local, rows, both_width)
+    if tensor_size == 2:
+        moe_give = lax.dynamic_slice_in_dim(moe_pair[0], (1 - my_tensor) * local, local, 0)
+        moe_keep = lax.dynamic_slice_in_dim(moe_pair[0], my_tensor * local, local, 0)
+        moe_sum = add(moe_keep, moe_near)
+        moe_given = swap(add(moe_give, moe_far).astype(bf16), "tensor")
+    else:
+        moe_sum = jnp.zeros((local, width), f32)
+        moe_given = scatter_rows(add(moe_pair[0], moe_far), tensor_size)
+    qkv_keep, qkv_give = halves(jnp.moveaxis(add(qkv_keep, qkv_given), 1, 0), my_y)
+    small = butterfly_sum(small, (("core", 2), ("z", z_size)))
+    small, qkv_given, out_given = together(small, swap(qkv_give, "y"), swap(out_give, "y"))
+
+    def z_scatter(part):
+        step = z_size // 2
+        while step:
+            keep, give = halves(
+                part.reshape(2, -1, shard_rows, part.shape[-1]), (my_z // step) % 2
+            )
+            pairs = [(i, i ^ step) for i in range(z_size)]
+            part = add(keep, lax.ppermute(give, "z", pairs))
+            step //= 2
+        return part.reshape(shard_rows, part.shape[-1])
+
+    dp_part = jnp.concatenate([add(qkv_keep, qkv_given), add(out_keep, out_given)], axis=-1)
+    dp_sum = z_scatter(dp_part)
+    small, moe_given, dp_sum = together(butterfly_sum(small, (("y", 2),)), moe_given, dp_sum)
+    qkv_sum, out_sum = dp_sum[:, :wide], dp_sum[:, wide:]
+    block_output = (hidden_state + residual_scale * add(moe_sum, moe_given)).astype(bf16)
+    small = butterfly_sum(small, (("tensor", tensor_size),))
+    owners.append(y_owners(core_owners(after(parts[-1], dp_sum))))
+    summed = jnp.concatenate(owners, axis=2)
+    summed = summed.reshape(experts_local, rows, both_width)
     both_rows = gate_weight.shape[1]
     qkv_sum = qkv_sum.reshape(shard_rows, groups, -1)
     return (

time: 786 us -> 668 us (0.85)
  waiting for transfers between devices: 318 us -> 235 us
  blocking collectives: 20.3 us -> 0 us
  starting transfers between devices: 48.6 us -> 31.9 us
    reduce_scatter x4 -> x2, waiting for transfers between devices: 52.4 us -> 0.01 us  [shards(): parts.append(lax.psum_scatter(part, 'z', scatter_dimension=0, tiled=False))]
    ppermute x51 -> x40, waiting for transfers between devices: 235 us -> 191 us  [swap(): return lax.ppermute(values, axis, [(0, 1), (1, 0)])]
    all_gather x1 -> x0, blocking collectives: 20.3 us -> none  [shards(): by_z = lax.all_gather(packed, 'z', axis=0, tiled=False)]
    another operation x28 -> x15, other arithmetic: 39.9 us -> 24.4 us  [the longest x3 8.38 us: gather_group(): return jnp.stack([own, across, own_core, swap(across, 'core')])]
    ppermute x51 -> x40, starting transfers between devices: 43.7 us -> 28.9 us  [swap(): return lax.ppermute(values, axis, [(0, 1), (1, 0)])]
    ppermute x0 -> x2, waiting for transfers between devices: none -> 14.6 us  [z_scatter(): part = add(keep, lax.ppermute(give, 'z', pairs))]
    ppermute x5, waiting for transfers between devices: 30.8 us -> 19.3 us  [butterfly_sum(): lax.ppermute(values, axis, [(i, i ^ step) for i in range(size)])]
    convert_element_type x9 -> x5, other arithmetic: 6.5 us -> 17.6 us  [the longest x2 11.5 us: add_core(): return (parts[:2].astype(f32) + given.astype(f32)).astype(bf16)]
  transfers between devices with their start and end apart: 66 -> 52, of which waited for: 33 -> 29; matrix products, arithmetic and copies ran while one was open for 19% -> 22% of each run, Pallas kernels for 26% -> 31%
where the time goes in v3:
time: 668 us; the launch traced here: 663 us
  waiting for transfers between devices  235 us (35%)
  Pallas kernels  203 us (30%)
  other arithmetic  89 us (13%)
  local copies, waits for them, and re-layouts  62 us (9%)
  starting transfers between devices  31.9 us (5%)
  matrix products  26.6 us (4%)
  between operations  15.1 us (2%)
    ppermute x40, waiting for transfers between devices, swap(): return lax.ppermute(values, axis, [(0, 1), (1, 0)])  191 us
    pallas_call x4, Pallas kernels, run_expert(): pl.pallas_call(functools.partial(expert_kernel, bool(carry), bool(shared)...  160 us
    ppermute x40, starting transfers between devices, swap(): return lax.ppermute(values, axis, [(0, 1), (1, 0)])  28.9 us
    pallas_call x1, Pallas kernels, attention_backward(): pl.pallas_call(attention_backward_kernel, grid=(groups,), in_specs=[wide,...  26.5 us
    ppermute x5, waiting for transfers between devices, butterfly_sum(): lax.ppermute(values, axis, [(i, i ^ step) for i in range(size)])  19.3 us
    pallas_call x1, Pallas kernels, attention_forward(): pl.pallas_call(attention_forward_kernel, grid=(groups,), in_specs=[wide,...  17.4 us
    unnamed x105, local copies, waits for them, and re-layouts  15.5 us
    ppermute x2, waiting for transfers between devices, z_scatter(): part = add(keep, lax.ppermute(give, 'z', pairs))  14.6 us
  transfers between devices with their start and end apart: 52, of which 29 were waited for; matrix products, arithmetic and copies ran while one was open for 22% of the time, Pallas kernels for 31%

profile of v3, /device:TPU:0, one launch (start us, length us, event | category | flops | bytes accessed | tf_op | source)
XLA Modules:
  0.0 663.0 jit_solution(7946856924847148114)
XLA Ops:
  22.9 17.3 %collective-permute-done = bf16[512,1024]{1,0:T(8,128)(2,1)} collective-permute-done((bf16[512,1024]{1,0:T(8,128)(2,1)}, bf16[512,1024]{1,0:T(8,128)(2,1)}, u32[]{:S(2)}, u32[]{:S(2)}) %collective-permute-start) | collective-permute-done | bytes 1048608 | tf_op jit(solution)/shard_map/ppermute | solution.py:58
  46.9 20.9 %collective-permute-done.3 = bf16[2,4,96,1024]{3,2,1,0:T(8,128)(2,1)} collective-permute-done((bf16[2,4,96,1024]{3,2,1,0:T(8,128)(2,1)}, bf16[2,4,96,1024]{3,2,1,0:T(8,128)(2,1)}, u32[]{:S(2)}, u32[]{:S(2)}) %collective-permute-start.3) | collective-permute-done | bytes 1572896 | tf_op jit(solution)/shard_map/ppermute | solution.py:58
  73.6 4.0 fusion.82
  80.2 4.6 collective-permute-done.5
  94.8 6.6 fusion.23.pre_ref
  102.6 17.4 %attention_forward.1 = (bf16[1024,512]{1,0:T(8,128)(2,1)}, bf16[1024,1024]{1,0:T(8,128)(2,1)}, f32[1024,512]{1,0:T(8,128)}) custom-call(f32[1024,1024]{1,0:T(8,128)} %fusion.23.pre_ref, f32[1024,128]{1,0:T(8,128)} %copy.48.cos_ref, f32[1024,128]{1,0:T(8,128)} %copy.49.sin_ref), custom_call_target="tpu_custom_call" | custom-call | flops 3221225472 | bytes 10485760 | tf_op jit(solution)/shard_map/attention_forward/pallas_call | solution.py:249
  126.8 24.7 %collective-permute-done.8 = bf16[512,1024]{1,0:T(8,128)(2,1)} collective-permute-done((bf16[512,1024]{1,0:T(8,128)(2,1)}, bf16[512,1024]{1,0:T(8,128)(2,1)}, u32[]{:S(2)}, u32[]{:S(2)}) %collective-permute-start.8) | collective-permute-done | bytes 1048608 | tf_op jit(solution)/shard_map/ppermute | solution.py:58
  158.3 5.7 pad_maximum_fusion.grad_ref
  164.0 16.3 %collective-permute-done.10 = bf16[512,1024]{1,0:T(8,128)(2,1)S(1)} collective-permute-done((bf16[512,1024]{1,0:T(8,128)(2,1)S(1)}, bf16[512,1024]{1,0:T(8,128)(2,1)S(1)}, u32[]{:S(2)}, u32[]{:S(2)}) %collective-permute-start.10) | collective-permute-done | bytes 1048608 | tf_op jit(solution)/shard_map/ppermute | solution.py:58
  187.3 12.4 %collective-permute-done.14 = bf16[256,1024]{1,0:T(8,128)(2,1)} collective-permute-done((bf16[256,1024]{1,0:T(8,128)(2,1)}, bf16[256,1024]{1,0:T(8,128)(2,1)}, u32[]{:S(2)}, u32[]{:S(2)}) %collective-permute-start.14) | collective-permute-done | bytes 524320 | tf_op jit(solution)/shard_map/ppermute | solution.py:58
  219.3 38.6 %expert.4 = (bf16[4,1024,1024]{2,1,0:T(8,128)(2,1)}, bf16[4,1024,1024]{2,1,0:T(8,128)(2,1)}, f32[4,1,1024]{2,1,0:T(1,128)}, bf16[4,2,4,96,1024]{4,3,2,1,0:T(8,128)(2,1)}) custom-call(s32[1]{0:T(128)} %bitcast.24.member_ref, bf16[4,1024,1024]{2,1,0:T(8,128)(2,1)} %copy-done.5, bf16[4,1024,1024]{2,1,0:T(8,128)(2,1)} %pad_maximum_fusion.grad_ref, ...), custom_call_target="tpu_custom_call" | custom-call | flops 22817013760 | bytes 56623104 | tf_op jit(solution)/shard_map/expert/pallas_call | solution.py:377
  257.9 40.3 %expert.5 = (bf16[4,1024,1024]{2,1,0:T(8,128)(2,1)}, bf16[4,1024,1024]{2,1,0:T(8,128)(2,1)}, f32[4,1,1024]{2,1,0:T(1,128)}, bf16[4,2,4,96,1024]{4,3,2,1,0:T(8,128)(2,1)}) custom-call(s32[1]{0:T(128)} %bitcast.24.member_ref, bf16[4,1024,1024]{2,1,0:T(8,128)(2,1)} %copy-done.5, ...), custom_call_target="tpu_custom_call", output_to_operand_aliasing={{3}: (8, {})} | custom-call | flops 22817013760 | bytes 56623104 | tf_op jit(solution)/shard_map/expert/pallas_call | solution.py:377
  298.3 10.2 %all-gather.8.cloned.1.call-done = bf16[8,4,96,1024]{3,2,1,0:T(8,128)(2,1)} async-done(((bf16[2,4,96,1024]{3,2,1,0:T(8,128)(2,1)}), bf16[8,4,96,1024]{3,2,1,0:T(8,128)(2,1)}) %all-gather.8.cloned.1.call-update) | async-done | bytes 6291472 | tf_op jit(solution)/shard_map/all_gather | solution.py:495
  308.5 40.4 %expert.6 = (bf16[4,1024,1024]{2,1,0:T(8,128)(2,1)}, bf16[4,1024,1024]{2,1,0:T(8,128)(2,1)}, f32[4,1,1024]{2,1,0:T(1,128)}, bf16[4,2,4,96,1024]{4,3,2,1,0:T(8,128)(2,1)}) custom-call(s32[1]{0:T(128)} %bitcast.24.member_ref, bf16[4,1024,1024]{2,1,0:T(8,128)(2,1)} %copy-done.5, bf16[4,1024,1024]{2,1,0:T(8,128)(2,1)} %pad_maximum_fusion.grad_ref, ...), custom_call_target="tpu_custom_call" | custom-call | flops 22817013760 | bytes 56623104 | tf_op jit(solution)/shard_map/expert/pallas_call | solution.py:377
  348.9 40.3 %expert.7 = (bf16[4,1024,1024]{2,1,0:T(8,128)(2,1)}, bf16[4,1024,1024]{2,1,0:T(8,128)(2,1)}, f32[4,1,1024]{2,1,0:T(1,128)}, bf16[4,2,4,96,1024]{4,3,2,1,0:T(8,128)(2,1)}) custom-call(s32[1]{0:T(128)} %bitcast.24.member_ref, bf16[4,1024,1024]{2,1,0:T(8,128)(2,1)} %copy-done.5, ...), custom_call_target="tpu_custom_call", output_to_operand_aliasing={{3}: (8, {})} | custom-call | flops 22817013760 | bytes 56623104 | tf_op jit(solution)/shard_map/expert/pallas_call | solution.py:377
  389.3 4.7 slice.222
  394.6 6.8 %collective-permute-done.19 = f32[2,4,1024]{2,1,0:T(4,128)S(1)} collective-permute-done((f32[2,4,1024]{2,1,0:T(4,128)S(1)}, f32[2,4,1024]{2,1,0:T(4,128)S(1)}, u32[]{:S(2)}, u32[]{:S(2)}) %collective-permute-start.19) | collective-permute-done | bytes 32800 | tf_op jit(solution)/shard_map/ppermute | solution.py:58
  409.6 5.9 add_convert_fusion.1
  428.4 4.4 collective-permute-done.22
  443.6 15.7 %collective-permute-done.25 = bf16[512,1024]{1,0:T(8,128)(2,1)S(1)} collective-permute-done((bf16[512,1024]{1,0:T(8,128)(2,1)}, bf16[512,1024]{1,0:T(8,128)(2,1)S(1)}, u32[]{:S(2)}, u32[]{:S(2)}) %collective-permute-start.25) | collective-permute-done | bytes 1048608 | tf_op jit(solution)/shard_map/ppermute | solution.py:58
  471.0 5.6 add_convert_fusion
  476.6 6.2 collective-permute-done.29
  484.1 7.7 %collective-permute-done.27 = bf16[512,1024]{1,0:T(8,128)(2,1)S(1)} collective-permute-done((bf16[512,1024]{1,0:T(8,128)(2,1)S(1)}, bf16[512,1024]{1,0:T(8,128)(2,1)S(1)}, u32[]{:S(2)}, u32[]{:S(2)}) %collective-permute-start.27) | collective-permute-done | bytes 1048608 | tf_op jit(solution)/shard_map/ppermute | solution.py:58
  504.3 26.5 %attention_backward.1 = bf16[1024,1024]{1,0:T(8,128)(2,1)} custom-call(bf16[1024,1024]{1,0:T(8,128)(2,1)} %get-tuple-element.113.rot_ref, bf16[1024,512]{1,0:T(8,128)(2,1)} %convolution_convert_fusion.grad_ref, f32[1024,512]{1,0:T(8,128)} %get-tuple-element.115.lse_ref, f32[1024,128]{1,0:T(8,128)} %copy.48.cos_ref, f32[1024,128]{1,0:T(8,128)} %copy.49.sin_ref), custom_call_target="tpu_custom_call" | custom-call | flops 8589934592 | bytes 10485760 | tf_op jit(solution)/shard_map/attention_backward/pallas_call | solution.py:273
  530.7 4.7 fusion.21
  542.8 18.0 %collective-permute-done.32 = bf16[512,1024]{1,0:T(8,128)(2,1)S(1)} collective-permute-done((bf16[512,1024]{1,0:T(8,128)(2,1)S(1)}, bf16[512,1024]{1,0:T(8,128)(2,1)S(1)}, u32[]{:S(2)}, u32[]{:S(2)}) %collective-permute-start.32) | collective-permute-done | bytes 1048608 | tf_op jit(solution)/shard_map/ppermute | solution.py:58
  567.5 4.1 collective-permute-done.36
  572.2 9.6 %collective-permute-done.37 = f32[34,1024]{1,0:T(8,128)} collective-permute-done((f32[34,1024]{1,0:T(8,128)S(1)}, f32[34,1024]{1,0:T(8,128)}, u32[]{:S(2)}, u32[]{:S(2)}) %collective-permute-start.37) | collective-permute-done | bytes 139296 | tf_op jit(solution)/shard_map/ppermute | solution.py:65
  593.8 14.2 %collective-permute-done.42 = bf16[2,64,1536]{2,1,0:T(8,128)(2,1)} collective-permute-done((bf16[2,64,1536]{2,1,0:T(8,128)(2,1)}, bf16[2,64,1536]{2,1,0:T(8,128)(2,1)}, u32[]{:S(2)}, u32[]{:S(2)}) %collective-permute-start.42) | collective-permute-done | bytes 393248 | tf_op jit(solution)/shard_map/ppermute | solution.py:649
  611.3 5.6 collective-permute-done.40
  623.9 5.2 fusion.13
  637.1 14.2 %collective-permute-done.46 = bf16[2,2,96,1024]{3,2,1,0:T(8,128)(2,1)S(1)} collective-permute-done((bf16[2,2,96,1024]{3,2,1,0:T(8,128)(2,1)S(1)}, bf16[2,2,96,1024]{3,2,1,0:T(8,128)(2,1)S(1)}, u32[]{:S(2)}, u32[]{:S(2)}) %collective-permute-start.46) | collective-permute-done | bytes 786464 | tf_op jit(solution)/shard_map/ppermute | solution.py:58
  (325 shorter events, 188.9 us)
Async XLA Ops:
  7.2 66.4 %all-gather.6.cloned.1.call-start = ((), (), s32[]{:S(2)}) async-start(), calls=%async_computation.2 | async-start | bytes 3342336 | tf_op jit(solution)/shard_map/all_gather | solution.py:459
  10.9 208.4 %all-gather.10.cloned.1.call-start = ((), (), s32[]{:S(2)}) async-start(), calls=%async_computation.6 | async-start | bytes 7864320 | tf_op jit(solution)/shard_map/all_gather | solution.py:495
  13.7 26.4 %collective-permute-start = (bf16[512,1024]{1,0:T(8,128)(2,1)}, bf16[512,1024]{1,0:T(8,128)(2,1)}, u32[]{:S(2)}, u32[]{:S(2)}) collective-permute-start(bf16[512,1024]{1,0:T(8,128)(2,1)} %fusion.7), channel_id=1, source_target_pairs={{0,1},{1,0},{2,3},{3,2},{4,5},{5,4},{6,7},{7,6},{8,9},{9,8},{10,11... | collective-permute-start | bytes 3145736 | tf_op jit(solution)/shard_map/ppermute | solution.py:58
  21.1 46.7 %collective-permute-start.3 = (bf16[2,4,96,1024]{3,2,1,0:T(8,128)(2,1)}, bf16[2,4,96,1024]{3,2,1,0:T(8,128)(2,1)}, u32[]{:S(2)}, u32[]{:S(2)}) collective-permute-start(bf16[2,4,96,1024]{3,2,1,0:T(8,128)(2,1)} %dynamic-slice_bitcast_fusion), channel_id=1, source_target_pairs={{0,4},{4,0},{1,5},{5,1},{2,6},{6,2},{3,7},{7,3},{8,12},{12,8},{9,1... | collective-permute-start | bytes 4718600 | tf_op jit(solution)/shard_map/ppermute | solution.py:58
  43.6 25.9 %collective-permute-start.1 = (bf16[512,1024]{1,0:T(8,128)(2,1)S(1)}, bf16[512,1024]{1,0:T(8,128)(2,1)S(1)}, u32[]{:S(2)}, u32[]{:S(2)}) collective-permute-start(bf16[512,1024]{1,0:T(8,128)(2,1)S(1)} %fusion.6), channel_id=1, source_target_pairs={{0,1},{1,0},{2,3},{3,2},{4,5},{5,4},{6,7},{7,6},{8,9},{9,8},{10,11... | collective-permute-start | bytes 3145736 | tf_op jit(solution)/shard_map/ppermute | solution.py:58
  46.8 23.0 %collective-permute-start.2 = (bf16[4,96,1024]{2,1,0:T(8,128)(2,1)S(1)}, bf16[4,96,1024]{2,1,0:T(8,128)(2,1)S(1)}, u32[]{:S(2)}, u32[]{:S(2)}) collective-permute-start(bf16[4,96,1024]{2,1,0:T(8,128)(2,1)S(1)} %get-tuple-element.146), channel_id=1, source_target_pairs={{0,2},{2,0},{1,3},{3,1},{4,6},{6,4},{5,7},{7,5},{8,10},{10,8},{9,1... | collective-permute-start | bytes 2359304 | tf_op jit(solution)/shard_map/ppermute | solution.py:58
  77.6 230.9 %all-gather.8.cloned.1.call-start = ((), (), s32[]{:S(2)}) async-start(), calls=%async_computation.5 | async-start | bytes 7864320 | tf_op jit(solution)/shard_map/all_gather | solution.py:495
  101.4 52.4 %collective-permute-start.9 = (bf16[1024,1024]{1,0:T(8,128)(2,1)S(1)}, bf16[1024,1024]{1,0:T(8,128)(2,1)}, u32[]{:S(2)}, u32[]{:S(2)}) collective-permute-start(bf16[1024,1024]{1,0:T(8,128)(2,1)S(1)} %pad_maximum_fusion.5), channel_id=1, source_target_pairs={{0,4},{4,0},{1,5},{5,1},{2,6},{6,2},{3,7},{7,3},{8,12},{12,8},{9,1... | collective-permute-start | bytes 6291464 | tf_op jit(solution)/shard_map/ppermute | solution.py:58
  126.0 25.6 %collective-permute-start.8 = (bf16[512,1024]{1,0:T(8,128)(2,1)}, bf16[512,1024]{1,0:T(8,128)(2,1)}, u32[]{:S(2)}, u32[]{:S(2)}) collective-permute-start(bf16[512,1024]{1,0:T(8,128)(2,1)} %dynamic-slice_convert_fusion.3), channel_id=1, source_target_pairs={{0,1},{1,0},{2,3},{3,2},{4,5},{5,4},{6,7},{7,6},{8,9},{9,8},{10,11... | collective-permute-start | bytes 3145736 | tf_op jit(solution)/shard_map/ppermute | solution.py:58
  126.8 29.2 %collective-permute-start.12 = (bf16[1024,1024]{1,0:T(8,128)(2,1)S(1)}, bf16[1024,1024]{1,0:T(8,128)(2,1)S(1)}, u32[]{:S(2)}, u32[]{:S(2)}) collective-permute-start(bf16[1024,1024]{1,0:T(8,128)(2,1)S(1)} %pad_maximum_fusion.5), channel_id=1, source_target_pairs={{0,2},{2,0},{1,3},{3,1},{4,6},{6,4},{5,7},{7,5},{8,10},{10,8},{9,1... | collective-permute-start | bytes 6291464 | tf_op jit(solution)/shard_map/ppermute | solution.py:58
  154.8 25.5 %collective-permute-start.10 = (bf16[512,1024]{1,0:T(8,128)(2,1)S(1)}, bf16[512,1024]{1,0:T(8,128)(2,1)S(1)}, u32[]{:S(2)}, u32[]{:S(2)}) collective-permute-start(bf16[512,1024]{1,0:T(8,128)(2,1)S(1)} %multiply_convert_fusion.1), channel_id=1, source_target_pairs={{0,1},{1,0},{2,3},{3,2},{4,5},{5,4},{6,7},{7,6},{8,9},{9,8},{10,11... | collective-permute-start | bytes 3145736 | tf_op jit(solution)/shard_map/ppermute | solution.py:58
  155.7 25.2 %collective-permute-start.11 = (bf16[512,1024]{1,0:T(8,128)(2,1)S(1)}, bf16[512,1024]{1,0:T(8,128)(2,1)S(1)}, u32[]{:S(2)}, u32[]{:S(2)}) collective-permute-start(bf16[512,1024]{1,0:T(8,128)(2,1)S(1)} %multiply_convert_fusion.1), channel_id=1, source_target_pairs={{0,4},{4,0},{1,5},{5,1},{2,6},{6,2},{3,7},{7,3},{8,12},{12,8},{9,1... | collective-permute-start | bytes 3145736 | tf_op jit(solution)/shard_map/ppermute | solution.py:58
  183.3 17.2 %collective-permute-start.16 = (bf16[1024,1024]{1,0:T(8,128)(2,1)}, bf16[1024,1024]{1,0:T(8,128)(2,1)}, u32[]{:S(2)}, u32[]{:S(2)}) collective-permute-start(bf16[1024,1024]{1,0:T(8,128)(2,1)} %get-tuple-element.160), channel_id=1, source_target_pairs={{0,2},{2,0},{1,3},{3,1},{4,6},{6,4},{5,7},{7,5},{8,10},{10,8},{9,1... | collective-permute-start | bytes 6291464 | tf_op jit(solution)/shard_map/ppermute | solution.py:58
  187.1 253.9 %reduce-scatter.3.cloned.1.call-start = ((), (), s32[]{:S(2)}) async-start(), calls=%async_computation.3 | async-start | bytes 7864320 | tf_op jit(solution)/shard_map/reduce_scatter | solution.py:551
  298.2 321.5 %reduce-scatter.5.cloned.1.call-start = ((), (), s32[]{:S(2)}) async-start(), calls=%async_computation.4 | async-start | bytes 7864320 | tf_op jit(solution)/shard_map/reduce_scatter | solution.py:551
  393.9 15.6 %collective-permute-start.18 = (bf16[2,1024,1024]{2,1,0:T(8,128)(2,1)}, bf16[2,1024,1024]{2,1,0:T(8,128)(2,1)}, u32[]{:S(2)}, u32[]{:S(2)}) collective-permute-start(bf16[2,1024,1024]{2,1,0:T(8,128)(2,1)} %slice.222), channel_id=1, source_target_pairs={{0,2},{2,0},{1,3},{3,1},{4,6},{6,4},{5,7},{7,5},{8,10},{10,8},{9,1... | collective-permute-start | bytes 12582920 | tf_op jit(solution)/shard_map/ppermute | solution.py:58
  425.8 45.1 %collective-permute-start.28 = (bf16[2,1024,1024]{2,1,0:T(8,128)(2,1)}, bf16[2,1024,1024]{2,1,0:T(8,128)(2,1)}, u32[]{:S(2)}, u32[]{:S(2)}) collective-permute-start(bf16[2,1024,1024]{2,1,0:T(8,128)(2,1)} %slice.245), channel_id=1, source_target_pairs={{0,2},{2,0},{1,3},{3,1},{4,6},{6,4},{5,7},{7,5},{8,10},{10,8},{9,1... | collective-permute-start | bytes 12582920 | tf_op jit(solution)/shard_map/ppermute | solution.py:58
  436.5 22.8 %collective-permute-start.25 = (bf16[512,1024]{1,0:T(8,128)(2,1)}, bf16[512,1024]{1,0:T(8,128)(2,1)S(1)}, u32[]{:S(2)}, u32[]{:S(2)}) collective-permute-start(bf16[512,1024]{1,0:T(8,128)(2,1)} %pad_maximum_fusion.13), channel_id=1, source_target_pairs={{0,4},{4,0},{1,5},{5,1},{2,6},{6,2},{3,7},{7,3},{8,12},{12,8},{9,1... | collective-permute-start | bytes 3145736 | tf_op jit(solution)/shard_map/ppermute | solution.py:58
  440.4 22.6 %collective-permute-start.24 = (bf16[512,1024]{1,0:T(8,128)(2,1)}, bf16[512,1024]{1,0:T(8,128)(2,1)}, u32[]{:S(2)}, u32[]{:S(2)}) collective-permute-start(bf16[512,1024]{1,0:T(8,128)(2,1)} %pad_maximum_fusion.12), channel_id=1, source_target_pairs={{0,1},{1,0},{2,3},{3,2},{4,5},{5,4},{6,7},{7,6},{8,9},{9,8},{10,11... | collective-permute-start | bytes 3145736 | tf_op jit(solution)/shard_map/ppermute | solution.py:58
  443.5 21.9 %collective-permute-start.26 = (bf16[2,2,96,1024]{3,2,0,1:T(8,128)(2,1)}, bf16[2,2,96,1024]{3,2,0,1:T(8,128)(2,1)}, u32[]{:S(2)}, u32[]{:S(2)}) collective-permute-start(bf16[2,2,96,1024]{3,2,0,1:T(8,128)(2,1)} %slice_bitcast_fusion.1), channel_id=1, source_target_pairs={{0,2},{2,0},{1,3},{3,1},{4,6},{6,4},{5,7},{7,5},{8,10},{10,8},{9,1... | collective-permute-start | bytes 2359304 | tf_op jit(solution)/shard_map/ppermute | solution.py:58
  466.9 15.9 %collective-permute-start.29 = (bf16[2,2,96,1024]{3,2,1,0:T(8,128)(2,1)S(1)}, bf16[2,2,96,1024]{3,2,1,0:T(8,128)(2,1)S(1)}, u32[]{:S(2)}, u32[]{:S(2)}) collective-permute-start(bf16[2,2,96,1024]{3,2,1,0:T(8,128)(2,1)S(1)} %slice_bitcast_fusion.3), channel_id=1, source_target_pairs={{0,4},{4,0},{1,5},{5,1},{2,6},{6,2},{3,7},{7,3},{8,12},{12,8},{9,1... | collective-permute-start | bytes 2359304 | tf_op jit(solution)/shard_map/ppermute | solution.py:58
  470.4 21.4 %collective-permute-start.27 = (bf16[512,1024]{1,0:T(8,128)(2,1)S(1)}, bf16[512,1024]{1,0:T(8,128)(2,1)S(1)}, u32[]{:S(2)}, u32[]{:S(2)}) collective-permute-start(bf16[512,1024]{1,0:T(8,128)(2,1)S(1)} %multiply_convert_fusion), channel_id=1, source_target_pairs={{0,1},{1,0},{2,3},{3,2},{4,5},{5,4},{6,7},{7,6},{8,9},{9,8},{10,11... | collective-permute-start | bytes 3145736 | tf_op jit(solution)/shard_map/ppermute | solution.py:58
  495.9 34.8 %collective-permute-start.31 = (bf16[4,2,64,512]{3,2,1,0:T(8,128)(2,1)}, bf16[4,2,64,512]{3,2,1,0:T(8,128)(2,1)}, u32[]{:S(2)}, u32[]{:S(2)}) collective-permute-start(bf16[4,2,64,512]{3,2,1,0:T(8,128)(2,1)} %fusion.46), channel_id=1, source_target_pairs={{0,2},{2,0},{1,3},{3,1},{4,6},{6,4},{5,7},{7,5},{8,10},{10,8},{9,1... | collective-permute-start | bytes 1572872 | tf_op jit(solution)/shard_map/ppermute | solution.py:58
  498.8 32.0 %collective-permute-start.30 = (bf16[512,1024]{1,0:T(8,128)(2,1)S(1)}, bf16[512,1024]{1,0:T(8,128)(2,1)}, u32[]{:S(2)}, u32[]{:S(2)}) collective-permute-start(bf16[512,1024]{1,0:T(8,128)(2,1)S(1)} %get-tuple-element.156), channel_id=1, source_target_pairs={{0,4},{4,0},{1,5},{5,1},{2,6},{6,2},{3,7},{7,3},{8,12},{12,8},{9,1... | collective-permute-start | bytes 3145736 | tf_op jit(solution)/shard_map/ppermute | solution.py:58
  499.4 61.9 %collective-permute-start.33 = (bf16[512,1024]{1,0:T(8,128)(2,1)}, bf16[512,1024]{1,0:T(8,128)(2,1)}, u32[]{:S(2)}, u32[]{:S(2)}) collective-permute-start(bf16[512,1024]{1,0:T(8,128)(2,1)} %get-tuple-element.155), channel_id=1, source_target_pairs={{0,4},{4,0},{1,5},{5,1},{2,6},{6,2},{3,7},{7,3},{8,12},{12,8},{9,1... | collective-permute-start | bytes 3145736 | tf_op jit(solution)/shard_map/ppermute | solution.py:58
  535.7 25.1 %collective-permute-start.32 = (bf16[512,1024]{1,0:T(8,128)(2,1)S(1)}, bf16[512,1024]{1,0:T(8,128)(2,1)S(1)}, u32[]{:S(2)}, u32[]{:S(2)}) collective-permute-start(bf16[512,1024]{1,0:T(8,128)(2,1)S(1)} %dynamic-slice_convert_fusion.1), channel_id=1, source_target_pairs={{0,1},{1,0},{2,3},{3,2},{4,5},{5,4},{6,7},{7,6},{8,9},{9,8},{10,11... | collective-permute-start | bytes 3145736 | tf_op jit(solution)/shard_map/ppermute | solution.py:58
  539.8 21.5 %collective-permute-start.34 = (bf16[4,2,64,1024]{3,2,1,0:T(8,128)(2,1)S(1)}, bf16[4,2,64,1024]{3,2,1,0:T(8,128)(2,1)S(1)}, u32[]{:S(2)}, u32[]{:S(2)}) collective-permute-start(bf16[4,2,64,1024]{3,2,1,0:T(8,128)(2,1)S(1)} %fusion.29), channel_id=1, source_target_pairs={{0,2},{2,0},{1,3},{3,1},{4,6},{6,4},{5,7},{7,5},{8,10},{10,8},{9,1... | collective-permute-start | bytes 3145736 | tf_op jit(solution)/shard_map/ppermute | solution.py:58
  564.6 20.3 %collective-permute-start.38 = (bf16[4,64,1024]{2,1,0:T(8,128)(2,1)}, bf16[4,64,1024]{2,1,0:T(8,128)(2,1)}, u32[]{:S(2)}, u32[]{:S(2)}) collective-permute-start(bf16[4,64,1024]{2,1,0:T(8,128)(2,1)} %fusion.47), channel_id=1, source_target_pairs={{0,4},{4,0},{1,5},{5,1},{2,6},{6,2},{3,7},{7,3},{8,12},{12,8},{9,1... | collective-permute-start | bytes 1572872 | tf_op jit(solution)/shard_map/ppermute | solution.py:58
  566.1 18.8 %collective-permute-start.39 = (bf16[4,64,512]{2,1,0:T(8,128)(2,1)}, bf16[4,64,512]{2,1,0:T(8,128)(2,1)}, u32[]{:S(2)}, u32[]{:S(2)}) collective-permute-start(bf16[4,64,512]{2,1,0:T(8,128)(2,1)} %fusion.52), channel_id=1, source_target_pairs={{0,4},{4,0},{1,5},{5,1},{2,6},{6,2},{3,7},{7,3},{8,12},{12,8},{9,1... | collective-permute-start | bytes 786440 | tf_op jit(solution)/shard_map/ppermute | solution.py:58
  589.7 18.4 %collective-permute-start.42 = (bf16[2,64,1536]{2,1,0:T(8,128)(2,1)}, bf16[2,64,1536]{2,1,0:T(8,128)(2,1)}, u32[]{:S(2)}, u32[]{:S(2)}) collective-permute-start(bf16[2,64,1536]{2,1,0:T(8,128)(2,1)} %fusion.50), channel_id=1, source_target_pairs={{0,16},{8,24},{16,0},{24,8},{1,17},{9,25},{17,1},{25,9},{2,18},{10... | collective-permute-start | bytes 1179656 | tf_op jit(solution)/shard_map/ppermute | solution.py:649
  593.3 26.5 %collective-permute-start.41 = (bf16[512,1024]{1,0:T(8,128)(2,1)}, bf16[512,1024]{1,0:T(8,128)(2,1)}, u32[]{:S(2)}, u32[]{:S(2)}) collective-permute-start(bf16[512,1024]{1,0:T(8,128)(2,1)} %fusion.15), channel_id=1, source_target_pairs={{0,1},{1,0},{2,3},{3,2},{4,5},{5,4},{6,7},{7,6},{8,9},{9,8},{10,11... | collective-permute-start | bytes 3145736 | tf_op jit(solution)/shard_map/ppermute | solution.py:58
  631.9 19.4 %collective-permute-start.46 = (bf16[2,2,96,1024]{3,2,1,0:T(8,128)(2,1)S(1)}, bf16[2,2,96,1024]{3,2,1,0:T(8,128)(2,1)S(1)}, u32[]{:S(2)}, u32[]{:S(2)}) collective-permute-start(bf16[2,2,96,1024]{3,2,1,0:T(8,128)(2,1)S(1)} %fusion.39), channel_id=1, source_target_pairs={{0,4},{4,0},{1,5},{5,1},{2,6},{6,2},{3,7},{7,3},{8,12},{12,8},{9,1... | collective-permute-start | bytes 2359304 | tf_op jit(solution)/shard_map/ppermute | solution.py:58
  (72 other events, 702.4 us)
Sparse Core Ops, SparseCore 0:
  11.0 57.9 all-gather.5
  77.8 115.5 all-gather.9
  195.0 113.5 all-gather.7
  310.7 108.9 reduce-scatter.2
  443.6 108.1 reduce-scatter.4

commit v4 on v3

--- a/solution.py
+++ b/solution.py
@@ -109,32 +109,42 @@
     return jnp.stack([own, across, swap(own, "core"), swap(across, "core")])
 
 
-def add_core(parts):
-    given = swap(parts[2:], "core")
-    return (parts[:2].astype(f32) + given.astype(f32)).astype(bf16)
-
-
-def scatter_group(pair, tensor_size):
-    own, across = pair[0].astype(f32), pair[1].astype(f32)
+def add(keep, given):
+    return keep.astype(f32) + given.astype(f32)
+
+
+def piece(near, given, sequence, which, rows):
+    return add(
+        lax.dynamic_slice_in_dim(near[sequence], which * rows, rows, 0),
+        lax.dynamic_slice_in_dim(given[sequence], which * rows, rows, 0),
+    )
+
+
+def scatter_group(near, given, tensor_size):
     if tensor_size != 2:
+        own, across = add(near[0], given[0]), add(near[1], given[1])
         own = own + swap(across.astype(bf16), "y").astype(f32)
         return scatter_rows(own, tensor_size)
     me = lax.axis_index("tensor")
-    rows = own.shape[0] // 2
+    rows = near.shape[1] // 2
     half = rows // 2
-
-    def take(values, which):
-        return lax.dynamic_slice_in_dim(values, which * rows, rows, 0)
-
-    mine, by_tensor = take(own, me), take(own, 1 - me)
-    by_y, corner = take(across, me), take(across, 1 - me).astype(bf16)
-    low, high = together(swap(corner[:half], "tensor"), swap(corner[half:], "y"))
-    by_y = jnp.concatenate([by_y[:half] + low.astype(f32), by_y[half:]], axis=0)
-    by_tensor = jnp.concatenate([by_tensor[:half], by_tensor[half:] + high.astype(f32)], axis=0)
-    from_tensor, from_y = together(
-        swap(by_tensor.astype(bf16), "tensor"), swap(by_y.astype(bf16), "y")
-    )
-    return mine + from_tensor.astype(f32) + from_y.astype(f32)
+    take = functools.partial(piece, near, given)
+    corner = take(1, 1 - me, rows).astype(bf16)
+    low, high = swap(corner[:half], "tensor"), swap(corner[half:], "y")
+    by_tensor, by_y = take(0, 1 - me, rows), take(1, me, rows)
+    first_tensor = swap(by_tensor[:half].astype(bf16), "tensor")
+    first_y = swap(by_y[half:].astype(bf16), "y")
+    low, high = together(low, high)
+    rest_tensor = swap(add(by_tensor[half:], high).astype(bf16), "tensor")
+    rest_y = swap(add(by_y[:half], low).astype(bf16), "y")
+    first_tensor, first_y, rest_tensor, rest_y = together(
+        first_tensor, first_y, rest_tensor, rest_y
+    )
+    mine = take(0, me, rows)
+    return mine + add(
+        jnp.concatenate([first_tensor, rest_tensor], axis=0),
+        jnp.concatenate([rest_y, first_y], axis=0),
+    )
 
 
 def rope_lanes(values, cosine, sine, first, direction):
@@ -287,14 +297,27 @@
 
 
 def expert_kernel(
-    carried, shared, member_ref, tokens_ref, grad_ref, code_ref, gate_ref, weight_ref, *refs
+    carried, shared, last, member_ref, tokens_ref, grad_ref, code_ref, gate_ref, weight_ref, *refs
 ):
     if carried:
         moe_in, normed_in, *refs = refs
     if shared:
         refs = refs[1:]
-    moe_ref, normed_ref, pair_ref, part_ref, both, down, both_acc, down_acc = refs
+    *sum_refs, pair_ref, part_ref, both, down, both_acc, down_acc = refs
     step = pl.program_id(0)
+
+    def put(place, values):
+        if not last:
+            sum_refs[place][0] = values
+            return
+
+        @pl.when(step < 2)
+        def _():
+            sum_refs[2 * place][0] = values
+
+        @pl.when(step >= 2)
+        def _():
+            sum_refs[2 * place + 1][0] = values
     shards_z, members, rows = weight_ref.shape[0], weight_ref.shape[2], weight_ref.shape[3]
     hidden = down.shape[0]
     both_rows = both.shape[0] // (shards_z * members)
@@ -335,7 +358,7 @@
     moe = contract(dispatch, weighted, 0, 0)
     if carried:
         moe = moe + moe_in[0].astype(f32)
-    moe_ref[0] = moe.astype(bf16)
+    put(0, moe.astype(bf16))
 
     slot_grad = jnp.dot(dispatch, grad_ref[0], preferred_element_type=f32)
     raw_grad = contract(slot_grad.astype(bf16), down[...], 1, 1)
@@ -355,7 +378,7 @@
     normed = contract(dispatch, in_grad, 0, 0)
     if carried:
         normed = normed + normed_in[0].astype(f32)
-    normed_ref[0] = normed.astype(bf16)
+    put(1, normed.astype(bf16))
 
     @pl.when(step == pl.num_programs(0) - 1)
     def _():
@@ -364,18 +387,27 @@
             part_ref[z, 0, rel, both_rows:, :] = down_acc[down_at, :].astype(bf16)
 
 
-def run_expert(member, tokens, grads, code, gate, weight, place, carry, shared):
+def run_expert(
+    member, tokens, grads, code, gate, weight, source, bunch, place, last, carry, shared
+):
     sequences, seq_len, width = tokens.shape
-    shards_z, bunch, members, rows, both_width = weight.shape
+    shards_z, held, members, rows, both_width = weight.shape
     hidden = both_width // 2
     per_seq = pl.BlockSpec((1, seq_len, width), lambda s: (s, 0, 0))
     per_row = pl.BlockSpec((1, 1, seq_len), lambda s: (s, 0, 0))
     one = (shards_z, 1, members, rows, both_width)
-    every = pl.BlockSpec(one, lambda s: (0, place, 0, 0, 0), pipeline_mode=pl.Buffered(1))
+    every = pl.BlockSpec(one, lambda s: (0, source, 0, 0, 0), pipeline_mode=pl.Buffered(1))
     part = pl.BlockSpec(one, lambda s: (0, place, 0, 0, 0))
     slots = sequences * CAP
+    if last:
+        near = pl.BlockSpec((1, seq_len, width), lambda s: (jnp.minimum(s, 1), 0, 0))
+        far = pl.BlockSpec((1, seq_len, width), lambda s: (jnp.maximum(s - 2, 0), 0, 0))
+        sums = [near, far, near, far]
+        sum_shapes = [jax.ShapeDtypeStruct((2, seq_len, width), bf16)] * 4
+    else:
+        sums, sum_shapes = [per_seq] * 2, [jax.ShapeDtypeStruct(tokens.shape, bf16)] * 2
     return pl.pallas_call(
-        functools.partial(expert_kernel, bool(carry), bool(shared)),
+        functools.partial(expert_kernel, bool(carry), bool(shared), last),
         grid=(sequences,),
         in_specs=[
             pl.BlockSpec(memory_space=pltpu.SMEM),
@@ -387,12 +419,11 @@
         ]
         + [per_seq] * len(carry)
         + [pl.BlockSpec(memory_space=pl.ANY)] * len(shared),
-        out_specs=[per_seq, per_seq, per_row, part],
-        out_shape=[
-            jax.ShapeDtypeStruct(tokens.shape, bf16),
-            jax.ShapeDtypeStruct(tokens.shape, bf16),
+        out_specs=sums + [per_row, part],
+        out_shape=sum_shapes
+        + [
             jax.ShapeDtypeStruct((sequences, 1, seq_len), f32),
-            jax.ShapeDtypeStruct(weight.shape, bf16),
+            jax.ShapeDtypeStruct((shards_z, bunch, members, rows, both_width), bf16),
         ],
         scratch_shapes=[
             pltpu.VMEM((width, both_width), bf16),
@@ -403,11 +434,11 @@
         compiler_params=pltpu.CompilerParams(vmem_limit_bytes=66_000_000),
         cost_estimate=pl.CostEstimate(
             flops=2 * slots * width * (4 * seq_len + 9 * hidden),
-            bytes_accessed=12 * sequences * seq_len * width + 4 * (weight.size // bunch),
+            bytes_accessed=12 * sequences * seq_len * width + 4 * (weight.size // held),
             transcendentals=slots * hidden,
         ),
         name="expert",
-        input_output_aliases={6 + len(carry): 3} if shared else {},
+        input_output_aliases={6 + len(carry): len(sums) + 1} if shared else {},
     )(member, tokens, grads, code, gate, weight, *carry, *shared)
 
 
@@ -481,18 +512,6 @@
         axis=1,
     )
     moe_own = gather_rows(moe_rows, tensor_size)
-    packed_full, attn_tokens, moe_own, members = together(
-        packed_full, attn_tokens, moe_own, members
-    )
-    qkv_full, out_full = packed_full[:, :wide], packed_full[:, wide:]
-    bunch = min(2, owned)
-    weights = []
-    for e in range(0, owned, bunch):
-        item = members[e : e + bunch]
-        if weights:
-            item = after(item, launched)
-        launched = item
-        weights.append(lax.all_gather(item, "z", axis=0, tiled=False))
 
     ids_t = expert_ids.T
     hits = jnp.zeros((expert_count, seq_len), jnp.bool_)
@@ -502,8 +521,6 @@
     earlier = (token_ids[:, None] < token_ids[None, :]).astype(bf16)
     rank = jnp.dot(hits.astype(bf16), earlier, preferred_element_type=f32)
     code = jnp.where(hits, jnp.where(rank < CAP, rank, -1.0), -2.0)
-    code_y = swap(code, "y")
-    codes = jnp.stack([code, code_y, swap(code, "core"), swap(code_y, "core")])
 
     half_dim = HEAD // 2
     frequency = rope_base ** (-(jnp.arange(half_dim, dtype=f32) * 2.0 / HEAD))
@@ -511,12 +528,27 @@
     cosine = jnp.tile(jnp.cos(angles), (1, 4))
     sine = jnp.tile(jnp.concatenate([-jnp.sin(angles), jnp.sin(angles)], axis=1), (1, 2))
 
+    packed_full, attn_tokens, moe_own, members, code, cosine, sine = together(
+        packed_full, attn_tokens, moe_own, members, code, cosine, sine
+    )
+    qkv_full, out_full = packed_full[:, :wide], packed_full[:, wide:]
+    bunch = min(2, owned)
+    weights, launched = [], None
+    for start, stop in [(0, bunch)] + [(e, e + 1) for e in range(bunch, owned)]:
+        item = members[start:stop]
+        if launched is not None:
+            item = after(item, launched)
+        launched = item
+        item = lax.all_gather(item, "z", axis=0, tiled=False)
+        weights += [(item, e) for e in range(stop - start)]
+
     qkv_pre = jnp.dot(attn_tokens, qkv_full, preferred_element_type=f32)
-    qkv_pre, moe_own, codes = together(qkv_pre, moe_own, codes)
+    qkv_pre, moe_own, code_y = together(qkv_pre, moe_own, swap(code, "y"))
     moe_across = swap(moe_own, "y")
     attn_mixed, qkv_rot, log_totals = attention_forward(qkv_pre, cosine, sine)
     attn_out = scatter_rows(contract(attn_mixed, out_full, 1, 1), tensor_size)
-    attn_out, moe_across = lax.optimization_barrier((attn_out, moe_across))
+    codes = jnp.stack([code, code_y, swap(code, "core"), swap(code_y, "core")])
+    attn_out, moe_across, codes = together(attn_out, moe_across, codes)
     moe_grad = jnp.stack([moe_own, moe_across, swap(moe_own, "core"), swap(moe_across, "core")])
     hidden_state = input_rows + residual_scale * attn_out
     ffn_normed = (hidden_state * row_scale(hidden_state) * ffn_gain).astype(bf16)
@@ -540,8 +572,10 @@
             moe_grad,
             code_own[:, e : e + 1],
             gate_own[:, e : e + 1],
-            weights[e // bunch],
+            *weights[e],
+            bunch,
             e % bunch,
+            e + 1 == owned,
             carry,
             shared,
         )
@@ -550,7 +584,7 @@
         if (e + 1) % bunch == 0:
             parts.append(lax.psum_scatter(part, "z", scatter_dimension=0, tiled=False))
             shared = ()
-    moe_parts, normed_parts = carry
+    moe_near, moe_give, normed_near, normed_give = carry
 
     pair_grad = jnp.concatenate(pairs, axis=1)
     pair_core = stacked(pair_grad[:2], swap(pair_grad[2:], "core"), core_first)
@@ -565,8 +599,8 @@
         local = seq_len // tensor_size
         pair_all = lax.all_gather(pair_y, "tensor", axis=0, tiled=True)
         pair_all = lax.dynamic_slice_in_dim(pair_all, my_tensor * local, local, 1)
-    normed_pair, pair_all = together(add_core(normed_parts), pair_all)
-    normed_local = scatter_group(normed_pair, tensor_size)
+    normed_given, pair_all = together(swap(normed_give, "core"), pair_all)
+    normed_local = scatter_group(normed_near, normed_given, tensor_size)
 
     def core_owners(part):
         part = jnp.moveaxis(part.reshape(bunch, 2, 2, rows, both_width), 2, 0)
@@ -577,7 +611,8 @@
         return stacked(keep, swap(give, "y"), y_first, 0)
 
     early = parts[:-1]
-    normed_local, *early = together(normed_local, *[core_owners(part) for part in early])
+    moe_given = swap(after(moe_give, normed_given), "core")
+    normed_local, moe_given = together(normed_local, moe_given)
     gates_local = lax.dynamic_slice_in_dim(gates[0], my_tensor * local, local, 1)
     gate_dot = jnp.sum(gates_local * pair_all, axis=0, keepdims=True)
     logit_low = (gates_local * (pair_all - gate_dot)).astype(bf16)
@@ -587,16 +622,19 @@
     state_grad, ffn_gain_part = norm_backward(normed_local, hidden_state, ffn_gain)
     state_grad = state_grad + grad_rows
     attn_grad_all = gather_rows((residual_scale * state_grad).astype(bf16), tensor_size)
-    moe_pair = add_core(after(moe_parts, normed_pair))
-    owners = [y_owners(part) for part in early]
-    attn_grad_all, moe_pair, *owners = together(attn_grad_all, moe_pair, *owners)
     if tensor_size == 2:
         local = seq_len // 2
-        moe_far = lax.dynamic_slice_in_dim(moe_pair[1], (1 - my_tensor) * local, local, 0)
-        moe_near = lax.dynamic_slice_in_dim(moe_pair[1], my_tensor * local, local, 0)
+        moe_piece = functools.partial(piece, moe_near, moe_given)
+        moe_far = moe_piece(1, 1 - my_tensor, local).astype(bf16)
+        moe_own_far = moe_piece(1, my_tensor, local).astype(bf16)
     else:
-        moe_far, moe_near = moe_pair[1], jnp.zeros((1, width), bf16)
-    moe_far = swap(moe_far, "y")
+        moe_far = add(moe_near[1], moe_given[1]).astype(bf16)
+        moe_own_far = jnp.zeros((1, width), bf16)
+    attn_grad_all, moe_far, moe_own_far = together(
+        attn_grad_all, swap(moe_far, "y"), moe_own_far
+    )
+    early = [core_owners(after(part, attn_grad_all)) for part in early]
+    moe_own_far = swap(moe_own_far, "y")
 
     def halves(part, mine):
         return at(part, mine), at(part, 1 - mine).astype(bf16)
@@ -604,23 +642,22 @@
     def by_dp(part):
         return part.reshape(z_size, 2, 2, shard_rows, part.shape[1])
 
-    def add(keep, given):
-        return keep.astype(f32) + given.astype(f32)
-
-    out_part = contract(attn_grad_all, attn_mixed, 0, 0)
-    out_keep, out_give = halves(jnp.moveaxis(by_dp(out_part), 2, 0), my_core)
-    out_given = swap(out_give, "core")
     mixed_grad = jnp.dot(attn_grad_all, out_full, preferred_element_type=f32).astype(bf16)
     qkv_pre_grad = attention_backward(qkv_rot, mixed_grad, log_totals, cosine, sine)
-    qkv_pre_grad, moe_far, out_given = together(qkv_pre_grad, moe_far, out_given)
-
-    out_keep, out_give = halves(jnp.moveaxis(add(out_keep, out_given), 1, 0), my_y)
+    qkv_pre_grad, moe_own_far = together(qkv_pre_grad, moe_own_far)
+
     attn_part = contract(qkv_pre_grad, qkv_full, 1, 1)
     attn_scattered = scatter_rows(attn_part, tensor_size)
-    qkv_part = contract(attn_tokens, qkv_pre_grad, 0, 0)
+    tokens_late, grads_late, _ = together(attn_tokens, attn_grad_all, attn_part)
+    qkv_part = contract(tokens_late, qkv_pre_grad, 0, 0)
     qkv_keep, qkv_give = halves(jnp.moveaxis(by_dp(qkv_part), 2, 0), my_core)
-    attn_normed_grad, moe_near, qkv_given = together(
-        attn_scattered, swap(moe_near, "y"), swap(qkv_give, "core")
+    out_part = contract(grads_late, attn_mixed, 0, 0)
+    out_keep, out_give = halves(jnp.moveaxis(by_dp(out_part), 2, 0), my_core)
+    attn_normed_grad, qkv_given, out_given, *owners = together(
+        attn_scattered,
+        swap(qkv_give, "core"),
+        swap(out_give, "core"),
+        *[y_owners(part) for part in early],
     )
     input_part, attn_gain_part = norm_backward(attn_normed_grad, input_rows, attn_gain)
     input_grad = (state_grad + input_part).astype(bf16)
@@ -628,35 +665,36 @@
         [router_part, ffn_gain_part[None, :], attn_gain_part[None, :]], axis=0
     )
     if tensor_size == 2:
-        moe_give = lax.dynamic_slice_in_dim(moe_pair[0], (1 - my_tensor) * local, local, 0)
-        moe_keep = lax.dynamic_slice_in_dim(moe_pair[0], my_tensor * local, local, 0)
-        moe_sum = add(moe_keep, moe_near)
-        moe_given = swap(add(moe_give, moe_far).astype(bf16), "tensor")
+        moe_sum = add(moe_piece(0, my_tensor, local), moe_own_far)
+        moe_given = swap(
+            add(moe_piece(0, 1 - my_tensor, local), moe_far).astype(bf16), "tensor"
+        )
     else:
         moe_sum = jnp.zeros((local, width), f32)
-        moe_given = scatter_rows(add(moe_pair[0], moe_far), tensor_size)
+        moe_given = scatter_rows(add(add(moe_near[0], moe_given[0]), moe_far), tensor_size)
     qkv_keep, qkv_give = halves(jnp.moveaxis(add(qkv_keep, qkv_given), 1, 0), my_y)
+    out_keep, out_give = halves(jnp.moveaxis(add(out_keep, out_given), 1, 0), my_y)
     small = butterfly_sum(small, (("core", 2), ("z", z_size)))
-    small, qkv_given, out_given = together(small, swap(qkv_give, "y"), swap(out_give, "y"))
-
-    def z_scatter(part):
-        step = z_size // 2
-        while step:
-            keep, give = halves(
-                part.reshape(2, -1, shard_rows, part.shape[-1]), (my_z // step) % 2
-            )
-            pairs = [(i, i ^ step) for i in range(z_size)]
-            part = add(keep, lax.ppermute(give, "z", pairs))
-            step //= 2
-        return part.reshape(shard_rows, part.shape[-1])
-
-    dp_part = jnp.concatenate([add(qkv_keep, qkv_given), add(out_keep, out_given)], axis=-1)
-    dp_sum = z_scatter(dp_part)
-    small, moe_given, dp_sum = together(butterfly_sum(small, (("y", 2),)), moe_given, dp_sum)
+    late = core_owners(after(parts[-1], attn_normed_grad))
+    small, qkv_given, out_given, moe_given, late = together(
+        small, swap(qkv_give, "y"), swap(out_give, "y"), moe_given, late
+    )
+    dp_sum = jnp.concatenate([add(qkv_keep, qkv_given), add(out_keep, out_given)], axis=-1)
+    step = 1
+    while step < z_size:
+        keep, give = halves(
+            jnp.moveaxis(dp_sum.reshape(-1, 2, shard_rows, dp_sum.shape[-1]), 1, 0),
+            (my_z // step) % 2,
+        )
+        dp_sum = add(keep, lax.ppermute(give, "z", [(i, i ^ step) for i in range(z_size)]))
+        step *= 2
+    dp_sum = dp_sum.reshape(shard_rows, dp_sum.shape[-1])
+    late = y_owners(late)
+    small, dp_sum = together(butterfly_sum(small, (("y", 2),)), dp_sum)
     qkv_sum, out_sum = dp_sum[:, :wide], dp_sum[:, wide:]
     block_output = (hidden_state + residual_scale * add(moe_sum, moe_given)).astype(bf16)
     small = butterfly_sum(small, (("tensor", tensor_size),))
-    owners.append(y_owners(core_owners(after(parts[-1], dp_sum))))
+    owners.append(late)
     summed = jnp.concatenate(owners, axis=2)
     summed = summed.reshape(experts_local, rows, both_width)
     both_rows = gate_weight.shape[1]

time: 668 us -> 621 us (0.930)
  waiting for transfers between devices: 235 us -> 206 us
  other arithmetic: 89 us -> 63.2 us
  local copies, waits for them, and re-layouts: 62 us -> 44.2 us
  starting transfers between devices: 31.9 us -> 47.9 us
    ppermute x40 -> x42, waiting for transfers between devices: 191 us -> 171 us  [swap(): return lax.ppermute(values, axis, [(0, 1), (1, 0)])]
    ppermute x2, waiting for transfers between devices: 14.6 us -> 4.3 us  [shards(): lax.ppermute(give, 'z', [(i, i ^ step) for i in range(z_size)])]
    all_gather x2 -> x3, waiting for transfers between devices: 10.2 us -> 0.04 us  [shards(): item = lax.all_gather(item, 'z', axis=0, tiled=False)]
    reduce_scatter x2, waiting for transfers between devices: 0.01 us -> 9.48 us  [shards(): parts.append(lax.psum_scatter(part, 'z', scatter_dimension=0, tiled=False))]
    convert_element_type x4 -> x6, other arithmetic: 17.4 us -> 9.02 us  [the longest x1 3.57 us: shards(): (hidden_state + residual_scale * add(moe_sum, moe_given)).astype(bf16)]
    ppermute x40 -> x42, starting transfers between devices: 28.9 us -> 35.6 us  [swap(): return lax.ppermute(values, axis, [(0, 1), (1, 0)])]
    unnamed x105 -> x103, local copies, waits for them, and re-layouts: 15.5 us -> 13.5 us
    slice x7 -> x6, local copies, waits for them, and re-layouts: 15.6 us -> 13.8 us  [the longest x1 5.26 us: piece(): near[sequence]]
  transfers between devices with their start and end apart: 52 -> 55, of which waited for: 29 -> 30; matrix products, arithmetic and copies ran while one was open for 22% -> 18% of each run, Pallas kernels for 31% -> 34%
where the time goes in v4:
time: 621 us; the launch traced here: 616 us
  Pallas kernels  209 us (34%)
  waiting for transfers between devices  206 us (33%)
  other arithmetic  63.2 us (10%)
  starting transfers between devices  47.9 us (8%)
  local copies, waits for them, and re-layouts  44.2 us (7%)
  matrix products  30.1 us (5%)
  between operations  15.6 us (3%)
    ppermute x42, waiting for transfers between devices, swap(): return lax.ppermute(values, axis, [(0, 1), (1, 0)])  171 us
    pallas_call x4, Pallas kernels, run_expert(): pl.pallas_call(functools.partial(expert_kernel, bool(carry), bool(shared)...  165 us
    ppermute x42, starting transfers between devices, swap(): return lax.ppermute(values, axis, [(0, 1), (1, 0)])  35.6 us
    pallas_call x1, Pallas kernels, attention_backward(): pl.pallas_call(attention_backward_kernel, grid=(groups,), in_specs=[wide,...  26.5 us
    ppermute x5, waiting for transfers between devices, butterfly_sum(): lax.ppermute(values, axis, [(i, i ^ step) for i in range(size)])  21.2 us
    pallas_call x1, Pallas kernels, attention_forward(): pl.pallas_call(attention_forward_kernel, grid=(groups,), in_specs=[wide,...  17.6 us
    dot_general x5, matrix products, contract(): lax.dot_general(left, right, (((left_dim,), (right_dim,)), ((), ())), pre...  15.6 us
    unnamed x103, local copies, waits for them, and re-layouts  13.5 us
  transfers between devices with their start and end apart: 55, of which 30 were waited for; matrix products, arithmetic and copies ran while one was open for 18% of the time, Pallas kernels for 34%

profile of v4, /device:TPU:0, one launch (start us, length us, event | category | flops | bytes accessed | tf_op | source)
XLA Modules:
  0.0 615.8 jit_solution(14151157940013874588)
XLA Ops:
  25.3 14.9 %collective-permute-done = bf16[512,1024]{1,0:T(8,128)(2,1)} collective-permute-done((bf16[512,1024]{1,0:T(8,128)(2,1)}, bf16[512,1024]{1,0:T(8,128)(2,1)}, u32[]{:S(2)}, u32[]{:S(2)}) %collective-permute-start) | collective-permute-done | bytes 1048608 | tf_op jit(solution)/shard_map/ppermute | solution.py:58
  45.8 22.0 %collective-permute-done.3 = bf16[2,4,96,1024]{3,2,1,0:T(8,128)(2,1)} collective-permute-done((bf16[2,4,96,1024]{3,2,1,0:T(8,128)(2,1)}, bf16[2,4,96,1024]{3,2,1,0:T(8,128)(2,1)}, u32[]{:S(2)}, u32[]{:S(2)}) %collective-permute-start.3) | collective-permute-done | bytes 1572896 | tf_op jit(solution)/shard_map/ppermute | solution.py:58
  78.9 6.6 %fusion.22.pre_ref = f32[1024,1024]{1,0:T(8,128)} fusion(bf16[1024,1024]{1,0:T(8,128)(2,1)} %pad_maximum_fusion.4, bf16[1024,1536]{1,0:T(8,128)(2,1)} %all-gather.8.cloned.1.call-done), kind=kOutput, calls=%fused_computation.57 | convolution fusion | flops 2147483648 | bytes 8388608 | tf_op jit(solution)/shard_map/dot_general | solution.py:545
  88.4 17.6 %attention_forward.1 = (bf16[1024,512]{1,0:T(8,128)(2,1)}, bf16[1024,1024]{1,0:T(8,128)(2,1)}, f32[1024,512]{1,0:T(8,128)}) custom-call(f32[1024,1024]{1,0:T(8,128)} %fusion.22.pre_ref, f32[1024,128]{1,0:T(8,128)} %copy.56.cos_ref, f32[1024,128]{1,0:T(8,128)} %copy.57.sin_ref), custom_call_target="tpu_custom_call" | custom-call | flops 3221225472 | bytes 10485760 | tf_op jit(solution)/shard_map/attention_forward/pallas_call | solution.py:259
  113.7 22.5 %collective-permute-done.6 = bf16[512,1024]{1,0:T(8,128)(2,1)} collective-permute-done((bf16[512,1024]{1,0:T(8,128)(2,1)S(1)}, bf16[512,1024]{1,0:T(8,128)(2,1)}, u32[]{:S(2)}, u32[]{:S(2)}) %collective-permute-start.6) | collective-permute-done | bytes 1048608 | tf_op jit(solution)/shard_map/ppermute | solution.py:58
  143.0 7.2 %pad_maximum_fusion.grad_ref = bf16[4,1024,1024]{2,1,0:T(8,128)(2,1)} fusion(bf16[1,1024,1024]{2,1,0:T(8,128)(2,1)} %bitcast.28, bf16[1,1024,1024]{2,1,0:T(8,128)(2,1)} %bitcast.27, bf16[1,1024,1024]{2,1,0:T(8,128)(2,1)} %bitcast.26, bf16[1,1024,1024]{2,1,0:T(8,128)(2,1)} %bitcast.25), kind=kLoop, calls=%fused_computation.1 | loop fusion | flops 12582912 | bytes 16777216 | tf_op jit(solution)/shard_map/stack | solution.py:552
  150.2 16.3 %collective-permute-done.10 = bf16[512,1024]{1,0:T(8,128)(2,1)S(1)} collective-permute-done((bf16[512,1024]{1,0:T(8,128)(2,1)S(1)}, bf16[512,1024]{1,0:T(8,128)(2,1)S(1)}, u32[]{:S(2)}, u32[]{:S(2)}) %collective-permute-start.10) | collective-permute-done | bytes 1048608 | tf_op jit(solution)/shard_map/ppermute | solution.py:58
  170.6 11.5 %collective-permute-done.14 = bf16[256,1024]{1,0:T(8,128)(2,1)S(1)} collective-permute-done((bf16[256,1024]{1,0:T(8,128)(2,1)S(1)}, bf16[256,1024]{1,0:T(8,128)(2,1)S(1)}, u32[]{:S(2)}, u32[]{:S(2)}) %collective-permute-start.14) | collective-permute-done | bytes 524320 | tf_op jit(solution)/shard_map/ppermute | solution.py:58
  188.6 3.5 collective-permute-done.17
  192.1 3.8 pad_maximum_fusion.1.tokens_ref
  201.3 39.1 %expert.4 = (bf16[4,1024,1024]{2,1,0:T(8,128)(2,1)}, bf16[4,1024,1024]{2,1,0:T(8,128)(2,1)}, f32[4,1,1024]{2,1,0:T(1,128)}, bf16[4,2,4,96,1024]{4,3,2,1,0:T(8,128)(2,1)}) custom-call(s32[1]{0:T(128)} %bitcast.24.member_ref, bf16[4,1024,1024]{2,1,0:T(8,128)(2,1)} %copy-done.6, bf16[4,1024,1024]{2,1,0:T(8,128)(2,1)} %pad_maximum_fusion.grad_ref, ...), custom_call_target="tpu_custom_call" | custom-call | flops 22817013760 | bytes 56623104 | tf_op jit(solution)/shard_map/expert/pallas_call | solution.py:409
  240.3 40.3 %expert.5 = (bf16[4,1024,1024]{2,1,0:T(8,128)(2,1)}, bf16[4,1024,1024]{2,1,0:T(8,128)(2,1)}, f32[4,1,1024]{2,1,0:T(1,128)}, bf16[4,2,4,96,1024]{4,3,2,1,0:T(8,128)(2,1)}) custom-call(s32[1]{0:T(128)} %bitcast.24.member_ref, bf16[4,1024,1024]{2,1,0:T(8,128)(2,1)} %copy-done.6, ...), custom_call_target="tpu_custom_call", output_to_operand_aliasing={{3}: (8, {})} | custom-call | flops 22817013760 | bytes 56623104 | tf_op jit(solution)/shard_map/expert/pallas_call | solution.py:409
  280.7 41.1 %expert.6 = (bf16[4,1024,1024]{2,1,0:T(8,128)(2,1)}, bf16[4,1024,1024]{2,1,0:T(8,128)(2,1)}, f32[4,1,1024]{2,1,0:T(1,128)}, bf16[4,2,4,96,1024]{4,3,2,1,0:T(8,128)(2,1)}) custom-call(s32[1]{0:T(128)} %bitcast.24.member_ref, bf16[4,1024,1024]{2,1,0:T(8,128)(2,1)} %copy-done.6, bf16[4,1024,1024]{2,1,0:T(8,128)(2,1)} %pad_maximum_fusion.grad_ref, ...), custom_call_target="tpu_custom_call" | custom-call | flops 22817013760 | bytes 56623104 | tf_op jit(solution)/shard_map/expert/pallas_call | solution.py:409
  321.9 44.6 %expert.7 = (bf16[2,1024,1024]{2,1,0:T(8,128)(2,1)}, bf16[2,1024,1024]{2,1,0:T(8,128)(2,1)}, bf16[2,1024,1024]{2,1,0:T(8,128)(2,1)}, bf16[2,1024,1024]{2,1,0:T(8...) custom-call(s32[1]{0:T(128)} %bitcast.24.member_ref, ...), custom_call_target="tpu_custom_call", output_to_operand_aliasing={{5}: (8, {})} | custom-call | flops 22817013760 | bytes 56623104 | tf_op jit(solution)/shard_map/expert/pallas_call | solution.py:409
  367.9 6.1 collective-permute-done.19
  378.6 3.5 collective-permute-done.21
  382.3 5.3 fusion.80
  396.0 10.1 %collective-permute-done.24 = bf16[256,1024]{1,0:T(8,128)(2,1)S(1)} collective-permute-done((bf16[256,1024]{1,0:T(8,128)(2,1)S(1)}, bf16[256,1024]{1,0:T(8,128)(2,1)S(1)}, u32[]{:S(2)}, u32[]{:S(2)}) %collective-permute-start.24) | collective-permute-done | bytes 524320 | tf_op jit(solution)/shard_map/ppermute | solution.py:58
  409.9 7.9 %collective-permute-done.23 = bf16[256,1024]{1,0:T(8,128)(2,1)S(1)} collective-permute-done((bf16[256,1024]{1,0:T(8,128)(2,1)S(1)}, bf16[256,1024]{1,0:T(8,128)(2,1)S(1)}, u32[]{:S(2)}, u32[]{:S(2)}) %collective-permute-start.23) | collective-permute-done | bytes 524320 | tf_op jit(solution)/shard_map/ppermute | solution.py:58
  417.8 10.5 %collective-permute-done.27 = bf16[256,1024]{1,0:T(8,128)(2,1)S(1)} collective-permute-done((bf16[256,1024]{1,0:T(8,128)(2,1)S(1)}, bf16[256,1024]{1,0:T(8,128)(2,1)S(1)}, u32[]{:S(2)}, u32[]{:S(2)}) %collective-permute-start.27) | collective-permute-done | bytes 524320 | tf_op jit(solution)/shard_map/ppermute | solution.py:58
  440.7 16.4 %collective-permute-done.29 = bf16[512,1024]{1,0:T(8,128)(2,1)} collective-permute-done((bf16[512,1024]{1,0:T(8,128)(2,1)S(1)}, bf16[512,1024]{1,0:T(8,128)(2,1)}, u32[]{:S(2)}, u32[]{:S(2)}) %collective-permute-start.29) | collective-permute-done | bytes 1048608 | tf_op jit(solution)/shard_map/ppermute | solution.py:58
  458.7 3.9 collective-permute-done.30
  466.6 3.5 convolution_convert_fusion.grad_ref
  470.1 26.5 %attention_backward.1 = bf16[1024,1024]{1,0:T(8,128)(2,1)} custom-call(bf16[1024,1024]{1,0:T(8,128)(2,1)} %get-tuple-element.131.rot_ref, bf16[1024,512]{1,0:T(8,128)(2,1)} %convolution_convert_fusion.grad_ref, f32[1024,512]{1,0:T(8,128)} %get-tuple-element.135.lse_ref, f32[1024,128]{1,0:T(8,128)} %copy.56.cos_ref, f32[1024,128]{1,0:T(8,128)} %copy.57.sin_ref), custom_call_target="tpu_custom_call" | custom-call | flops 8589934592 | bytes 10485760 | tf_op jit(solution)/shard_map/attention_backward/pallas_call | solution.py:283
  496.5 6.6 %fusion.20 = f32[1024,1024]{1,0:T(8,128)} fusion(bf16[1024,1024]{1,0:T(8,128)(2,1)} %attention_backward.1, bf16[1024,1536]{1,0:T(8,128)(2,1)} %all-gather.8.cloned.1.call-done), kind=kOutput, calls=%fused_computation.55 | convolution fusion | flops 2147483648 | bytes 8388608 | tf_op jit(solution)/shard_map/dot_general | solution.py:29
  507.1 4.0 fusion.92
  517.1 13.7 %collective-permute-done.32 = bf16[512,1024]{1,0:T(8,128)(2,1)S(1)} collective-permute-done((bf16[512,1024]{1,0:T(8,128)(2,1)S(1)}, bf16[512,1024]{1,0:T(8,128)(2,1)S(1)}, u32[]{:S(2)}, u32[]{:S(2)}) %collective-permute-start.32) | collective-permute-done | bytes 1048608 | tf_op jit(solution)/shard_map/ppermute | solution.py:58
  536.3 9.5 %reduce-scatter.5.cloned.1.call-done = bf16[1,2,4,96,1024]{4,3,2,1,0:T(8,128)(2,1)} async-done(((bf16[4,2,4,96,1024]{4,3,2,1,0:T(8,128)(2,1)}), bf16[1,2,4,96,1024]{4,3,2,1,0:T(8,128)(2,1)}) %reduce-scatter.5.cloned.1.call-update) | async-done | bytes 1572880 | tf_op jit(solution)/shard_map/reduce_scatter | solution.py:585
  559.4 7.2 %collective-permute-done.39 = f32[34,1024]{1,0:T(8,128)S(1)} collective-permute-done((f32[34,1024]{1,0:T(8,128)S(1)}, f32[34,1024]{1,0:T(8,128)S(1)}, u32[]{:S(2)}, u32[]{:S(2)}) %collective-permute-start.39) | collective-permute-done | bytes 139296 | tf_op jit(solution)/shard_map/ppermute | solution.py:65
  574.3 4.3 collective-permute-done.45
  581.7 3.6 fusion.19
  585.3 9.1 %collective-permute-done.44 = f32[34,1024]{1,0:T(8,128)S(1)} collective-permute-done((f32[34,1024]{1,0:T(8,128)S(1)}, f32[34,1024]{1,0:T(8,128)S(1)}, u32[]{:S(2)}, u32[]{:S(2)}) %collective-permute-start.44) | collective-permute-done | bytes 139296 | tf_op jit(solution)/shard_map/ppermute | solution.py:65
  (325 shorter events, 157.8 us)
Async XLA Ops:
  7.2 67.4 %all-gather.8.cloned.1.call-start = ((), (), s32[]{:S(2)}) async-start(), calls=%async_computation.2 | async-start | bytes 3342336 | tf_op jit(solution)/shard_map/all_gather | solution.py:490
  10.9 190.4 %all-gather.14.cloned.1.call-start = ((), (), s32[]{:S(2)}) async-start(), calls=%async_computation.7 | async-start | bytes 7864320 | tf_op jit(solution)/shard_map/all_gather | solution.py:542
  13.7 26.4 %collective-permute-start = (bf16[512,1024]{1,0:T(8,128)(2,1)}, bf16[512,1024]{1,0:T(8,128)(2,1)}, u32[]{:S(2)}, u32[]{:S(2)}) collective-permute-start(bf16[512,1024]{1,0:T(8,128)(2,1)} %fusion.7), channel_id=1, source_target_pairs={{0,1},{1,0},{2,3},{3,2},{4,5},{5,4},{6,7},{7,6},{8,9},{9,8},{10,11... | collective-permute-start | bytes 3145736 | tf_op jit(solution)/shard_map/ppermute | solution.py:58
  21.1 46.7 %collective-permute-start.3 = (bf16[2,4,96,1024]{3,2,1,0:T(8,128)(2,1)}, bf16[2,4,96,1024]{3,2,1,0:T(8,128)(2,1)}, u32[]{:S(2)}, u32[]{:S(2)}) collective-permute-start(bf16[2,4,96,1024]{3,2,1,0:T(8,128)(2,1)} %dynamic-slice_bitcast_fusion), channel_id=1, source_target_pairs={{0,4},{4,0},{1,5},{5,1},{2,6},{6,2},{3,7},{7,3},{8,12},{12,8},{9,1... | collective-permute-start | bytes 4718600 | tf_op jit(solution)/shard_map/ppermute | solution.py:58
  25.1 46.7 %collective-permute-start.2 = (bf16[4,96,1024]{2,1,0:T(8,128)(2,1)}, bf16[4,96,1024]{2,1,0:T(8,128)(2,1)}, u32[]{:S(2)}, u32[]{:S(2)}) collective-permute-start(bf16[4,96,1024]{2,1,0:T(8,128)(2,1)} %get-tuple-element.182), channel_id=1, source_target_pairs={{0,2},{2,0},{1,3},{3,1},{4,6},{6,4},{5,7},{7,5},{8,10},{10,8},{9,1... | collective-permute-start | bytes 2359304 | tf_op jit(solution)/shard_map/ppermute | solution.py:58
  43.5 26.4 %collective-permute-start.1 = (bf16[512,1024]{1,0:T(8,128)(2,1)S(1)}, bf16[512,1024]{1,0:T(8,128)(2,1)S(1)}, u32[]{:S(2)}, u32[]{:S(2)}) collective-permute-start(bf16[512,1024]{1,0:T(8,128)(2,1)S(1)} %fusion.6), channel_id=1, source_target_pairs={{0,1},{1,0},{2,3},{3,2},{4,5},{5,4},{6,7},{7,6},{8,9},{9,8},{10,11... | collective-permute-start | bytes 3145736 | tf_op jit(solution)/shard_map/ppermute | solution.py:58
  77.4 203.3 %all-gather.12.cloned.1.call-start = ((), (), s32[]{:S(2)}) async-start(), calls=%async_computation.6 | async-start | bytes 3932160 | tf_op jit(solution)/shard_map/all_gather | solution.py:542
  87.6 50.9 %collective-permute-start.7 = (bf16[1024,1024]{1,0:T(8,128)(2,1)}, bf16[1024,1024]{1,0:T(8,128)(2,1)}, u32[]{:S(2)}, u32[]{:S(2)}) collective-permute-start(bf16[1024,1024]{1,0:T(8,128)(2,1)} %pad_maximum_fusion.5), channel_id=1, source_target_pairs={{0,4},{4,0},{1,5},{5,1},{2,6},{6,2},{3,7},{7,3},{8,12},{12,8},{9,1... | collective-permute-start | bytes 6291464 | tf_op jit(solution)/shard_map/ppermute | solution.py:58
  111.0 25.2 %collective-permute-start.6 = (bf16[512,1024]{1,0:T(8,128)(2,1)S(1)}, bf16[512,1024]{1,0:T(8,128)(2,1)}, u32[]{:S(2)}, u32[]{:S(2)}) collective-permute-start(bf16[512,1024]{1,0:T(8,128)(2,1)S(1)} %dynamic-slice_convert_fusion.1), channel_id=1, source_target_pairs={{0,1},{1,0},{2,3},{3,2},{4,5},{5,4},{6,7},{7,6},{8,9},{9,8},{10,11... | collective-permute-start | bytes 3145736 | tf_op jit(solution)/shard_map/ppermute | solution.py:58
  111.8 31.0 %collective-permute-start.12 = (bf16[1024,1024]{1,0:T(8,128)(2,1)}, bf16[1024,1024]{1,0:T(8,128)(2,1)}, u32[]{:S(2)}, u32[]{:S(2)}) collective-permute-start(bf16[1024,1024]{1,0:T(8,128)(2,1)} %pad_maximum_fusion.5), channel_id=1, source_target_pairs={{0,2},{2,0},{1,3},{3,1},{4,6},{6,4},{5,7},{7,5},{8,10},{10,8},{9,1... | collective-permute-start | bytes 6291464 | tf_op jit(solution)/shard_map/ppermute | solution.py:58
  139.9 181.9 %all-gather.10.cloned.1.call-start = ((), (), s32[]{:S(2)}) async-start(), calls=%async_computation.5 | async-start | bytes 3932160 | tf_op jit(solution)/shard_map/all_gather | solution.py:542
  140.8 25.6 %collective-permute-start.10 = (bf16[512,1024]{1,0:T(8,128)(2,1)S(1)}, bf16[512,1024]{1,0:T(8,128)(2,1)S(1)}, u32[]{:S(2)}, u32[]{:S(2)}) collective-permute-start(bf16[512,1024]{1,0:T(8,128)(2,1)S(1)} %multiply_convert_fusion.1), channel_id=1, source_target_pairs={{0,1},{1,0},{2,3},{3,2},{4,5},{5,4},{6,7},{7,6},{8,9},{9,8},{10,11... | collective-permute-start | bytes 3145736 | tf_op jit(solution)/shard_map/ppermute | solution.py:58
  141.2 25.3 %collective-permute-start.11 = (bf16[512,1024]{1,0:T(8,128)(2,1)S(1)}, bf16[512,1024]{1,0:T(8,128)(2,1)S(1)}, u32[]{:S(2)}, u32[]{:S(2)}) collective-permute-start(bf16[512,1024]{1,0:T(8,128)(2,1)S(1)} %multiply_convert_fusion.1), channel_id=1, source_target_pairs={{0,4},{4,0},{1,5},{5,1},{2,6},{6,2},{3,7},{7,3},{8,12},{12,8},{9,1... | collective-permute-start | bytes 3145736 | tf_op jit(solution)/shard_map/ppermute | solution.py:58
  187.6 315.5 %reduce-scatter.3.cloned.1.call-start = ((), (), s32[]{:S(2)}) async-start(), calls=%async_computation.3 | async-start | bytes 7864320 | tf_op jit(solution)/shard_map/reduce_scatter | solution.py:585
  280.6 265.1 %reduce-scatter.5.cloned.1.call-start = ((), (), s32[]{:S(2)}) async-start(), calls=%async_computation.4 | async-start | bytes 7864320 | tf_op jit(solution)/shard_map/reduce_scatter | solution.py:585
  382.2 47.0 %collective-permute-start.28 = (bf16[2,1024,1024]{2,1,0:T(8,128)(2,1)}, bf16[2,1024,1024]{2,1,0:T(8,128)(2,1)S(1)}, u32[]{:S(2)}, u32[]{:S(2)}) collective-permute-start(bf16[2,1024,1024]{2,1,0:T(8,128)(2,1)} %get-tuple-element.129), channel_id=1, source_target_pairs={{0,2},{2,0},{1,3},{3,1},{4,6},{6,4},{5,7},{7,5},{8,10},{10,8},{9,1... | collective-permute-start | bytes 12582920 | tf_op jit(solution)/shard_map/ppermute | solution.py:58
  393.4 24.4 %collective-permute-start.23 = (bf16[256,1024]{1,0:T(8,128)(2,1)S(1)}, bf16[256,1024]{1,0:T(8,128)(2,1)S(1)}, u32[]{:S(2)}, u32[]{:S(2)}) collective-permute-start(bf16[256,1024]{1,0:T(8,128)(2,1)S(1)} %fusion.48), channel_id=1, source_target_pairs={{0,4},{4,0},{1,5},{5,1},{2,6},{6,2},{3,7},{7,3},{8,12},{12,8},{9,1... | collective-permute-start | bytes 1572872 | tf_op jit(solution)/shard_map/ppermute | solution.py:58
  394.4 23.4 %collective-permute-start.22 = (bf16[256,1024]{1,0:T(8,128)(2,1)S(1)}, bf16[256,1024]{1,0:T(8,128)(2,1)S(1)}, u32[]{:S(2)}, u32[]{:S(2)}) collective-permute-start(bf16[256,1024]{1,0:T(8,128)(2,1)S(1)} %fusion.47), channel_id=1, source_target_pairs={{0,1},{1,0},{2,3},{3,2},{4,5},{5,4},{6,7},{7,6},{8,9},{9,8},{10,11... | collective-permute-start | bytes 1572872 | tf_op jit(solution)/shard_map/ppermute | solution.py:58
  406.7 21.5 %collective-permute-start.27 = (bf16[256,1024]{1,0:T(8,128)(2,1)S(1)}, bf16[256,1024]{1,0:T(8,128)(2,1)S(1)}, u32[]{:S(2)}, u32[]{:S(2)}) collective-permute-start(bf16[256,1024]{1,0:T(8,128)(2,1)S(1)} %fusion.32), channel_id=1, source_target_pairs={{0,4},{4,0},{1,5},{5,1},{2,6},{6,2},{3,7},{7,3},{8,12},{12,8},{9,1... | collective-permute-start | bytes 1572872 | tf_op jit(solution)/shard_map/ppermute | solution.py:58
  408.5 19.7 %collective-permute-start.26 = (bf16[256,1024]{1,0:T(8,128)(2,1)S(1)}, bf16[256,1024]{1,0:T(8,128)(2,1)S(1)}, u32[]{:S(2)}, u32[]{:S(2)}) collective-permute-start(bf16[256,1024]{1,0:T(8,128)(2,1)S(1)} %fusion.34), channel_id=1, source_target_pairs={{0,1},{1,0},{2,3},{3,2},{4,5},{5,4},{6,7},{7,6},{8,9},{9,8},{10,11... | collective-permute-start | bytes 1572872 | tf_op jit(solution)/shard_map/ppermute | solution.py:58
  432.5 24.7 %collective-permute-start.29 = (bf16[512,1024]{1,0:T(8,128)(2,1)S(1)}, bf16[512,1024]{1,0:T(8,128)(2,1)}, u32[]{:S(2)}, u32[]{:S(2)}) collective-permute-start(bf16[512,1024]{1,0:T(8,128)(2,1)S(1)} %get-tuple-element.161), channel_id=1, source_target_pairs={{0,1},{1,0},{2,3},{3,2},{4,5},{5,4},{6,7},{7,6},{8,9},{9,8},{10,11... | collective-permute-start | bytes 3145736 | tf_op jit(solution)/shard_map/ppermute | solution.py:58
  438.1 24.5 %collective-permute-start.30 = (bf16[512,1024]{1,0:T(8,128)(2,1)}, bf16[512,1024]{1,0:T(8,128)(2,1)}, u32[]{:S(2)}, u32[]{:S(2)}) collective-permute-start(bf16[512,1024]{1,0:T(8,128)(2,1)} %get-tuple-element.170), channel_id=1, source_target_pairs={{0,4},{4,0},{1,5},{5,1},{2,6},{6,2},{3,7},{7,3},{8,12},{12,8},{9,1... | collective-permute-start | bytes 3145736 | tf_op jit(solution)/shard_map/ppermute | solution.py:58
  462.6 33.9 %collective-permute-start.31 = (bf16[512,1024]{1,0:T(8,128)(2,1)}, bf16[512,1024]{1,0:T(8,128)(2,1)}, u32[]{:S(2)}, u32[]{:S(2)}) collective-permute-start(bf16[512,1024]{1,0:T(8,128)(2,1)} %get-tuple-element.136), channel_id=1, source_target_pairs={{0,4},{4,0},{1,5},{5,1},{2,6},{6,2},{3,7},{7,3},{8,12},{12,8},{9,1... | collective-permute-start | bytes 3145736 | tf_op jit(solution)/shard_map/ppermute | solution.py:58
  465.5 101.5 %collective-permute-start.42 = (bf16[512,1024]{1,0:T(8,128)(2,1)S(1)}, bf16[512,1024]{1,0:T(8,128)(2,1)}, u32[]{:S(2)}, u32[]{:S(2)}) collective-permute-start(bf16[512,1024]{1,0:T(8,128)(2,1)S(1)} %fusion.15), channel_id=1, source_target_pairs={{0,1},{1,0},{2,3},{3,2},{4,5},{5,4},{6,7},{7,6},{8,9},{9,8},{10,11... | collective-permute-start | bytes 3145736 | tf_op jit(solution)/shard_map/ppermute | solution.py:58
  506.0 24.9 %collective-permute-start.32 = (bf16[512,1024]{1,0:T(8,128)(2,1)S(1)}, bf16[512,1024]{1,0:T(8,128)(2,1)S(1)}, u32[]{:S(2)}, u32[]{:S(2)}) collective-permute-start(bf16[512,1024]{1,0:T(8,128)(2,1)S(1)} %dynamic-slice_convert_fusion), channel_id=1, source_target_pairs={{0,1},{1,0},{2,3},{3,2},{4,5},{5,4},{6,7},{7,6},{8,9},{9,8},{10,11... | collective-permute-start | bytes 3145736 | tf_op jit(solution)/shard_map/ppermute | solution.py:58
  511.4 22.4 %collective-permute-start.33 = (bf16[4,2,64,1024]{3,2,0,1:T(8,128)(2,1)S(1)}, bf16[4,2,64,1024]{3,2,0,1:T(8,128)(2,1)S(1)}, u32[]{:S(2)}, u32[]{:S(2)}) collective-permute-start(bf16[4,2,64,1024]{3,2,0,1:T(8,128)(2,1)S(1)} %fusion.30), channel_id=1, source_target_pairs={{0,2},{2,0},{1,3},{3,1},{4,6},{6,4},{5,7},{7,5},{8,10},{10,8},{9,1... | collective-permute-start | bytes 3145736 | tf_op jit(solution)/shard_map/ppermute | solution.py:58
  513.4 19.0 %collective-permute-start.36 = (bf16[2,2,96,1024]{3,2,1,0:T(8,128)(2,1)S(1)}, bf16[2,2,96,1024]{3,2,1,0:T(8,128)(2,1)S(1)}, u32[]{:S(2)}, u32[]{:S(2)}) collective-permute-start(bf16[2,2,96,1024]{3,2,1,0:T(8,128)(2,1)S(1)} %fusion.40), channel_id=1, source_target_pairs={{0,4},{4,0},{1,5},{5,1},{2,6},{6,2},{3,7},{7,3},{8,12},{12,8},{9,1... | collective-permute-start | bytes 2359304 | tf_op jit(solution)/shard_map/ppermute | solution.py:58
  515.9 17.9 %collective-permute-start.34 = (bf16[4,2,64,512]{3,2,0,1:T(8,128)(2,1)S(1)}, bf16[4,2,64,512]{3,2,0,1:T(8,128)(2,1)S(1)}, u32[]{:S(2)}, u32[]{:S(2)}) collective-permute-start(bf16[4,2,64,512]{3,2,0,1:T(8,128)(2,1)S(1)} %fusion.46), channel_id=1, source_target_pairs={{0,2},{2,0},{1,3},{3,1},{4,6},{6,4},{5,7},{7,5},{8,10},{10,8},{9,1... | collective-permute-start | bytes 1572872 | tf_op jit(solution)/shard_map/ppermute | solution.py:58
  547.4 19.1 %collective-permute-start.43 = (bf16[2,2,96,1024]{3,2,1,0:T(8,128)(2,1)S(1)}, bf16[2,2,96,1024]{3,2,1,0:T(8,128)(2,1)S(1)}, u32[]{:S(2)}, u32[]{:S(2)}) collective-permute-start(bf16[2,2,96,1024]{3,2,1,0:T(8,128)(2,1)S(1)} %get-tuple-element.204), channel_id=1, source_target_pairs={{0,2},{2,0},{1,3},{3,1},{4,6},{6,4},{5,7},{7,5},{8,10},{10,8},{9,1... | collective-permute-start | bytes 2359304 | tf_op jit(solution)/shard_map/ppermute | solution.py:58
  548.3 18.7 %collective-permute-start.41 = (bf16[4,64,512]{2,1,0:T(8,128)(2,1)S(1)}, bf16[4,64,512]{2,1,0:T(8,128)(2,1)S(1)}, u32[]{:S(2)}, u32[]{:S(2)}) collective-permute-start(bf16[4,64,512]{2,1,0:T(8,128)(2,1)S(1)} %fusion.51), channel_id=1, source_target_pairs={{0,4},{4,0},{1,5},{5,1},{2,6},{6,2},{3,7},{7,3},{8,12},{12,8},{9,1... | collective-permute-start | bytes 786440 | tf_op jit(solution)/shard_map/ppermute | solution.py:58
  572.2 30.4 %collective-permute-start.48 = (bf16[2,2,96,1024]{3,2,1,0:T(8,128)(2,1)S(1)}, bf16[2,2,96,1024]{3,2,1,0:T(8,128)(2,1)}, u32[]{:S(2)}, u32[]{:S(2)}) collective-permute-start(bf16[2,2,96,1024]{3,2,1,0:T(8,128)(2,1)S(1)} %slice_bitcast_fusion.6), channel_id=1, source_target_pairs={{0,4},{4,0},{1,5},{5,1},{2,6},{6,2},{3,7},{7,3},{8,12},{12,8},{9,1... | collective-permute-start | bytes 2359304 | tf_op jit(solution)/shard_map/ppermute | solution.py:58
  573.8 20.7 %collective-permute-start.44 = (f32[34,1024]{1,0:T(8,128)S(1)}, f32[34,1024]{1,0:T(8,128)S(1)}, u32[]{:S(2)}, u32[]{:S(2)}) collective-permute-start(f32[34,1024]{1,0:T(8,128)S(1)} %add.269), channel_id=1, source_target_pairs={{0,4},{4,0},{1,5},{5,1},{2,6},{6,2},{3,7},{7,3},{8,12},{12,8},{9,1... | collective-permute-start | bytes 417800 | tf_op jit(solution)/shard_map/ppermute | solution.py:65
  (73 other events, 811.6 us)
Sparse Core Ops, SparseCore 0:
  11.0 57.9 all-gather.7
  77.6 115.7 all-gather.13
  195.5 61.6 all-gather.11
  258.6 62.0 all-gather.9
  322.8 109.4 reduce-scatter.2
  434.4 111.2 reduce-scatter.4

commit v5 on v4

--- a/solution.py
+++ b/solution.py
@@ -114,10 +114,9 @@
 
 
 def piece(near, given, sequence, which, rows):
-    return add(
-        lax.dynamic_slice_in_dim(near[sequence], which * rows, rows, 0),
-        lax.dynamic_slice_in_dim(given[sequence], which * rows, rows, 0),
-    )
+    start = (jnp.int32(sequence), which.astype(jnp.int32) * rows, jnp.int32(0))
+    shape = (1, rows, near.shape[2])
+    return add(lax.dynamic_slice(near, start, shape), lax.dynamic_slice(given, start, shape))[0]
 
 
 def scatter_group(near, given, tensor_size):
@@ -130,6 +129,8 @@
     half = rows // 2
     take = functools.partial(piece, near, given)
     corner = take(1, 1 - me, rows).astype(bf16)
+    corner, near, given = together(corner, near, given)
+    take = functools.partial(piece, near, given)
     low, high = swap(corner[:half], "tensor"), swap(corner[half:], "y")
     by_tensor, by_y = take(0, 1 - me, rows), take(1, me, rows)
     first_tensor = swap(by_tensor[:half].astype(bf16), "tensor")
@@ -311,13 +312,8 @@
             sum_refs[place][0] = values
             return
 
-        @pl.when(step < 2)
-        def _():
-            sum_refs[2 * place][0] = values
-
-        @pl.when(step >= 2)
-        def _():
-            sum_refs[2 * place + 1][0] = values
+        sum_refs[2 * place][0] = values
+        sum_refs[2 * place + 1][0] = values
     shards_z, members, rows = weight_ref.shape[0], weight_ref.shape[2], weight_ref.shape[3]
     hidden = down.shape[0]
     both_rows = both.shape[0] // (shards_z * members)
@@ -400,10 +396,12 @@
     part = pl.BlockSpec(one, lambda s: (0, place, 0, 0, 0))
     slots = sequences * CAP
     if last:
-        near = pl.BlockSpec((1, seq_len, width), lambda s: (jnp.minimum(s, 1), 0, 0))
+        near = pl.BlockSpec((1, seq_len, width), lambda s: (jnp.minimum(s, 2), 0, 0))
         far = pl.BlockSpec((1, seq_len, width), lambda s: (jnp.maximum(s - 2, 0), 0, 0))
         sums = [near, far, near, far]
-        sum_shapes = [jax.ShapeDtypeStruct((2, seq_len, width), bf16)] * 4
+        sum_shapes = [
+            jax.ShapeDtypeStruct((count, seq_len, width), bf16) for count in (3, 2, 3, 2)
+        ]
     else:
         sums, sum_shapes = [per_seq] * 2, [jax.ShapeDtypeStruct(tokens.shape, bf16)] * 2
     return pl.pallas_call(
@@ -587,7 +585,9 @@
     moe_near, moe_give, normed_near, normed_give = carry
 
     pair_grad = jnp.concatenate(pairs, axis=1)
-    pair_core = stacked(pair_grad[:2], swap(pair_grad[2:], "core"), core_first)
+    pair_given = swap(pair_grad[2:], "core")
+    normed_give = after(normed_give, pair_given)
+    pair_core = stacked(pair_grad[:2], pair_given, core_first)
     pair_y = in_order(pair_core[0], swap(pair_core[1], "y"), y_first)
     pair_y = pair_y.reshape(experts_local, seq_len)
     if tensor_size == 2:
@@ -626,6 +626,8 @@
         local = seq_len // 2
         moe_piece = functools.partial(piece, moe_near, moe_given)
         moe_far = moe_piece(1, 1 - my_tensor, local).astype(bf16)
+        moe_far, moe_given = together(moe_far, moe_given)
+        moe_piece = functools.partial(piece, moe_near, moe_given)
         moe_own_far = moe_piece(1, my_tensor, local).astype(bf16)
     else:
         moe_far = add(moe_near[1], moe_given[1]).astype(bf16)
@@ -644,7 +646,7 @@
 
     mixed_grad = jnp.dot(attn_grad_all, out_full, preferred_element_type=f32).astype(bf16)
     qkv_pre_grad = attention_backward(qkv_rot, mixed_grad, log_totals, cosine, sine)
-    qkv_pre_grad, moe_own_far = together(qkv_pre_grad, moe_own_far)
+    qkv_pre_grad, moe_own_far, *early = together(qkv_pre_grad, moe_own_far, *early)
 
     attn_part = contract(qkv_pre_grad, qkv_full, 1, 1)
     attn_scattered = scatter_rows(attn_part, tensor_size)
@@ -657,7 +659,7 @@
         attn_scattered,
         swap(qkv_give, "core"),
         swap(out_give, "core"),
-        *[y_owners(part) for part in early],
+        *[y_owners(after(part, qkv_pre_grad)) for part in early],
     )
     input_part, attn_gain_part = norm_backward(attn_normed_grad, input_rows, attn_gain)
     input_grad = (state_grad + input_part).astype(bf16)
@@ -674,26 +676,33 @@
         moe_given = scatter_rows(add(add(moe_near[0], moe_given[0]), moe_far), tensor_size)
     qkv_keep, qkv_give = halves(jnp.moveaxis(add(qkv_keep, qkv_given), 1, 0), my_y)
     out_keep, out_give = halves(jnp.moveaxis(add(out_keep, out_given), 1, 0), my_y)
-    small = butterfly_sum(small, (("core", 2), ("z", z_size)))
-    late = core_owners(after(parts[-1], attn_normed_grad))
-    small, qkv_given, out_given, moe_given, late = together(
-        small, swap(qkv_give, "y"), swap(out_give, "y"), moe_given, late
-    )
+    small = butterfly_sum(small, (("core", 2), ("tensor", tensor_size)))
+    small, qkv_given, out_given, moe_given = together(
+        small, swap(qkv_give, "y"), swap(out_give, "y"), moe_given
+    )
+    late = core_owners(after(parts[-1], small))
     dp_sum = jnp.concatenate([add(qkv_keep, qkv_given), add(out_keep, out_given)], axis=-1)
+
+    def z_pairs(step):
+        return [(i, i ^ step) for i in range(z_size)]
+
+    def z_halve(part, step):
+        part = jnp.moveaxis(part.reshape(-1, 2, shard_rows, part.shape[-1]), 1, 0)
+        keep, give = halves(part, (my_z // step) % 2)
+        return add(keep, lax.ppermute(give, "z", z_pairs(step)))
+
+    small = butterfly_sum(small, (("y", 2),))
     step = 1
     while step < z_size:
-        keep, give = halves(
-            jnp.moveaxis(dp_sum.reshape(-1, 2, shard_rows, dp_sum.shape[-1]), 1, 0),
-            (my_z // step) % 2,
-        )
-        dp_sum = add(keep, lax.ppermute(give, "z", [(i, i ^ step) for i in range(z_size)]))
+        if 2 * step == z_size:
+            dp_sum, small, late = together(dp_sum, small, late)
+        dp_sum = z_halve(dp_sum, step)
+        small = small + lax.ppermute(small, "z", z_pairs(step))
         step *= 2
     dp_sum = dp_sum.reshape(shard_rows, dp_sum.shape[-1])
     late = y_owners(late)
-    small, dp_sum = together(butterfly_sum(small, (("y", 2),)), dp_sum)
     qkv_sum, out_sum = dp_sum[:, :wide], dp_sum[:, wide:]
     block_output = (hidden_state + residual_scale * add(moe_sum, moe_given)).astype(bf16)
-    small = butterfly_sum(small, (("tensor", tensor_size),))
     owners.append(late)
     summed = jnp.concatenate(owners, axis=2)
     summed = summed.reshape(experts_local, rows, both_width)

time: 621 us -> 602 us (0.969)
  local copies, waits for them, and re-layouts: 44.2 us -> 29.6 us
  other arithmetic: 63.2 us -> 75.7 us
    ppermute x5 -> x3, waiting for transfers between devices: 21.2 us -> 4.02 us  [butterfly_sum(): lax.ppermute(values, axis, [(i, i ^ step) for i in range(size)])]
    ppermute x2 -> x4, waiting for transfers between devices: 4.3 us -> 18.3 us  [the longest x2 16.1 us: shards(): small = small + lax.ppermute(small, 'z', z_pairs(step))]
    slice x4 -> x1, local copies, waits for them, and re-layouts: 9.71 us -> 0.01 us  [shards(): pair_given = swap(pair_grad[2:], 'core')]
    reduce_scatter x2, waiting for transfers between devices: 9.48 us -> 0.3 us  [shards(): parts.append(lax.psum_scatter(part, 'z', scatter_dimension=0, tiled=False))]
    ppermute x42, waiting for transfers between devices: 171 us -> 179 us  [swap(): return lax.ppermute(values, axis, [(0, 1), (1, 0)])]
    unnamed x103 -> x75, local copies, waits for them, and re-layouts: 13.5 us -> 9.34 us
  transfers between devices with their start and end apart: 55 -> 55, of which waited for: 30 -> 31; matrix products, arithmetic and copies ran while one was open for 18% -> 18% of each run, Pallas kernels for 34% -> 35%
where the time goes in v5:
time: 602 us; the launch traced here: 597 us
  Pallas kernels  208 us (35%)
  waiting for transfers between devices  202 us (34%)
  other arithmetic  75.7 us (13%)
  starting transfers between devices  42.1 us (7%)
  local copies, waits for them, and re-layouts  29.6 us (5%)
  matrix products  24.2 us (4%)
  between operations  15.7 us (3%)
    ppermute x42, waiting for transfers between devices, swap(): return lax.ppermute(values, axis, [(0, 1), (1, 0)])  179 us
    pallas_call x4, Pallas kernels, run_expert(): pl.pallas_call(functools.partial(expert_kernel, bool(carry), bool(shared)...  164 us
    ppermute x42, starting transfers between devices, swap(): return lax.ppermute(values, axis, [(0, 1), (1, 0)])  33.2 us
    pallas_call x1, Pallas kernels, attention_backward(): pl.pallas_call(attention_backward_kernel, grid=(groups,), in_specs=[wide,...  26.6 us
    pallas_call x1, Pallas kernels, attention_forward(): pl.pallas_call(attention_forward_kernel, grid=(groups,), in_specs=[wide,...  17.6 us
    ppermute x2, waiting for transfers between devices, shards(): small = small + lax.ppermute(small, 'z', z_pairs(step))  16.1 us
  transfers between devices with their start and end apart: 55, of which 31 were waited for; matrix products, arithmetic and copies ran while one was open for 18% of the time, Pallas kernels for 35%

profile of v5, /device:TPU:0, one launch (start us, length us, event | category | flops | bytes accessed | tf_op | source)
XLA Modules:
  0.0 596.8 jit_solution(9998839759886491403)
XLA Ops:
  13.7 3.0 collective-permute-start
  25.3 14.9 %collective-permute-done = bf16[512,1024]{1,0:T(8,128)(2,1)} collective-permute-done((bf16[512,1024]{1,0:T(8,128)(2,1)}, bf16[512,1024]{1,0:T(8,128)(2,1)}, u32[]{:S(2)}, u32[]{:S(2)}) %collective-permute-start) | collective-permute-done | bytes 1048608 | tf_op jit(solution)/shard_map/ppermute | solution.py:58
  45.8 22.0 %collective-permute-done.3 = bf16[2,4,96,1024]{3,2,1,0:T(8,128)(2,1)} collective-permute-done((bf16[2,4,96,1024]{3,2,1,0:T(8,128)(2,1)}, bf16[2,4,96,1024]{3,2,1,0:T(8,128)(2,1)}, u32[]{:S(2)}, u32[]{:S(2)}) %collective-permute-start.3) | collective-permute-done | bytes 1572896 | tf_op jit(solution)/shard_map/ppermute | solution.py:58
  78.9 6.6 %fusion.22.pre_ref = f32[1024,1024]{1,0:T(8,128)} fusion(bf16[1024,1024]{1,0:T(8,128)(2,1)} %pad_maximum_fusion.4, bf16[1024,1536]{1,0:T(8,128)(2,1)} %all-gather.8.cloned.1.call-done), kind=kOutput, calls=%fused_computation.57 | convolution fusion | flops 2147483648 | bytes 8388608 | tf_op jit(solution)/shard_map/dot_general | solution.py:543
  88.4 17.6 %attention_forward.1 = (bf16[1024,512]{1,0:T(8,128)(2,1)}, bf16[1024,1024]{1,0:T(8,128)(2,1)}, f32[1024,512]{1,0:T(8,128)}) custom-call(f32[1024,1024]{1,0:T(8,128)} %fusion.22.pre_ref, f32[1024,128]{1,0:T(8,128)} %copy.56.cos_ref, f32[1024,128]{1,0:T(8,128)} %copy.57.sin_ref), custom_call_target="tpu_custom_call" | custom-call | flops 3221225472 | bytes 10485760 | tf_op jit(solution)/shard_map/attention_forward/pallas_call | solution.py:260
  113.7 22.5 %collective-permute-done.6 = bf16[512,1024]{1,0:T(8,128)(2,1)} collective-permute-done((bf16[512,1024]{1,0:T(8,128)(2,1)S(1)}, bf16[512,1024]{1,0:T(8,128)(2,1)}, u32[]{:S(2)}, u32[]{:S(2)}) %collective-permute-start.6) | collective-permute-done | bytes 1048608 | tf_op jit(solution)/shard_map/ppermute | solution.py:58
  143.0 7.2 %pad_maximum_fusion.grad_ref = bf16[4,1024,1024]{2,1,0:T(8,128)(2,1)} fusion(bf16[1,1024,1024]{2,1,0:T(8,128)(2,1)} %bitcast.28, bf16[1,1024,1024]{2,1,0:T(8,128)(2,1)} %bitcast.27, bf16[1,1024,1024]{2,1,0:T(8,128)(2,1)} %bitcast.26, bf16[1,1024,1024]{2,1,0:T(8,128)(2,1)} %bitcast.25), kind=kLoop, calls=%fused_computation.1 | loop fusion | flops 12582912 | bytes 16777216 | tf_op jit(solution)/shard_map/stack | solution.py:550
  150.2 16.2 %collective-permute-done.11 = bf16[512,1024]{1,0:T(8,128)(2,1)S(1)} collective-permute-done((bf16[512,1024]{1,0:T(8,128)(2,1)S(1)}, bf16[512,1024]{1,0:T(8,128)(2,1)S(1)}, u32[]{:S(2)}, u32[]{:S(2)}) %collective-permute-start.11) | collective-permute-done | bytes 1048608 | tf_op jit(solution)/shard_map/ppermute | solution.py:58
  169.7 13.2 %collective-permute-done.14 = bf16[256,1024]{1,0:T(8,128)(2,1)S(1)} collective-permute-done((bf16[256,1024]{1,0:T(8,128)(2,1)S(1)}, bf16[256,1024]{1,0:T(8,128)(2,1)S(1)}, u32[]{:S(2)}, u32[]{:S(2)}) %collective-permute-start.14) | collective-permute-done | bytes 524320 | tf_op jit(solution)/shard_map/ppermute | solution.py:58
  188.4 3.5 collective-permute-done.17
  191.9 3.8 pad_maximum_fusion.1.tokens_ref
  201.1 39.1 %expert.4 = (bf16[4,1024,1024]{2,1,0:T(8,128)(2,1)}, bf16[4,1024,1024]{2,1,0:T(8,128)(2,1)}, f32[4,1,1024]{2,1,0:T(1,128)}, bf16[4,2,4,96,1024]{4,3,2,1,0:T(8,128)(2,1)}) custom-call(s32[1]{0:T(128)} %bitcast.24.member_ref, bf16[4,1024,1024]{2,1,0:T(8,128)(2,1)} %copy-done.5, bf16[4,1024,1024]{2,1,0:T(8,128)(2,1)} %pad_maximum_fusion.grad_ref, ...), custom_call_target="tpu_custom_call" | custom-call | flops 22817013760 | bytes 56623104 | tf_op jit(solution)/shard_map/expert/pallas_call | solution.py:407
  240.2 40.3 %expert.5 = (bf16[4,1024,1024]{2,1,0:T(8,128)(2,1)}, bf16[4,1024,1024]{2,1,0:T(8,128)(2,1)}, f32[4,1,1024]{2,1,0:T(1,128)}, bf16[4,2,4,96,1024]{4,3,2,1,0:T(8,128)(2,1)}) custom-call(s32[1]{0:T(128)} %bitcast.24.member_ref, bf16[4,1024,1024]{2,1,0:T(8,128)(2,1)} %copy-done.5, ...), custom_call_target="tpu_custom_call", output_to_operand_aliasing={{3}: (8, {})} | custom-call | flops 22817013760 | bytes 56623104 | tf_op jit(solution)/shard_map/expert/pallas_call | solution.py:407
  280.5 41.1 %expert.6 = (bf16[4,1024,1024]{2,1,0:T(8,128)(2,1)}, bf16[4,1024,1024]{2,1,0:T(8,128)(2,1)}, f32[4,1,1024]{2,1,0:T(1,128)}, bf16[4,2,4,96,1024]{4,3,2,1,0:T(8,128)(2,1)}) custom-call(s32[1]{0:T(128)} %bitcast.24.member_ref, bf16[4,1024,1024]{2,1,0:T(8,128)(2,1)} %copy-done.5, bf16[4,1024,1024]{2,1,0:T(8,128)(2,1)} %pad_maximum_fusion.grad_ref, ...), custom_call_target="tpu_custom_call" | custom-call | flops 22817013760 | bytes 56623104 | tf_op jit(solution)/shard_map/expert/pallas_call | solution.py:407
  321.7 43.0 %expert.7 = (bf16[3,1024,1024]{2,1,0:T(8,128)(2,1)}, bf16[2,1024,1024]{2,1,0:T(8,128)(2,1)}, bf16[3,1024,1024]{2,1,0:T(8,128)(2,1)}, bf16[2,1024,1024]{2,1,0:T(8...) custom-call(s32[1]{0:T(128)} %bitcast.24.member_ref, ...), custom_call_target="tpu_custom_call", output_to_operand_aliasing={{5}: (8, {})} | custom-call | flops 22817013760 | bytes 56623104 | tf_op jit(solution)/shard_map/expert/pallas_call | solution.py:407
  367.6 3.4 collective-permute-done.20
  379.5 3.1 convert_add_fusion.3
  384.9 7.2 %collective-permute-done.25 = bf16[256,1024]{1,0:T(8,128)(2,1)S(1)} collective-permute-done((bf16[256,1024]{1,0:T(8,128)(2,1)S(1)}, bf16[256,1024]{1,0:T(8,128)(2,1)S(1)}, u32[]{:S(2)}, u32[]{:S(2)}) %collective-permute-start.25) | collective-permute-done | bytes 524320 | tf_op jit(solution)/shard_map/ppermute | solution.py:58
  395.9 8.0 %collective-permute-done.22 = bf16[256,1024]{1,0:T(8,128)(2,1)S(1)} collective-permute-done((bf16[256,1024]{1,0:T(8,128)(2,1)S(1)}, bf16[256,1024]{1,0:T(8,128)(2,1)S(1)}, u32[]{:S(2)}, u32[]{:S(2)}) %collective-permute-start.22) | collective-permute-done | bytes 524320 | tf_op jit(solution)/shard_map/ppermute | solution.py:58
  403.9 10.5 %collective-permute-done.26 = bf16[256,1024]{1,0:T(8,128)(2,1)S(1)} collective-permute-done((bf16[256,1024]{1,0:T(8,128)(2,1)S(1)}, bf16[256,1024]{1,0:T(8,128)(2,1)S(1)}, u32[]{:S(2)}, u32[]{:S(2)}) %collective-permute-start.26) | collective-permute-done | bytes 524320 | tf_op jit(solution)/shard_map/ppermute | solution.py:58
  427.4 2.9 fusion.30
  430.4 14.5 %collective-permute-done.29 = bf16[512,1024]{1,0:T(8,128)(2,1)} collective-permute-done((bf16[512,1024]{1,0:T(8,128)(2,1)S(1)}, bf16[512,1024]{1,0:T(8,128)(2,1)}, u32[]{:S(2)}, u32[]{:S(2)}) %collective-permute-start.29) | collective-permute-done | bytes 1048608 | tf_op jit(solution)/shard_map/ppermute | solution.py:58
  453.8 3.5 convolution_convert_fusion.grad_ref
  460.9 26.6 %attention_backward.1 = bf16[1024,1024]{1,0:T(8,128)(2,1)} custom-call(bf16[1024,1024]{1,0:T(8,128)(2,1)} %get-tuple-element.144.rot_ref, bf16[1024,512]{1,0:T(8,128)(2,1)} %convolution_convert_fusion.grad_ref, f32[1024,512]{1,0:T(8,128)} %get-tuple-element.149.lse_ref, f32[1024,128]{1,0:T(8,128)} %copy.56.cos_ref, f32[1024,128]{1,0:T(8,128)} %copy.57.sin_ref), custom_call_target="tpu_custom_call" | custom-call | flops 8589934592 | bytes 10485760 | tf_op jit(solution)/shard_map/attention_backward/pallas_call | solution.py:284
  499.7 9.7 %collective-permute-done.36 = bf16[2,2,96,1024]{3,2,1,0:T(8,128)(2,1)S(1)} collective-permute-done((bf16[2,2,96,1024]{3,2,1,0:T(8,128)(2,1)S(1)}, bf16[2,2,96,1024]{3,2,1,0:T(8,128)(2,1)S(1)}, u32[]{:S(2)}, u32[]{:S(2)}) %collective-permute-start.36) | collective-permute-done | bytes 786464 | tf_op jit(solution)/shard_map/ppermute | solution.py:58
  510.8 11.0 %collective-permute-done.33 = bf16[512,1024]{1,0:T(8,128)(2,1)S(1)} collective-permute-done((bf16[512,1024]{1,0:T(8,128)(2,1)S(1)}, bf16[512,1024]{1,0:T(8,128)(2,1)S(1)}, u32[]{:S(2)}, u32[]{:S(2)}) %collective-permute-start.33) | collective-permute-done | bytes 1048608 | tf_op jit(solution)/shard_map/ppermute | solution.py:58
  528.9 3.2 collective-permute-done.38
  533.0 10.8 %collective-permute-done.39 = bf16[4,64,1024]{2,1,0:T(8,128)(2,1)S(1)} collective-permute-done((bf16[4,64,1024]{2,1,0:T(8,128)(2,1)S(1)}, bf16[4,64,1024]{2,1,0:T(8,128)(2,1)S(1)}, u32[]{:S(2)}, u32[]{:S(2)}) %collective-permute-start.39) | collective-permute-done | bytes 524320 | tf_op jit(solution)/shard_map/ppermute | solution.py:58
  551.2 4.2 fusion.19
  555.4 6.1 %collective-permute-done.44 = f32[34,1024]{1,0:T(8,128)S(1)} collective-permute-done((f32[34,1024]{1,0:T(8,128)S(1)}, f32[34,1024]{1,0:T(8,128)S(1)}, u32[]{:S(2)}, u32[]{:S(2)}) %collective-permute-start.44) | collective-permute-done | bytes 139296 | tf_op jit(solution)/shard_map/ppermute | solution.py:700
  562.0 3.0 collective-permute-start.46
  566.8 10.0 %collective-permute-done.46 = f32[34,1024]{1,0:T(8,128)S(1)} collective-permute-done((f32[34,1024]{1,0:T(8,128)S(1)}, f32[34,1024]{1,0:T(8,128)S(1)}, u32[]{:S(2)}, u32[]{:S(2)}) %collective-permute-start.46) | collective-permute-done | bytes 139296 | tf_op jit(solution)/shard_map/ppermute | solution.py:700
  (296 shorter events, 149.6 us)
Async XLA Ops:
  7.2 67.4 %all-gather.8.cloned.1.call-start = ((), (), s32[]{:S(2)}) async-start(), calls=%async_computation.2 | async-start | bytes 3342336 | tf_op jit(solution)/shard_map/all_gather | solution.py:488
  10.9 190.2 %all-gather.14.cloned.1.call-start = ((), (), s32[]{:S(2)}) async-start(), calls=%async_computation.7 | async-start | bytes 7864320 | tf_op jit(solution)/shard_map/all_gather | solution.py:540
  13.7 26.4 %collective-permute-start = (bf16[512,1024]{1,0:T(8,128)(2,1)}, bf16[512,1024]{1,0:T(8,128)(2,1)}, u32[]{:S(2)}, u32[]{:S(2)}) collective-permute-start(bf16[512,1024]{1,0:T(8,128)(2,1)} %fusion.7), channel_id=1, source_target_pairs={{0,1},{1,0},{2,3},{3,2},{4,5},{5,4},{6,7},{7,6},{8,9},{9,8},{10,11... | collective-permute-start | bytes 3145736 | tf_op jit(solution)/shard_map/ppermute | solution.py:58
  21.1 46.7 %collective-permute-start.3 = (bf16[2,4,96,1024]{3,2,1,0:T(8,128)(2,1)}, bf16[2,4,96,1024]{3,2,1,0:T(8,128)(2,1)}, u32[]{:S(2)}, u32[]{:S(2)}) collective-permute-start(bf16[2,4,96,1024]{3,2,1,0:T(8,128)(2,1)} %dynamic-slice_bitcast_fusion), channel_id=1, source_target_pairs={{0,4},{4,0},{1,5},{5,1},{2,6},{6,2},{3,7},{7,3},{8,12},{12,8},{9,1... | collective-permute-start | bytes 4718600 | tf_op jit(solution)/shard_map/ppermute | solution.py:58
  25.0 46.7 %collective-permute-start.2 = (bf16[4,96,1024]{2,1,0:T(8,128)(2,1)}, bf16[4,96,1024]{2,1,0:T(8,128)(2,1)}, u32[]{:S(2)}, u32[]{:S(2)}) collective-permute-start(bf16[4,96,1024]{2,1,0:T(8,128)(2,1)} %get-tuple-element.188), channel_id=1, source_target_pairs={{0,2},{2,0},{1,3},{3,1},{4,6},{6,4},{5,7},{7,5},{8,10},{10,8},{9,1... | collective-permute-start | bytes 2359304 | tf_op jit(solution)/shard_map/ppermute | solution.py:58
  43.5 26.4 %collective-permute-start.1 = (bf16[512,1024]{1,0:T(8,128)(2,1)S(1)}, bf16[512,1024]{1,0:T(8,128)(2,1)S(1)}, u32[]{:S(2)}, u32[]{:S(2)}) collective-permute-start(bf16[512,1024]{1,0:T(8,128)(2,1)S(1)} %fusion.6), channel_id=1, source_target_pairs={{0,1},{1,0},{2,3},{3,2},{4,5},{5,4},{6,7},{7,6},{8,9},{9,8},{10,11... | collective-permute-start | bytes 3145736 | tf_op jit(solution)/shard_map/ppermute | solution.py:58
  77.4 203.1 %all-gather.12.cloned.1.call-start = ((), (), s32[]{:S(2)}) async-start(), calls=%async_computation.6 | async-start | bytes 3932160 | tf_op jit(solution)/shard_map/all_gather | solution.py:540
  87.6 50.8 %collective-permute-start.7 = (bf16[1024,1024]{1,0:T(8,128)(2,1)}, bf16[1024,1024]{1,0:T(8,128)(2,1)}, u32[]{:S(2)}, u32[]{:S(2)}) collective-permute-start(bf16[1024,1024]{1,0:T(8,128)(2,1)} %pad_maximum_fusion.5), channel_id=1, source_target_pairs={{0,4},{4,0},{1,5},{5,1},{2,6},{6,2},{3,7},{7,3},{8,12},{12,8},{9,1... | collective-permute-start | bytes 6291464 | tf_op jit(solution)/shard_map/ppermute | solution.py:58
  111.0 25.2 %collective-permute-start.6 = (bf16[512,1024]{1,0:T(8,128)(2,1)S(1)}, bf16[512,1024]{1,0:T(8,128)(2,1)}, u32[]{:S(2)}, u32[]{:S(2)}) collective-permute-start(bf16[512,1024]{1,0:T(8,128)(2,1)S(1)} %dynamic-slice_convert_fusion.1), channel_id=1, source_target_pairs={{0,1},{1,0},{2,3},{3,2},{4,5},{5,4},{6,7},{7,6},{8,9},{9,8},{10,11... | collective-permute-start | bytes 3145736 | tf_op jit(solution)/shard_map/ppermute | solution.py:58
  111.8 31.0 %collective-permute-start.12 = (bf16[1024,1024]{1,0:T(8,128)(2,1)}, bf16[1024,1024]{1,0:T(8,128)(2,1)}, u32[]{:S(2)}, u32[]{:S(2)}) collective-permute-start(bf16[1024,1024]{1,0:T(8,128)(2,1)} %pad_maximum_fusion.5), channel_id=1, source_target_pairs={{0,2},{2,0},{1,3},{3,1},{4,6},{6,4},{5,7},{7,5},{8,10},{10,8},{9,1... | collective-permute-start | bytes 6291464 | tf_op jit(solution)/shard_map/ppermute | solution.py:58
  139.8 181.9 %all-gather.10.cloned.1.call-start = ((), (), s32[]{:S(2)}) async-start(), calls=%async_computation.5 | async-start | bytes 3932160 | tf_op jit(solution)/shard_map/all_gather | solution.py:540
  140.8 25.6 %collective-permute-start.11 = (bf16[512,1024]{1,0:T(8,128)(2,1)S(1)}, bf16[512,1024]{1,0:T(8,128)(2,1)S(1)}, u32[]{:S(2)}, u32[]{:S(2)}) collective-permute-start(bf16[512,1024]{1,0:T(8,128)(2,1)S(1)} %multiply_convert_fusion.1), channel_id=1, source_target_pairs={{0,4},{4,0},{1,5},{5,1},{2,6},{6,2},{3,7},{7,3},{8,12},{12,8},{9,1... | collective-permute-start | bytes 3145736 | tf_op jit(solution)/shard_map/ppermute | solution.py:58
  142.0 25.3 %collective-permute-start.10 = (bf16[512,1024]{1,0:T(8,128)(2,1)S(1)}, bf16[512,1024]{1,0:T(8,128)(2,1)S(1)}, u32[]{:S(2)}, u32[]{:S(2)}) collective-permute-start(bf16[512,1024]{1,0:T(8,128)(2,1)S(1)} %multiply_convert_fusion.1), channel_id=1, source_target_pairs={{0,1},{1,0},{2,3},{3,2},{4,5},{5,4},{6,7},{7,6},{8,9},{9,8},{10,11... | collective-permute-start | bytes 3145736 | tf_op jit(solution)/shard_map/ppermute | solution.py:58
  187.5 269.8 %reduce-scatter.3.cloned.1.call-start = ((), (), s32[]{:S(2)}) async-start(), calls=%async_computation.3 | async-start | bytes 7864320 | tf_op jit(solution)/shard_map/reduce_scatter | solution.py:583
  280.5 265.3 %reduce-scatter.5.cloned.1.call-start = ((), (), s32[]{:S(2)}) async-start(), calls=%async_computation.4 | async-start | bytes 7864320 | tf_op jit(solution)/shard_map/reduce_scatter | solution.py:583
  375.2 41.7 %collective-permute-start.28 = (bf16[2,1024,1024]{2,1,0:T(8,128)(2,1)}, bf16[2,1024,1024]{2,1,0:T(8,128)(2,1)}, u32[]{:S(2)}, u32[]{:S(2)}) collective-permute-start(bf16[2,1024,1024]{2,1,0:T(8,128)(2,1)} %get-tuple-element.141), channel_id=1, source_target_pairs={{0,2},{2,0},{1,3},{3,1},{4,6},{6,4},{5,7},{7,5},{8,10},{10,8},{9,1... | collective-permute-start | bytes 12582920 | tf_op jit(solution)/shard_map/ppermute | solution.py:58
  382.7 21.2 %collective-permute-start.22 = (bf16[256,1024]{1,0:T(8,128)(2,1)S(1)}, bf16[256,1024]{1,0:T(8,128)(2,1)S(1)}, u32[]{:S(2)}, u32[]{:S(2)}) collective-permute-start(bf16[256,1024]{1,0:T(8,128)(2,1)S(1)} %fusion.47), channel_id=1, source_target_pairs={{0,1},{1,0},{2,3},{3,2},{4,5},{5,4},{6,7},{7,6},{8,9},{9,8},{10,11... | collective-permute-start | bytes 1572872 | tf_op jit(solution)/shard_map/ppermute | solution.py:58
  383.3 20.6 %collective-permute-start.23 = (bf16[256,1024]{1,0:T(8,128)(2,1)S(1)}, bf16[256,1024]{1,0:T(8,128)(2,1)S(1)}, u32[]{:S(2)}, u32[]{:S(2)}) collective-permute-start(bf16[256,1024]{1,0:T(8,128)(2,1)S(1)} %fusion.48), channel_id=1, source_target_pairs={{0,4},{4,0},{1,5},{5,1},{2,6},{6,2},{3,7},{7,3},{8,12},{12,8},{9,1... | collective-permute-start | bytes 1572872 | tf_op jit(solution)/shard_map/ppermute | solution.py:58
  393.0 21.4 %collective-permute-start.26 = (bf16[256,1024]{1,0:T(8,128)(2,1)S(1)}, bf16[256,1024]{1,0:T(8,128)(2,1)S(1)}, u32[]{:S(2)}, u32[]{:S(2)}) collective-permute-start(bf16[256,1024]{1,0:T(8,128)(2,1)S(1)} %fusion.35), channel_id=1, source_target_pairs={{0,1},{1,0},{2,3},{3,2},{4,5},{5,4},{6,7},{7,6},{8,9},{9,8},{10,11... | collective-permute-start | bytes 1572872 | tf_op jit(solution)/shard_map/ppermute | solution.py:58
  394.7 19.7 %collective-permute-start.27 = (bf16[256,1024]{1,0:T(8,128)(2,1)S(1)}, bf16[256,1024]{1,0:T(8,128)(2,1)S(1)}, u32[]{:S(2)}, u32[]{:S(2)}) collective-permute-start(bf16[256,1024]{1,0:T(8,128)(2,1)S(1)} %fusion.33), channel_id=1, source_target_pairs={{0,4},{4,0},{1,5},{5,1},{2,6},{6,2},{3,7},{7,3},{8,12},{12,8},{9,1... | collective-permute-start | bytes 1572872 | tf_op jit(solution)/shard_map/ppermute | solution.py:58
  420.2 24.7 %collective-permute-start.29 = (bf16[512,1024]{1,0:T(8,128)(2,1)S(1)}, bf16[512,1024]{1,0:T(8,128)(2,1)}, u32[]{:S(2)}, u32[]{:S(2)}) collective-permute-start(bf16[512,1024]{1,0:T(8,128)(2,1)S(1)} %get-tuple-element.177), channel_id=1, source_target_pairs={{0,1},{1,0},{2,3},{3,2},{4,5},{5,4},{6,7},{7,6},{8,9},{9,8},{10,11... | collective-permute-start | bytes 3145736 | tf_op jit(solution)/shard_map/ppermute | solution.py:58
  424.8 24.6 %collective-permute-start.30 = (bf16[512,1024]{1,0:T(8,128)(2,1)}, bf16[512,1024]{1,0:T(8,128)(2,1)}, u32[]{:S(2)}, u32[]{:S(2)}) collective-permute-start(bf16[512,1024]{1,0:T(8,128)(2,1)} %fusion.29), channel_id=1, source_target_pairs={{0,4},{4,0},{1,5},{5,1},{2,6},{6,2},{3,7},{7,3},{8,12},{12,8},{9,1... | collective-permute-start | bytes 3145736 | tf_op jit(solution)/shard_map/ppermute | solution.py:58
  451.9 80.3 %collective-permute-start.41 = (bf16[512,1024]{1,0:T(8,128)(2,1)S(1)}, bf16[512,1024]{1,0:T(8,128)(2,1)}, u32[]{:S(2)}, u32[]{:S(2)}) collective-permute-start(bf16[512,1024]{1,0:T(8,128)(2,1)S(1)} %fusion.15), channel_id=1, source_target_pairs={{0,1},{1,0},{2,3},{3,2},{4,5},{5,4},{6,7},{7,6},{8,9},{9,8},{10,11... | collective-permute-start | bytes 3145736 | tf_op jit(solution)/shard_map/ppermute | solution.py:58
  452.3 37.0 %collective-permute-start.31 = (bf16[512,1024]{1,0:T(8,128)(2,1)}, bf16[512,1024]{1,0:T(8,128)(2,1)}, u32[]{:S(2)}, u32[]{:S(2)}) collective-permute-start(bf16[512,1024]{1,0:T(8,128)(2,1)} %fusion.30), channel_id=1, source_target_pairs={{0,4},{4,0},{1,5},{5,1},{2,6},{6,2},{3,7},{7,3},{8,12},{12,8},{9,1... | collective-permute-start | bytes 3145736 | tf_op jit(solution)/shard_map/ppermute | solution.py:58
  460.9 26.6 %collective-permute-start.32 = (bf16[2,2,96,1024]{3,2,0,1:T(8,128)(2,1)}, bf16[2,2,96,1024]{3,2,0,1:T(8,128)(2,1)}, u32[]{:S(2)}, u32[]{:S(2)}) collective-permute-start(bf16[2,2,96,1024]{3,2,0,1:T(8,128)(2,1)} %slice_bitcast_fusion.4), channel_id=1, source_target_pairs={{0,2},{2,0},{1,3},{3,1},{4,6},{6,4},{5,7},{7,5},{8,10},{10,8},{9,1... | collective-permute-start | bytes 2359304 | tf_op jit(solution)/shard_map/ppermute | solution.py:58
  489.4 19.9 %collective-permute-start.36 = (bf16[2,2,96,1024]{3,2,1,0:T(8,128)(2,1)S(1)}, bf16[2,2,96,1024]{3,2,1,0:T(8,128)(2,1)S(1)}, u32[]{:S(2)}, u32[]{:S(2)}) collective-permute-start(bf16[2,2,96,1024]{3,2,1,0:T(8,128)(2,1)S(1)} %slice_bitcast_fusion.7), channel_id=1, source_target_pairs={{0,4},{4,0},{1,5},{5,1},{2,6},{6,2},{3,7},{7,3},{8,12},{12,8},{9,1... | collective-permute-start | bytes 2359304 | tf_op jit(solution)/shard_map/ppermute | solution.py:58
  496.2 25.5 %collective-permute-start.33 = (bf16[512,1024]{1,0:T(8,128)(2,1)S(1)}, bf16[512,1024]{1,0:T(8,128)(2,1)S(1)}, u32[]{:S(2)}, u32[]{:S(2)}) collective-permute-start(bf16[512,1024]{1,0:T(8,128)(2,1)S(1)} %dynamic-slice_convert_fusion), channel_id=1, source_target_pairs={{0,1},{1,0},{2,3},{3,2},{4,5},{5,4},{6,7},{7,6},{8,9},{9,8},{10,11... | collective-permute-start | bytes 3145736 | tf_op jit(solution)/shard_map/ppermute | solution.py:58
  497.7 24.5 %collective-permute-start.34 = (bf16[4,2,64,1024]{3,2,0,1:T(8,128)(2,1)S(1)}, bf16[4,2,64,1024]{3,2,0,1:T(8,128)(2,1)S(1)}, u32[]{:S(2)}, u32[]{:S(2)}) collective-permute-start(bf16[4,2,64,1024]{3,2,0,1:T(8,128)(2,1)S(1)} %fusion.31), channel_id=1, source_target_pairs={{0,2},{2,0},{1,3},{3,1},{4,6},{6,4},{5,7},{7,5},{8,10},{10,8},{9,1... | collective-permute-start | bytes 3145736 | tf_op jit(solution)/shard_map/ppermute | solution.py:58
  499.2 22.9 %collective-permute-start.35 = (bf16[4,2,64,512]{3,2,0,1:T(8,128)(2,1)S(1)}, bf16[4,2,64,512]{3,2,0,1:T(8,128)(2,1)S(1)}, u32[]{:S(2)}, u32[]{:S(2)}) collective-permute-start(bf16[4,2,64,512]{3,2,0,1:T(8,128)(2,1)S(1)} %fusion.46), channel_id=1, source_target_pairs={{0,2},{2,0},{1,3},{3,1},{4,6},{6,4},{5,7},{7,5},{8,10},{10,8},{9,1... | collective-permute-start | bytes 1572872 | tf_op jit(solution)/shard_map/ppermute | solution.py:58
  524.6 19.2 %collective-permute-start.39 = (bf16[4,64,1024]{2,1,0:T(8,128)(2,1)S(1)}, bf16[4,64,1024]{2,1,0:T(8,128)(2,1)S(1)}, u32[]{:S(2)}, u32[]{:S(2)}) collective-permute-start(bf16[4,64,1024]{2,1,0:T(8,128)(2,1)S(1)} %fusion.45), channel_id=1, source_target_pairs={{0,4},{4,0},{1,5},{5,1},{2,6},{6,2},{3,7},{7,3},{8,12},{12,8},{9,1... | collective-permute-start | bytes 1572872 | tf_op jit(solution)/shard_map/ppermute | solution.py:58
  565.1 15.2 %collective-permute-start.47 = (bf16[1,64,1536]{2,1,0:T(8,128)(2,1)S(1)}, bf16[1,64,1536]{2,1,0:T(8,128)(2,1)S(1)}, u32[]{:S(2)}, u32[]{:S(2)}) collective-permute-start(bf16[1,64,1536]{2,1,0:T(8,128)(2,1)S(1)} %dynamic-slice_convert_fusion.5), channel_id=1, source_target_pairs={{0,16},{8,24},{16,0},{24,8},{1,17},{9,25},{17,1},{25,9},{2,18},{10... | collective-permute-start | bytes 589832 | tf_op jit(solution)/shard_map/ppermute | solution.py:692
  565.2 18.3 %collective-permute-start.48 = (bf16[2,2,96,1024]{3,2,1,0:T(8,128)(2,1)S(1)}, bf16[2,2,96,1024]{3,2,1,0:T(8,128)(2,1)}, u32[]{:S(2)}, u32[]{:S(2)}) collective-permute-start(bf16[2,2,96,1024]{3,2,1,0:T(8,128)(2,1)S(1)} %slice_bitcast_fusion.6), channel_id=1, source_target_pairs={{0,4},{4,0},{1,5},{5,1},{2,6},{6,2},{3,7},{7,3},{8,12},{12,8},{9,1... | collective-permute-start | bytes 2359304 | tf_op jit(solution)/shard_map/ppermute | solution.py:58
  (59 other events, 739.3 us)
Sparse Core Ops, SparseCore 0:
  11.0 57.9 all-gather.7
  77.5 115.7 all-gather.13
  195.4 61.6 all-gather.11
  258.5 62.0 all-gather.9
  322.8 109.4 reduce-scatter.2
  434.4 111.2 reduce-scatter.4

commit v6 on v5

--- a/solution.py
+++ b/solution.py
@@ -477,15 +477,19 @@
         ordered = [jnp.where(is_first, mine, theirs), jnp.where(is_first, theirs, mine)]
         return jnp.stack(ordered, axis)
 
-    packed = jnp.concatenate(
-        [
-            jnp.concatenate([query_weight.reshape(shard_rows, groups, -1), kv_weight], axis=2)
-            .reshape(shard_rows, wide),
-            out_weight.T,
-        ],
-        axis=1,
-    )
-    packed_full = lax.all_gather(packed, ("z", "y", "core"), axis=0, tiled=True)
+    qkv_shard = jnp.concatenate(
+        [query_weight.reshape(shard_rows, groups, -1), kv_weight], axis=2
+    ).reshape(shard_rows, wide)
+    qkv_full = lax.all_gather(qkv_shard, ("z", "y", "core"), axis=0, tiled=True)
+
+    out_z, step = out_weight.T[None], 1
+    while step < z_size:
+        other = lax.ppermute(out_z, "z", [(i, i ^ step) for i in range(z_size)])
+        high = (my_z // step) % 2 == 1
+        out_z = jnp.concatenate(
+            [jnp.where(high, other, out_z), jnp.where(high, out_z, other)], axis=0
+        )
+        step *= 2
 
     input_rows = block_input.astype(f32)
     attn_normed = (input_rows * row_scale(input_rows) * attn_gain).astype(bf16)
@@ -499,16 +503,21 @@
     rows, both_width = experts.shape[1:]
     grouped = experts.reshape(2, 2, owned, rows, both_width)
     own_y, give_y = at(grouped, my_y), at(grouped, 1 - my_y)
-    from_y = swap(give_y, "y")
-    members = jnp.stack(
-        [
-            at(own_y, my_core),
-            swap(at(own_y, 1 - my_core), "core"),
-            at(from_y, my_core),
-            swap(at(from_y, 1 - my_core), "core"),
-        ],
-        axis=1,
-    )
+    bunch = min(2, owned)
+
+    def gather_members(near, far):
+        return jnp.stack(
+            [
+                at(near, my_core),
+                swap(at(near, 1 - my_core), "core"),
+                at(far, my_core),
+                swap(at(far, 1 - my_core), "core"),
+            ],
+            axis=1,
+        )
+
+    first_y = swap(give_y[:, :bunch], "y")
+    first_members = gather_members(own_y[:, :bunch], first_y)
     moe_own = gather_rows(moe_rows, tensor_size)
 
     ids_t = expert_ids.T
@@ -520,33 +529,40 @@
     rank = jnp.dot(hits.astype(bf16), earlier, preferred_element_type=f32)
     code = jnp.where(hits, jnp.where(rank < CAP, rank, -1.0), -2.0)
 
-    half_dim = HEAD // 2
-    frequency = rope_base ** (-(jnp.arange(half_dim, dtype=f32) * 2.0 / HEAD))
+    lane = jnp.arange(LANES)
+    frequency = rope_base ** (-((lane % HALF).astype(f32) * 2.0 / HEAD))
     angles = positions.astype(f32)[:, None] * frequency[None, :]
-    cosine = jnp.tile(jnp.cos(angles), (1, 4))
-    sine = jnp.tile(jnp.concatenate([-jnp.sin(angles), jnp.sin(angles)], axis=1), (1, 2))
-
-    packed_full, attn_tokens, moe_own, members, code, cosine, sine = together(
-        packed_full, attn_tokens, moe_own, members, code, cosine, sine
-    )
-    qkv_full, out_full = packed_full[:, :wide], packed_full[:, wide:]
-    bunch = min(2, owned)
+    cosine = jnp.cos(angles)
+    sine = jnp.sin(angles) * jnp.where(lane % HEAD < HALF, -1.0, 1.0)[None, :]
+
+    later_y = [swap(give_y[:, e : e + 1], "y") for e in range(bunch, owned)]
+    out_y = stacked(out_z, swap(out_z, "y"), y_first)
+    qkv_full, attn_tokens, moe_own, first_members, code, cosine, sine, out_y, *later_y = together(
+        qkv_full, attn_tokens, moe_own, first_members, code, cosine, sine, out_y, *later_y
+    )
+    qkv_pre = jnp.dot(attn_tokens, qkv_full, preferred_element_type=f32)
+    qkv_pre, moe_own, code_y = together(qkv_pre, moe_own, swap(code, "y"))
+    members = [first_members] + [
+        gather_members(own_y[:, e : e + 1], item)
+        for e, item in zip(range(bunch, owned), later_y)
+    ]
     weights, launched = [], None
-    for start, stop in [(0, bunch)] + [(e, e + 1) for e in range(bunch, owned)]:
-        item = members[start:stop]
+    for item in members:
         if launched is not None:
             item = after(item, launched)
         launched = item
-        item = lax.all_gather(item, "z", axis=0, tiled=False)
-        weights += [(item, e) for e in range(stop - start)]
-
-    qkv_pre = jnp.dot(attn_tokens, qkv_full, preferred_element_type=f32)
-    qkv_pre, moe_own, code_y = together(qkv_pre, moe_own, swap(code, "y"))
+        gathered = lax.all_gather(item, "z", axis=0, tiled=False)
+        weights += [(gathered, e) for e in range(item.shape[0])]
+    out_other = swap(out_y, "core")
     moe_across = swap(moe_own, "y")
     attn_mixed, qkv_rot, log_totals = attention_forward(qkv_pre, cosine, sine)
+    attn_mixed, out_other = together(attn_mixed, out_other)
+    out_full = jnp.stack(
+        [jnp.where(core_first, out_y, out_other), jnp.where(core_first, out_other, out_y)], 2
+    ).reshape(width, -1)
     attn_out = scatter_rows(contract(attn_mixed, out_full, 1, 1), tensor_size)
     codes = jnp.stack([code, code_y, swap(code, "core"), swap(code_y, "core")])
-    attn_out, moe_across, codes = together(attn_out, moe_across, codes)
+    attn_out, moe_across, codes, _ = together(attn_out, moe_across, codes, launched)
     moe_grad = jnp.stack([moe_own, moe_across, swap(moe_own, "core"), swap(moe_across, "core")])
     hidden_state = input_rows + residual_scale * attn_out
     ffn_normed = (hidden_state * row_scale(hidden_state) * ffn_gain).astype(bf16)

time: 602 us -> 597 us (level)
  waiting for transfers between devices: 202 us -> 185 us
  starting transfers between devices: 42.1 us -> 51.6 us
  other arithmetic: 75.7 us -> 82.9 us
    ppermute x42 -> x50, waiting for transfers between devices: 179 us -> 159 us  [swap(): return lax.ppermute(values, axis, [(0, 1), (1, 0)])]
    ppermute x42 -> x50, starting transfers between devices: 33.2 us -> 36.9 us  [swap(): return lax.ppermute(values, axis, [(0, 1), (1, 0)])]
  transfers between devices with their start and end apart: 55 -> 65, of which waited for: 31 -> 33; matrix products, arithmetic and copies ran while one was open for 18% -> 20% of each run, Pallas kernels for 35% -> 35%
where the time goes in v6:
time: 597 us; the launch traced here: 592 us
  Pallas kernels  208 us (35%)
  waiting for transfers between devices  185 us (31%)
  other arithmetic  82.9 us (14%)
  starting transfers between devices  51.6 us (9%)
  local copies, waits for them, and re-layouts  26.2 us (4%)
  matrix products  22.1 us (4%)
  between operations  15.8 us (3%)
    pallas_call x4, Pallas kernels, run_expert(): pl.pallas_call(functools.partial(expert_kernel, bool(carry), bool(shared)...  164 us
    ppermute x50, waiting for transfers between devices, swap(): return lax.ppermute(values, axis, [(0, 1), (1, 0)])  159 us
    ppermute x50, starting transfers between devices, swap(): return lax.ppermute(values, axis, [(0, 1), (1, 0)])  36.9 us
    pallas_call x1, Pallas kernels, attention_backward(): pl.pallas_call(attention_backward_kernel, grid=(groups,), in_specs=[wide,...  26.6 us
    ppermute x2, waiting for transfers between devices, shards(): small = small + lax.ppermute(small, 'z', z_pairs(step))  17.8 us
    pallas_call x1, Pallas kernels, attention_forward(): pl.pallas_call(attention_forward_kernel, grid=(groups,), in_specs=[wide,...  17.5 us
  transfers between devices with their start and end apart: 65, of which 33 were waited for; matrix products, arithmetic and copies ran while one was open for 20% of the time, Pallas kernels for 35%

profile of v6, /device:TPU:0, one launch (start us, length us, event | category | flops | bytes accessed | tf_op | source)
XLA Modules:
  0.0 591.6 jit_solution(8753053654065102396)
XLA Ops:
  9.9 3.1 collective-permute-start.5
  26.7 3.1 fusion.38
  34.3 7.1 %collective-permute-done = bf16[512,1024]{1,0:T(8,128)(2,1)} collective-permute-done((bf16[512,1024]{1,0:T(8,128)(2,1)}, bf16[512,1024]{1,0:T(8,128)(2,1)}, u32[]{:S(2)}, u32[]{:S(2)}) %collective-permute-start) | collective-permute-done | bytes 1048608 | tf_op jit(solution)/shard_map/ppermute | solution.py:58
  48.0 10.5 %collective-permute-done.3 = bf16[2,2,96,1024]{3,2,1,0:T(8,128)(2,1)} collective-permute-done((bf16[2,2,96,1024]{3,2,1,0:T(8,128)(2,1)}, bf16[2,2,96,1024]{3,2,1,0:T(8,128)(2,1)}, u32[]{:S(2)}, u32[]{:S(2)}) %collective-permute-start.3) | collective-permute-done | bytes 786464 | tf_op jit(solution)/shard_map/ppermute | solution.py:58
  75.3 6.6 %fusion.86.pre_ref = f32[1024,1024]{1,0:T(8,128)} fusion(bf16[1024,1024]{1,0:T(8,128)(2,1)} %pad_maximum_fusion.3, bf16[1024,1024]{1,0:T(8,128)(2,1)} %all-gather.8.cloned.1.call-done), kind=kOutput, calls=%fused_computation.249 | convolution fusion | flops 2147483648 | bytes 8388608 | tf_op jit(solution)/shard_map/dot_general | solution.py:543
  82.5 17.5 %attention_forward.1 = (bf16[1024,512]{1,0:T(8,128)(2,1)}, bf16[1024,1024]{1,0:T(8,128)(2,1)}, f32[1024,512]{1,0:T(8,128)}) custom-call(f32[1024,1024]{1,0:T(8,128)} %fusion.86.pre_ref, f32[1024,128]{1,0:T(8,128)} %get-tuple-element.103.cos_ref, f32[1024,128]{1,0:T(8,128)} %get-tuple-element.104.sin_ref), custom_call_target="tpu_custom_call" | custom-call | flops 3221225472 | bytes 10485760 | tf_op jit(solution)/shard_map/attention_forward/pallas_call | solution.py:260
  111.1 3.0 collective-permute-done.15
  115.0 14.6 %collective-permute-done.12 = bf16[512,1024]{1,0:T(8,128)(2,1)} collective-permute-done((bf16[512,1024]{1,0:T(8,128)(2,1)}, bf16[512,1024]{1,0:T(8,128)(2,1)}, u32[]{:S(2)}, u32[]{:S(2)}) %collective-permute-start.12) | collective-permute-done | bytes 1048608 | tf_op jit(solution)/shard_map/ppermute | solution.py:58
  136.4 7.2 %pad_maximum_fusion.grad_ref = bf16[4,1024,1024]{2,1,0:T(8,128)(2,1)} fusion(bf16[1,1024,1024]{2,1,0:T(8,128)(2,1)} %bitcast.44, bf16[1,1024,1024]{2,1,0:T(8,128)(2,1)} %bitcast.43, bf16[1,1024,1024]{2,1,0:T(8,128)(2,1)} %bitcast.42, bf16[1,1024,1024]{2,1,0:T(8,128)(2,1)} %bitcast.41), kind=kLoop, calls=%fused_computation.1 | loop fusion | flops 12582912 | bytes 16777216 | tf_op jit(solution)/shard_map/stack | solution.py:566
  143.6 14.9 %collective-permute-done.21 = bf16[512,1024]{1,0:T(8,128)(2,1)S(1)} collective-permute-done((bf16[512,1024]{1,0:T(8,128)(2,1)S(1)}, bf16[512,1024]{1,0:T(8,128)(2,1)S(1)}, u32[]{:S(2)}, u32[]{:S(2)}) %collective-permute-start.21) | collective-permute-done | bytes 1048608 | tf_op jit(solution)/shard_map/ppermute | solution.py:58
  162.2 13.1 %collective-permute-done.24 = bf16[256,1024]{1,0:T(8,128)(2,1)S(1)} collective-permute-done((bf16[256,1024]{1,0:T(8,128)(2,1)S(1)}, bf16[256,1024]{1,0:T(8,128)(2,1)S(1)}, u32[]{:S(2)}, u32[]{:S(2)}) %collective-permute-start.24) | collective-permute-done | bytes 524320 | tf_op jit(solution)/shard_map/ppermute | solution.py:58
  180.9 3.5 collective-permute-done.27
  184.4 3.8 pad_maximum_fusion.1.tokens_ref
  193.5 39.3 %expert.4 = (bf16[4,1024,1024]{2,1,0:T(8,128)(2,1)}, bf16[4,1024,1024]{2,1,0:T(8,128)(2,1)}, f32[4,1,1024]{2,1,0:T(1,128)}, bf16[4,2,4,96,1024]{4,3,2,1,0:T(8,128)(2,1)}) custom-call(s32[1]{0:T(128)} %bitcast.40.member_ref, bf16[4,1024,1024]{2,1,0:T(8,128)(2,1)} %copy-done.5, bf16[4,1024,1024]{2,1,0:T(8,128)(2,1)} %pad_maximum_fusion.grad_ref, ...), custom_call_target="tpu_custom_call" | custom-call | flops 22817013760 | bytes 56623104 | tf_op jit(solution)/shard_map/expert/pallas_call | solution.py:407
  232.8 40.3 %expert.5 = (bf16[4,1024,1024]{2,1,0:T(8,128)(2,1)}, bf16[4,1024,1024]{2,1,0:T(8,128)(2,1)}, f32[4,1,1024]{2,1,0:T(1,128)}, bf16[4,2,4,96,1024]{4,3,2,1,0:T(8,128)(2,1)}) custom-call(s32[1]{0:T(128)} %bitcast.40.member_ref, bf16[4,1024,1024]{2,1,0:T(8,128)(2,1)} %copy-done.5, ...), custom_call_target="tpu_custom_call", output_to_operand_aliasing={{3}: (8, {})} | custom-call | flops 22817013760 | bytes 56623104 | tf_op jit(solution)/shard_map/expert/pallas_call | solution.py:407
  273.2 41.1 %expert.6 = (bf16[4,1024,1024]{2,1,0:T(8,128)(2,1)}, bf16[4,1024,1024]{2,1,0:T(8,128)(2,1)}, f32[4,1,1024]{2,1,0:T(1,128)}, bf16[4,2,4,96,1024]{4,3,2,1,0:T(8,128)(2,1)}) custom-call(s32[1]{0:T(128)} %bitcast.40.member_ref, bf16[4,1024,1024]{2,1,0:T(8,128)(2,1)} %copy-done.5, bf16[4,1024,1024]{2,1,0:T(8,128)(2,1)} %pad_maximum_fusion.grad_ref, ...), custom_call_target="tpu_custom_call" | custom-call | flops 22817013760 | bytes 56623104 | tf_op jit(solution)/shard_map/expert/pallas_call | solution.py:407
  315.4 42.9 %expert.7 = (bf16[3,1024,1024]{2,1,0:T(8,128)(2,1)}, bf16[2,1024,1024]{2,1,0:T(8,128)(2,1)}, bf16[3,1024,1024]{2,1,0:T(8,128)(2,1)}, bf16[2,1024,1024]{2,1,0:T(8...) custom-call(s32[1]{0:T(128)} %bitcast.40.member_ref, ...), custom_call_target="tpu_custom_call", output_to_operand_aliasing={{5}: (8, {})} | custom-call | flops 22817013760 | bytes 56623104 | tf_op jit(solution)/shard_map/expert/pallas_call | solution.py:407
  373.9 3.1 convert_add_fusion.3
  378.3 7.4 %collective-permute-done.35 = bf16[256,1024]{1,0:T(8,128)(2,1)S(1)} collective-permute-done((bf16[256,1024]{1,0:T(8,128)(2,1)S(1)}, bf16[256,1024]{1,0:T(8,128)(2,1)S(1)}, u32[]{:S(2)}, u32[]{:S(2)}) %collective-permute-start.35) | collective-permute-done | bytes 524320 | tf_op jit(solution)/shard_map/ppermute | solution.py:58
  389.7 8.8 %collective-permute-done.32 = bf16[256,1024]{1,0:T(8,128)(2,1)S(1)} collective-permute-done((bf16[256,1024]{1,0:T(8,128)(2,1)S(1)}, bf16[256,1024]{1,0:T(8,128)(2,1)S(1)}, u32[]{:S(2)}, u32[]{:S(2)}) %collective-permute-start.32) | collective-permute-done | bytes 524320 | tf_op jit(solution)/shard_map/ppermute | solution.py:58
  398.4 10.5 %collective-permute-done.36 = bf16[256,1024]{1,0:T(8,128)(2,1)S(1)} collective-permute-done((bf16[256,1024]{1,0:T(8,128)(2,1)S(1)}, bf16[256,1024]{1,0:T(8,128)(2,1)S(1)}, u32[]{:S(2)}, u32[]{:S(2)}) %collective-permute-start.36) | collective-permute-done | bytes 524320 | tf_op jit(solution)/shard_map/ppermute | solution.py:58
  421.1 3.0 fusion.26
  424.1 15.3 %collective-permute-done.39 = bf16[512,1024]{1,0:T(8,128)(2,1)} collective-permute-done((bf16[512,1024]{1,0:T(8,128)(2,1)S(1)}, bf16[512,1024]{1,0:T(8,128)(2,1)}, u32[]{:S(2)}, u32[]{:S(2)}) %collective-permute-start.39) | collective-permute-done | bytes 1048608 | tf_op jit(solution)/shard_map/ppermute | solution.py:58
  453.2 26.6 %attention_backward.1 = bf16[1024,1024]{1,0:T(8,128)(2,1)} custom-call(bf16[1024,1024]{1,0:T(8,128)(2,1)} %get-tuple-element.154.rot_ref, bf16[1024,512]{1,0:T(8,128)(2,1)} %convolution_convert_fusion.grad_ref, f32[1024,512]{1,0:T(8,128)} %get-tuple-element.159.lse_ref, f32[1024,128]{1,0:T(8,128)} %get-tuple-element.103.cos_ref, ...), custom_call_target="tpu_custom_call" | custom-call | flops 8589934592 | bytes 10485760 | tf_op jit(solution)/shard_map/attention_backward/pallas_call | solution.py:284
  492.2 9.3 %collective-permute-done.46 = bf16[2,2,96,1024]{3,2,1,0:T(8,128)(2,1)S(1)} collective-permute-done((bf16[2,2,96,1024]{3,2,1,0:T(8,128)(2,1)S(1)}, bf16[2,2,96,1024]{3,2,1,0:T(8,128)(2,1)S(1)}, u32[]{:S(2)}, u32[]{:S(2)}) %collective-permute-start.46) | collective-permute-done | bytes 786464 | tf_op jit(solution)/shard_map/ppermute | solution.py:58
  502.9 11.2 %collective-permute-done.43 = bf16[512,1024]{1,0:T(8,128)(2,1)S(1)} collective-permute-done((bf16[512,1024]{1,0:T(8,128)(2,1)S(1)}, bf16[512,1024]{1,0:T(8,128)(2,1)S(1)}, u32[]{:S(2)}, u32[]{:S(2)}) %collective-permute-start.43) | collective-permute-done | bytes 1048608 | tf_op jit(solution)/shard_map/ppermute | solution.py:58
  521.5 3.0 collective-permute-done.48
  525.4 10.8 %collective-permute-done.49 = bf16[4,64,1024]{2,1,0:T(8,128)(2,1)S(1)} collective-permute-done((bf16[4,64,1024]{2,1,0:T(8,128)(2,1)S(1)}, bf16[4,64,1024]{2,1,0:T(8,128)(2,1)S(1)}, u32[]{:S(2)}, u32[]{:S(2)}) %collective-permute-start.49) | collective-permute-done | bytes 524320 | tf_op jit(solution)/shard_map/ppermute | solution.py:58
  544.3 4.2 fusion.19
  548.4 7.8 %collective-permute-done.54 = f32[34,1024]{1,0:T(8,128)S(1)} collective-permute-done((f32[34,1024]{1,0:T(8,128)S(1)}, f32[34,1024]{1,0:T(8,128)S(1)}, u32[]{:S(2)}, u32[]{:S(2)}) %collective-permute-start.54) | collective-permute-done | bytes 139296 | tf_op jit(solution)/shard_map/ppermute | solution.py:716
  556.8 3.0 collective-permute-start.56
  561.5 10.1 %collective-permute-done.56 = f32[34,1024]{1,0:T(8,128)S(1)} collective-permute-done((f32[34,1024]{1,0:T(8,128)S(1)}, f32[34,1024]{1,0:T(8,128)S(1)}, u32[]{:S(2)}, u32[]{:S(2)}) %collective-permute-start.56) | collective-permute-done | bytes 139296 | tf_op jit(solution)/shard_map/ppermute | solution.py:716
  (344 shorter events, 170.3 us)
Async XLA Ops:
  7.2 66.3 %all-gather.8.cloned.1.call-start = ((), (), s32[]{:S(2)}) async-start(), calls=%async_computation.2 | async-start | bytes 2228224 | tf_op jit(solution)/shard_map/all_gather | solution.py:483
  9.9 183.6 %all-gather.14.cloned.1.call-start = ((), (), s32[]{:S(2)}) async-start(), calls=%async_computation.7 | async-start | bytes 7864320 | tf_op jit(solution)/shard_map/all_gather | solution.py:554
  9.9 21.7 %collective-permute-start.5 = (bf16[1,64,512]{2,1,0:T(8,128)(2,1)}, bf16[1,64,512]{2,1,0:T(8,128)(2,1)S(1)}, u32[]{:S(2)}, u32[]{:S(2)}) collective-permute-start(bf16[1,64,512]{2,1,0:T(8,128)(2,1)} %bitcast.290), channel_id=1, source_target_pairs={{0,8},{8,0},{16,24},{24,16},{1,9},{9,1},{17,25},{25,17},{2,10},{10... | collective-permute-start | bytes 196616 | tf_op jit(solution)/shard_map/ppermute | solution.py:487
  16.6 24.9 %collective-permute-start = (bf16[512,1024]{1,0:T(8,128)(2,1)}, bf16[512,1024]{1,0:T(8,128)(2,1)}, u32[]{:S(2)}, u32[]{:S(2)}) collective-permute-start(bf16[512,1024]{1,0:T(8,128)(2,1)} %fusion.7), channel_id=1, source_target_pairs={{0,1},{1,0},{2,3},{3,2},{4,5},{5,4},{6,7},{7,6},{8,9},{9,8},{10,11... | collective-permute-start | bytes 3145736 | tf_op jit(solution)/shard_map/ppermute | solution.py:58
  22.0 42.4 %collective-permute-start.2 = (bf16[2,96,1024]{2,1,0:T(8,128)(2,1)}, bf16[2,96,1024]{2,1,0:T(8,128)(2,1)}, u32[]{:S(2)}, u32[]{:S(2)}) collective-permute-start(bf16[2,96,1024]{2,1,0:T(8,128)(2,1)} %get-tuple-element.228), channel_id=1, source_target_pairs={{0,2},{2,0},{1,3},{3,1},{4,6},{6,4},{5,7},{7,5},{8,10},{10,8},{9,1... | collective-permute-start | bytes 1179656 | tf_op jit(solution)/shard_map/ppermute | solution.py:58
  23.7 48.5 %collective-permute-start.9 = (bf16[2,1,96,1024]{3,2,1,0:T(8,128)(2,1)}, bf16[2,1,96,1024]{3,2,1,0:T(8,128)(2,1)}, u32[]{:S(2)}, u32[]{:S(2)}) collective-permute-start(bf16[2,1,96,1024]{3,2,1,0:T(8,128)(2,1)} %get-tuple-element.221), channel_id=1, source_target_pairs={{0,4},{4,0},{1,5},{5,1},{2,6},{6,2},{3,7},{7,3},{8,12},{12,8},{9,1... | collective-permute-start | bytes 1179656 | tf_op jit(solution)/shard_map/ppermute | solution.py:58
  26.2 32.3 %collective-permute-start.3 = (bf16[2,2,96,1024]{3,2,1,0:T(8,128)(2,1)}, bf16[2,2,96,1024]{3,2,1,0:T(8,128)(2,1)}, u32[]{:S(2)}, u32[]{:S(2)}) collective-permute-start(bf16[2,2,96,1024]{3,2,1,0:T(8,128)(2,1)} %slice.225), channel_id=1, source_target_pairs={{0,4},{4,0},{1,5},{5,1},{2,6},{6,2},{3,7},{7,3},{8,12},{12,8},{9,1... | collective-permute-start | bytes 2359304 | tf_op jit(solution)/shard_map/ppermute | solution.py:58
  44.8 24.1 %collective-permute-start.1 = (bf16[512,1024]{1,0:T(8,128)(2,1)}, bf16[512,1024]{1,0:T(8,128)(2,1)}, u32[]{:S(2)}, u32[]{:S(2)}) collective-permute-start(bf16[512,1024]{1,0:T(8,128)(2,1)} %fusion.6), channel_id=1, source_target_pairs={{0,1},{1,0},{2,3},{3,2},{4,5},{5,4},{6,7},{7,6},{8,9},{9,8},{10,11... | collective-permute-start | bytes 3145736 | tf_op jit(solution)/shard_map/ppermute | solution.py:58
  73.5 199.7 %all-gather.12.cloned.1.call-start = ((), (), s32[]{:S(2)}) async-start(), calls=%async_computation.6 | async-start | bytes 3932160 | tf_op jit(solution)/shard_map/all_gather | solution.py:554
  75.3 24.7 %collective-permute-start.11 = (bf16[4,2,64,512]{3,2,1,0:T(8,128)(2,1)S(1)}, bf16[4,2,64,512]{3,2,1,0:T(8,128)(2,1)}, u32[]{:S(2)}, u32[]{:S(2)}) collective-permute-start(bf16[4,2,64,512]{3,2,1,0:T(8,128)(2,1)S(1)} %pad_maximum_fusion.16), channel_id=1, source_target_pairs={{0,2},{2,0},{1,3},{3,1},{4,6},{6,4},{5,7},{7,5},{8,10},{10,8},{9,1... | collective-permute-start | bytes 1572872 | tf_op jit(solution)/shard_map/ppermute | solution.py:58
  81.9 49.9 %collective-permute-start.13 = (bf16[1024,1024]{1,0:T(8,128)(2,1)}, bf16[1024,1024]{1,0:T(8,128)(2,1)}, u32[]{:S(2)}, u32[]{:S(2)}) collective-permute-start(bf16[1024,1024]{1,0:T(8,128)(2,1)} %pad_maximum_fusion.4), channel_id=1, source_target_pairs={{0,4},{4,0},{1,5},{5,1},{2,6},{6,2},{3,7},{7,3},{8,12},{12,8},{9,1... | collective-permute-start | bytes 6291464 | tf_op jit(solution)/shard_map/ppermute | solution.py:58
  104.0 25.6 %collective-permute-start.12 = (bf16[512,1024]{1,0:T(8,128)(2,1)}, bf16[512,1024]{1,0:T(8,128)(2,1)}, u32[]{:S(2)}, u32[]{:S(2)}) collective-permute-start(bf16[512,1024]{1,0:T(8,128)(2,1)} %dynamic-slice_convert_fusion.1), channel_id=1, source_target_pairs={{0,1},{1,0},{2,3},{3,2},{4,5},{5,4},{6,7},{7,6},{8,9},{9,8},{10,11... | collective-permute-start | bytes 3145736 | tf_op jit(solution)/shard_map/ppermute | solution.py:58
  109.6 25.5 %collective-permute-start.22 = (bf16[1024,1024]{1,0:T(8,128)(2,1)}, bf16[1024,1024]{1,0:T(8,128)(2,1)}, u32[]{:S(2)}, u32[]{:S(2)}) collective-permute-start(bf16[1024,1024]{1,0:T(8,128)(2,1)} %pad_maximum_fusion.4), channel_id=1, source_target_pairs={{0,2},{2,0},{1,3},{3,1},{4,6},{6,4},{5,7},{7,5},{8,10},{10,8},{9,1... | collective-permute-start | bytes 6291464 | tf_op jit(solution)/shard_map/ppermute | solution.py:58
  131.9 183.5 %all-gather.10.cloned.1.call-start = ((), (), s32[]{:S(2)}) async-start(), calls=%async_computation.5 | async-start | bytes 3932160 | tf_op jit(solution)/shard_map/all_gather | solution.py:554
  132.9 25.6 %collective-permute-start.21 = (bf16[512,1024]{1,0:T(8,128)(2,1)S(1)}, bf16[512,1024]{1,0:T(8,128)(2,1)S(1)}, u32[]{:S(2)}, u32[]{:S(2)}) collective-permute-start(bf16[512,1024]{1,0:T(8,128)(2,1)S(1)} %multiply_convert_fusion.1), channel_id=1, source_target_pairs={{0,4},{4,0},{1,5},{5,1},{2,6},{6,2},{3,7},{7,3},{8,12},{12,8},{9,1... | collective-permute-start | bytes 3145736 | tf_op jit(solution)/shard_map/ppermute | solution.py:58
  134.4 25.3 %collective-permute-start.20 = (bf16[512,1024]{1,0:T(8,128)(2,1)S(1)}, bf16[512,1024]{1,0:T(8,128)(2,1)S(1)}, u32[]{:S(2)}, u32[]{:S(2)}) collective-permute-start(bf16[512,1024]{1,0:T(8,128)(2,1)S(1)} %multiply_convert_fusion.1), channel_id=1, source_target_pairs={{0,1},{1,0},{2,3},{3,2},{4,5},{5,4},{6,7},{7,6},{8,9},{9,8},{10,11... | collective-permute-start | bytes 3145736 | tf_op jit(solution)/shard_map/ppermute | solution.py:58
  179.9 269.6 %reduce-scatter.3.cloned.1.call-start = ((), (), s32[]{:S(2)}) async-start(), calls=%async_computation.3 | async-start | bytes 7864320 | tf_op jit(solution)/shard_map/reduce_scatter | solution.py:599
  273.1 267.4 %reduce-scatter.5.cloned.1.call-start = ((), (), s32[]{:S(2)}) async-start(), calls=%async_computation.4 | async-start | bytes 7864320 | tf_op jit(solution)/shard_map/reduce_scatter | solution.py:599
  368.7 42.7 %collective-permute-start.38 = (bf16[2,1024,1024]{2,1,0:T(8,128)(2,1)}, bf16[2,1024,1024]{2,1,0:T(8,128)(2,1)}, u32[]{:S(2)}, u32[]{:S(2)}) collective-permute-start(bf16[2,1024,1024]{2,1,0:T(8,128)(2,1)} %get-tuple-element.151), channel_id=1, source_target_pairs={{0,2},{2,0},{1,3},{3,1},{4,6},{6,4},{5,7},{7,5},{8,10},{10,8},{9,1... | collective-permute-start | bytes 12582920 | tf_op jit(solution)/shard_map/ppermute | solution.py:58
  377.0 21.4 %collective-permute-start.32 = (bf16[256,1024]{1,0:T(8,128)(2,1)S(1)}, bf16[256,1024]{1,0:T(8,128)(2,1)S(1)}, u32[]{:S(2)}, u32[]{:S(2)}) collective-permute-start(bf16[256,1024]{1,0:T(8,128)(2,1)S(1)} %fusion.41), channel_id=1, source_target_pairs={{0,1},{1,0},{2,3},{3,2},{4,5},{5,4},{6,7},{7,6},{8,9},{9,8},{10,11... | collective-permute-start | bytes 1572872 | tf_op jit(solution)/shard_map/ppermute | solution.py:58
  377.8 20.6 %collective-permute-start.33 = (bf16[256,1024]{1,0:T(8,128)(2,1)S(1)}, bf16[256,1024]{1,0:T(8,128)(2,1)S(1)}, u32[]{:S(2)}, u32[]{:S(2)}) collective-permute-start(bf16[256,1024]{1,0:T(8,128)(2,1)S(1)} %fusion.42), channel_id=1, source_target_pairs={{0,4},{4,0},{1,5},{5,1},{2,6},{6,2},{3,7},{7,3},{8,12},{12,8},{9,1... | collective-permute-start | bytes 1572872 | tf_op jit(solution)/shard_map/ppermute | solution.py:58
  387.5 21.4 %collective-permute-start.36 = (bf16[256,1024]{1,0:T(8,128)(2,1)S(1)}, bf16[256,1024]{1,0:T(8,128)(2,1)S(1)}, u32[]{:S(2)}, u32[]{:S(2)}) collective-permute-start(bf16[256,1024]{1,0:T(8,128)(2,1)S(1)} %fusion.31), channel_id=1, source_target_pairs={{0,1},{1,0},{2,3},{3,2},{4,5},{5,4},{6,7},{7,6},{8,9},{9,8},{10,11... | collective-permute-start | bytes 1572872 | tf_op jit(solution)/shard_map/ppermute | solution.py:58
  389.0 19.9 %collective-permute-start.37 = (bf16[256,1024]{1,0:T(8,128)(2,1)S(1)}, bf16[256,1024]{1,0:T(8,128)(2,1)S(1)}, u32[]{:S(2)}, u32[]{:S(2)}) collective-permute-start(bf16[256,1024]{1,0:T(8,128)(2,1)S(1)} %fusion.29), channel_id=1, source_target_pairs={{0,4},{4,0},{1,5},{5,1},{2,6},{6,2},{3,7},{7,3},{8,12},{12,8},{9,1... | collective-permute-start | bytes 1572872 | tf_op jit(solution)/shard_map/ppermute | solution.py:58
  414.7 24.6 %collective-permute-start.39 = (bf16[512,1024]{1,0:T(8,128)(2,1)S(1)}, bf16[512,1024]{1,0:T(8,128)(2,1)}, u32[]{:S(2)}, u32[]{:S(2)}) collective-permute-start(bf16[512,1024]{1,0:T(8,128)(2,1)S(1)} %get-tuple-element.187), channel_id=1, source_target_pairs={{0,1},{1,0},{2,3},{3,2},{4,5},{5,4},{6,7},{7,6},{8,9},{9,8},{10,11... | collective-permute-start | bytes 3145736 | tf_op jit(solution)/shard_map/ppermute | solution.py:58
  419.1 24.6 %collective-permute-start.40 = (bf16[512,1024]{1,0:T(8,128)(2,1)}, bf16[512,1024]{1,0:T(8,128)(2,1)}, u32[]{:S(2)}, u32[]{:S(2)}) collective-permute-start(bf16[512,1024]{1,0:T(8,128)(2,1)} %fusion.25), channel_id=1, source_target_pairs={{0,4},{4,0},{1,5},{5,1},{2,6},{6,2},{3,7},{7,3},{8,12},{12,8},{9,1... | collective-permute-start | bytes 3145736 | tf_op jit(solution)/shard_map/ppermute | solution.py:58
  446.2 78.4 %collective-permute-start.51 = (bf16[512,1024]{1,0:T(8,128)(2,1)S(1)}, bf16[512,1024]{1,0:T(8,128)(2,1)}, u32[]{:S(2)}, u32[]{:S(2)}) collective-permute-start(bf16[512,1024]{1,0:T(8,128)(2,1)S(1)} %fusion.15), channel_id=1, source_target_pairs={{0,1},{1,0},{2,3},{3,2},{4,5},{5,4},{6,7},{7,6},{8,9},{9,8},{10,11... | collective-permute-start | bytes 3145736 | tf_op jit(solution)/shard_map/ppermute | solution.py:58
  446.8 34.7 %collective-permute-start.41 = (bf16[512,1024]{1,0:T(8,128)(2,1)}, bf16[512,1024]{1,0:T(8,128)(2,1)}, u32[]{:S(2)}, u32[]{:S(2)}) collective-permute-start(bf16[512,1024]{1,0:T(8,128)(2,1)} %fusion.26), channel_id=1, source_target_pairs={{0,4},{4,0},{1,5},{5,1},{2,6},{6,2},{3,7},{7,3},{8,12},{12,8},{9,1... | collective-permute-start | bytes 3145736 | tf_op jit(solution)/shard_map/ppermute | solution.py:58
  453.2 26.6 %collective-permute-start.42 = (bf16[2,2,96,1024]{3,2,0,1:T(8,128)(2,1)}, bf16[2,2,96,1024]{3,2,0,1:T(8,128)(2,1)}, u32[]{:S(2)}, u32[]{:S(2)}) collective-permute-start(bf16[2,2,96,1024]{3,2,0,1:T(8,128)(2,1)} %slice_bitcast_fusion.4), channel_id=1, source_target_pairs={{0,2},{2,0},{1,3},{3,1},{4,6},{6,4},{5,7},{7,5},{8,10},{10,8},{9,1... | collective-permute-start | bytes 2359304 | tf_op jit(solution)/shard_map/ppermute | solution.py:58
  481.5 20.0 %collective-permute-start.46 = (bf16[2,2,96,1024]{3,2,1,0:T(8,128)(2,1)S(1)}, bf16[2,2,96,1024]{3,2,1,0:T(8,128)(2,1)S(1)}, u32[]{:S(2)}, u32[]{:S(2)}) collective-permute-start(bf16[2,2,96,1024]{3,2,1,0:T(8,128)(2,1)S(1)} %slice_bitcast_fusion.7), channel_id=1, source_target_pairs={{0,4},{4,0},{1,5},{5,1},{2,6},{6,2},{3,7},{7,3},{8,12},{12,8},{9,1... | collective-permute-start | bytes 2359304 | tf_op jit(solution)/shard_map/ppermute | solution.py:58
  488.5 25.6 %collective-permute-start.43 = (bf16[512,1024]{1,0:T(8,128)(2,1)S(1)}, bf16[512,1024]{1,0:T(8,128)(2,1)S(1)}, u32[]{:S(2)}, u32[]{:S(2)}) collective-permute-start(bf16[512,1024]{1,0:T(8,128)(2,1)S(1)} %dynamic-slice_convert_fusion), channel_id=1, source_target_pairs={{0,1},{1,0},{2,3},{3,2},{4,5},{5,4},{6,7},{7,6},{8,9},{9,8},{10,11... | collective-permute-start | bytes 3145736 | tf_op jit(solution)/shard_map/ppermute | solution.py:58
  490.2 24.4 %collective-permute-start.44 = (bf16[4,2,64,1024]{3,2,0,1:T(8,128)(2,1)S(1)}, bf16[4,2,64,1024]{3,2,0,1:T(8,128)(2,1)S(1)}, u32[]{:S(2)}, u32[]{:S(2)}) collective-permute-start(bf16[4,2,64,1024]{3,2,0,1:T(8,128)(2,1)S(1)} %fusion.27), channel_id=1, source_target_pairs={{0,2},{2,0},{1,3},{3,1},{4,6},{6,4},{5,7},{7,5},{8,10},{10,8},{9,1... | collective-permute-start | bytes 3145736 | tf_op jit(solution)/shard_map/ppermute | solution.py:58
  491.9 22.7 %collective-permute-start.45 = (bf16[4,2,64,512]{3,2,0,1:T(8,128)(2,1)S(1)}, bf16[4,2,64,512]{3,2,0,1:T(8,128)(2,1)S(1)}, u32[]{:S(2)}, u32[]{:S(2)}) collective-permute-start(bf16[4,2,64,512]{3,2,0,1:T(8,128)(2,1)S(1)} %fusion.40), channel_id=1, source_target_pairs={{0,2},{2,0},{1,3},{3,1},{4,6},{6,4},{5,7},{7,5},{8,10},{10,8},{9,1... | collective-permute-start | bytes 1572872 | tf_op jit(solution)/shard_map/ppermute | solution.py:58
  (78 other events, 943.2 us)
Sparse Core Ops, SparseCore 0:
  10.8 49.7 all-gather.7
  73.7 114.9 all-gather.13
  190.2 61.6 all-gather.11
  253.3 62.0 all-gather.9
  317.6 109.4 reduce-scatter.2
  429.2 111.2 reduce-scatter.4

commit v7 on v6

--- a/solution.py
+++ b/solution.py
@@ -175,14 +175,13 @@
     block = min(BLOCK, seq_len)
     for start in range(0, seq_len, block):
         stop = start + block
-        allowed = causal(block, stop, start)
         total = jnp.zeros((block, LANES), f32)
         lses = []
         for head in (0, 1):
             scores = (
                 contract(query[start:stop], keys[head][:stop], 1, 1) * attn_scale
             )
-            scores = jnp.where(allowed, scores, masked_score)
+            scores = causal_scores(scores, start)
             top = jnp.max(scores, axis=1, keepdims=True)
             raised = jnp.exp(scores - top)
             summed = jnp.sum(raised, axis=1, keepdims=True)
@@ -200,6 +199,12 @@
     keys = [jnp.where(low, kv, zero).astype(bf16), jnp.where(low, zero, turned).astype(bf16)]
     values_in = [jnp.where(low, turned, zero).astype(bf16), jnp.where(low, zero, kv).astype(bf16)]
     return keys, values_in
+
+
+def causal_scores(scores, start):
+    rows = scores.shape[0]
+    last = jnp.where(causal(rows, rows, 0), scores[:, start:], masked_score)
+    return last if start == 0 else jnp.concatenate([scores[:, :start], last], axis=1)
 
 
 def causal(rows, columns, start):
@@ -222,14 +227,13 @@
     block = min(BLOCK, seq_len)
     for start in range(0, seq_len, block):
         stop = start + block
-        allowed = causal(block, stop, start)
         query = rot_ref[start:stop, :LANES]
         grad = grad_ref[start:stop, :]
         query_grad = jnp.zeros((block, LANES), f32)
         for head in (0, 1):
             scores = contract(query, keys[head][:stop], 1, 1) * attn_scale
             log_total = lse_ref[start:stop, head * HEAD : head * HEAD + 1]
-            prob = jnp.where(allowed, jnp.exp(jnp.where(allowed, scores - log_total, 0.0)), 0.0)
+            prob = jnp.exp(causal_scores(scores, start) - log_total)
             prob_grad = contract(grad, values_in[head][:stop], 1, 1)
             row_dot = jnp.sum(prob * prob_grad, axis=1, keepdims=True)
             score_grad = (prob * (prob_grad - row_dot)).astype(bf16)

time: 597 us -> 597 us (level)
  no operation moved by 1% of the time
where the time goes in v7:
time: 597 us; the launch traced here: 592 us
  Pallas kernels  208 us (35%)
  waiting for transfers between devices  185 us (31%)
  other arithmetic  82.9 us (14%)
  starting transfers between devices  51.6 us (9%)
  local copies, waits for them, and re-layouts  26.2 us (4%)
  matrix products  22.1 us (4%)
  between operations  15.8 us (3%)
    pallas_call x4, Pallas kernels, run_expert(): pl.pallas_call(functools.partial(expert_kernel, bool(carry), bool(shared)...  164 us
    ppermute x50, waiting for transfers between devices, swap(): return lax.ppermute(values, axis, [(0, 1), (1, 0)])  159 us
    ppermute x50, starting transfers between devices, swap(): return lax.ppermute(values, axis, [(0, 1), (1, 0)])  36.8 us
    pallas_call x1, Pallas kernels, attention_backward(): pl.pallas_call(attention_backward_kernel, grid=(groups,), in_specs=[wide,...  26.6 us
    ppermute x2, waiting for transfers between devices, shards(): small = small + lax.ppermute(small, 'z', z_pairs(step))  17.8 us
    pallas_call x1, Pallas kernels, attention_forward(): pl.pallas_call(attention_forward_kernel, grid=(groups,), in_specs=[wide,...  17.5 us
  transfers between devices with their start and end apart: 65, of which 33 were waited for; matrix products, arithmetic and copies ran while one was open for 20% of the time, Pallas kernels for 35%

profile of v7, /device:TPU:0, one launch (start us, length us, event | category | flops | bytes accessed | tf_op | source)
XLA Modules:
  0.0 591.6 jit_solution(10065183241504414418)
XLA Ops:
  9.9 3.1 collective-permute-start.5
  26.7 3.1 fusion.38
  34.3 7.1 %collective-permute-done = bf16[512,1024]{1,0:T(8,128)(2,1)} collective-permute-done((bf16[512,1024]{1,0:T(8,128)(2,1)}, bf16[512,1024]{1,0:T(8,128)(2,1)}, u32[]{:S(2)}, u32[]{:S(2)}) %collective-permute-start) | collective-permute-done | bytes 1048608 | tf_op jit(solution)/shard_map/ppermute | solution.py:58
  48.0 10.5 %collective-permute-done.3 = bf16[2,2,96,1024]{3,2,1,0:T(8,128)(2,1)} collective-permute-done((bf16[2,2,96,1024]{3,2,1,0:T(8,128)(2,1)}, bf16[2,2,96,1024]{3,2,1,0:T(8,128)(2,1)}, u32[]{:S(2)}, u32[]{:S(2)}) %collective-permute-start.3) | collective-permute-done | bytes 786464 | tf_op jit(solution)/shard_map/ppermute | solution.py:58
  75.3 6.6 %fusion.86.pre_ref = f32[1024,1024]{1,0:T(8,128)} fusion(bf16[1024,1024]{1,0:T(8,128)(2,1)} %pad_maximum_fusion.3, bf16[1024,1024]{1,0:T(8,128)(2,1)} %all-gather.8.cloned.1.call-done), kind=kOutput, calls=%fused_computation.249 | convolution fusion | flops 2147483648 | bytes 8388608 | tf_op jit(solution)/shard_map/dot_general | solution.py:547
  82.5 17.5 %attention_forward.1 = (bf16[1024,512]{1,0:T(8,128)(2,1)}, bf16[1024,1024]{1,0:T(8,128)(2,1)}, f32[1024,512]{1,0:T(8,128)}) custom-call(f32[1024,1024]{1,0:T(8,128)} %fusion.86.pre_ref, f32[1024,128]{1,0:T(8,128)} %get-tuple-element.103.cos_ref, f32[1024,128]{1,0:T(8,128)} %get-tuple-element.104.sin_ref), custom_call_target="tpu_custom_call" | custom-call | flops 3221225472 | bytes 10485760 | tf_op jit(solution)/shard_map/attention_forward/pallas_call | solution.py:264
  111.1 3.0 collective-permute-done.15
  115.0 14.6 %collective-permute-done.12 = bf16[512,1024]{1,0:T(8,128)(2,1)} collective-permute-done((bf16[512,1024]{1,0:T(8,128)(2,1)}, bf16[512,1024]{1,0:T(8,128)(2,1)}, u32[]{:S(2)}, u32[]{:S(2)}) %collective-permute-start.12) | collective-permute-done | bytes 1048608 | tf_op jit(solution)/shard_map/ppermute | solution.py:58
  136.3 7.2 %pad_maximum_fusion.grad_ref = bf16[4,1024,1024]{2,1,0:T(8,128)(2,1)} fusion(bf16[1,1024,1024]{2,1,0:T(8,128)(2,1)} %bitcast.44, bf16[1,1024,1024]{2,1,0:T(8,128)(2,1)} %bitcast.43, bf16[1,1024,1024]{2,1,0:T(8,128)(2,1)} %bitcast.42, bf16[1,1024,1024]{2,1,0:T(8,128)(2,1)} %bitcast.41), kind=kLoop, calls=%fused_computation.1 | loop fusion | flops 12582912 | bytes 16777216 | tf_op jit(solution)/shard_map/stack | solution.py:570
  143.5 14.9 %collective-permute-done.21 = bf16[512,1024]{1,0:T(8,128)(2,1)S(1)} collective-permute-done((bf16[512,1024]{1,0:T(8,128)(2,1)S(1)}, bf16[512,1024]{1,0:T(8,128)(2,1)S(1)}, u32[]{:S(2)}, u32[]{:S(2)}) %collective-permute-start.21) | collective-permute-done | bytes 1048608 | tf_op jit(solution)/shard_map/ppermute | solution.py:58
  162.1 13.1 %collective-permute-done.24 = bf16[256,1024]{1,0:T(8,128)(2,1)S(1)} collective-permute-done((bf16[256,1024]{1,0:T(8,128)(2,1)S(1)}, bf16[256,1024]{1,0:T(8,128)(2,1)S(1)}, u32[]{:S(2)}, u32[]{:S(2)}) %collective-permute-start.24) | collective-permute-done | bytes 524320 | tf_op jit(solution)/shard_map/ppermute | solution.py:58
  180.8 3.5 collective-permute-done.27
  184.3 3.8 pad_maximum_fusion.1.tokens_ref
  193.5 39.3 %expert.4 = (bf16[4,1024,1024]{2,1,0:T(8,128)(2,1)}, bf16[4,1024,1024]{2,1,0:T(8,128)(2,1)}, f32[4,1,1024]{2,1,0:T(1,128)}, bf16[4,2,4,96,1024]{4,3,2,1,0:T(8,128)(2,1)}) custom-call(s32[1]{0:T(128)} %bitcast.40.member_ref, bf16[4,1024,1024]{2,1,0:T(8,128)(2,1)} %copy-done.5, bf16[4,1024,1024]{2,1,0:T(8,128)(2,1)} %pad_maximum_fusion.grad_ref, ...), custom_call_target="tpu_custom_call" | custom-call | flops 22817013760 | bytes 56623104 | tf_op jit(solution)/shard_map/expert/pallas_call | solution.py:411
  232.8 40.3 %expert.5 = (bf16[4,1024,1024]{2,1,0:T(8,128)(2,1)}, bf16[4,1024,1024]{2,1,0:T(8,128)(2,1)}, f32[4,1,1024]{2,1,0:T(1,128)}, bf16[4,2,4,96,1024]{4,3,2,1,0:T(8,128)(2,1)}) custom-call(s32[1]{0:T(128)} %bitcast.40.member_ref, bf16[4,1024,1024]{2,1,0:T(8,128)(2,1)} %copy-done.5, ...), custom_call_target="tpu_custom_call", output_to_operand_aliasing={{3}: (8, {})} | custom-call | flops 22817013760 | bytes 56623104 | tf_op jit(solution)/shard_map/expert/pallas_call | solution.py:411
  273.1 41.1 %expert.6 = (bf16[4,1024,1024]{2,1,0:T(8,128)(2,1)}, bf16[4,1024,1024]{2,1,0:T(8,128)(2,1)}, f32[4,1,1024]{2,1,0:T(1,128)}, bf16[4,2,4,96,1024]{4,3,2,1,0:T(8,128)(2,1)}) custom-call(s32[1]{0:T(128)} %bitcast.40.member_ref, bf16[4,1024,1024]{2,1,0:T(8,128)(2,1)} %copy-done.5, bf16[4,1024,1024]{2,1,0:T(8,128)(2,1)} %pad_maximum_fusion.grad_ref, ...), custom_call_target="tpu_custom_call" | custom-call | flops 22817013760 | bytes 56623104 | tf_op jit(solution)/shard_map/expert/pallas_call | solution.py:411
  315.4 42.9 %expert.7 = (bf16[3,1024,1024]{2,1,0:T(8,128)(2,1)}, bf16[2,1024,1024]{2,1,0:T(8,128)(2,1)}, bf16[3,1024,1024]{2,1,0:T(8,128)(2,1)}, bf16[2,1024,1024]{2,1,0:T(8...) custom-call(s32[1]{0:T(128)} %bitcast.40.member_ref, ...), custom_call_target="tpu_custom_call", output_to_operand_aliasing={{5}: (8, {})} | custom-call | flops 22817013760 | bytes 56623104 | tf_op jit(solution)/shard_map/expert/pallas_call | solution.py:411
  373.9 3.1 convert_add_fusion.3
  378.3 7.4 %collective-permute-done.35 = bf16[256,1024]{1,0:T(8,128)(2,1)S(1)} collective-permute-done((bf16[256,1024]{1,0:T(8,128)(2,1)S(1)}, bf16[256,1024]{1,0:T(8,128)(2,1)S(1)}, u32[]{:S(2)}, u32[]{:S(2)}) %collective-permute-start.35) | collective-permute-done | bytes 524320 | tf_op jit(solution)/shard_map/ppermute | solution.py:58
  389.7 8.8 %collective-permute-done.32 = bf16[256,1024]{1,0:T(8,128)(2,1)S(1)} collective-permute-done((bf16[256,1024]{1,0:T(8,128)(2,1)S(1)}, bf16[256,1024]{1,0:T(8,128)(2,1)S(1)}, u32[]{:S(2)}, u32[]{:S(2)}) %collective-permute-start.32) | collective-permute-done | bytes 524320 | tf_op jit(solution)/shard_map/ppermute | solution.py:58
  398.4 10.5 %collective-permute-done.36 = bf16[256,1024]{1,0:T(8,128)(2,1)S(1)} collective-permute-done((bf16[256,1024]{1,0:T(8,128)(2,1)S(1)}, bf16[256,1024]{1,0:T(8,128)(2,1)S(1)}, u32[]{:S(2)}, u32[]{:S(2)}) %collective-permute-start.36) | collective-permute-done | bytes 524320 | tf_op jit(solution)/shard_map/ppermute | solution.py:58
  421.1 3.0 fusion.26
  424.1 15.3 %collective-permute-done.39 = bf16[512,1024]{1,0:T(8,128)(2,1)} collective-permute-done((bf16[512,1024]{1,0:T(8,128)(2,1)S(1)}, bf16[512,1024]{1,0:T(8,128)(2,1)}, u32[]{:S(2)}, u32[]{:S(2)}) %collective-permute-start.39) | collective-permute-done | bytes 1048608 | tf_op jit(solution)/shard_map/ppermute | solution.py:58
  453.2 26.6 %attention_backward.1 = bf16[1024,1024]{1,0:T(8,128)(2,1)} custom-call(bf16[1024,1024]{1,0:T(8,128)(2,1)} %get-tuple-element.154.rot_ref, bf16[1024,512]{1,0:T(8,128)(2,1)} %convolution_convert_fusion.grad_ref, f32[1024,512]{1,0:T(8,128)} %get-tuple-element.159.lse_ref, f32[1024,128]{1,0:T(8,128)} %get-tuple-element.103.cos_ref, ...), custom_call_target="tpu_custom_call" | custom-call | flops 8589934592 | bytes 10485760 | tf_op jit(solution)/shard_map/attention_backward/pallas_call | solution.py:288
  492.2 9.3 %collective-permute-done.46 = bf16[2,2,96,1024]{3,2,1,0:T(8,128)(2,1)S(1)} collective-permute-done((bf16[2,2,96,1024]{3,2,1,0:T(8,128)(2,1)S(1)}, bf16[2,2,96,1024]{3,2,1,0:T(8,128)(2,1)S(1)}, u32[]{:S(2)}, u32[]{:S(2)}) %collective-permute-start.46) | collective-permute-done | bytes 786464 | tf_op jit(solution)/shard_map/ppermute | solution.py:58
  502.9 11.2 %collective-permute-done.43 = bf16[512,1024]{1,0:T(8,128)(2,1)S(1)} collective-permute-done((bf16[512,1024]{1,0:T(8,128)(2,1)S(1)}, bf16[512,1024]{1,0:T(8,128)(2,1)S(1)}, u32[]{:S(2)}, u32[]{:S(2)}) %collective-permute-start.43) | collective-permute-done | bytes 1048608 | tf_op jit(solution)/shard_map/ppermute | solution.py:58
  521.5 3.0 collective-permute-done.48
  525.4 10.8 %collective-permute-done.49 = bf16[4,64,1024]{2,1,0:T(8,128)(2,1)S(1)} collective-permute-done((bf16[4,64,1024]{2,1,0:T(8,128)(2,1)S(1)}, bf16[4,64,1024]{2,1,0:T(8,128)(2,1)S(1)}, u32[]{:S(2)}, u32[]{:S(2)}) %collective-permute-start.49) | collective-permute-done | bytes 524320 | tf_op jit(solution)/shard_map/ppermute | solution.py:58
  544.3 4.2 fusion.19
  548.4 7.8 %collective-permute-done.54 = f32[34,1024]{1,0:T(8,128)S(1)} collective-permute-done((f32[34,1024]{1,0:T(8,128)S(1)}, f32[34,1024]{1,0:T(8,128)S(1)}, u32[]{:S(2)}, u32[]{:S(2)}) %collective-permute-start.54) | collective-permute-done | bytes 139296 | tf_op jit(solution)/shard_map/ppermute | solution.py:720
  556.8 3.0 collective-permute-start.56
  561.5 10.0 %collective-permute-done.56 = f32[34,1024]{1,0:T(8,128)S(1)} collective-permute-done((f32[34,1024]{1,0:T(8,128)S(1)}, f32[34,1024]{1,0:T(8,128)S(1)}, u32[]{:S(2)}, u32[]{:S(2)}) %collective-permute-start.56) | collective-permute-done | bytes 139296 | tf_op jit(solution)/shard_map/ppermute | solution.py:720
  (344 shorter events, 170.3 us)
Async XLA Ops:
  7.2 66.3 %all-gather.8.cloned.1.call-start = ((), (), s32[]{:S(2)}) async-start(), calls=%async_computation.2 | async-start | bytes 2228224 | tf_op jit(solution)/shard_map/all_gather | solution.py:487
  9.9 183.6 %all-gather.14.cloned.1.call-start = ((), (), s32[]{:S(2)}) async-start(), calls=%async_computation.7 | async-start | bytes 7864320 | tf_op jit(solution)/shard_map/all_gather | solution.py:558
  9.9 21.7 %collective-permute-start.5 = (bf16[1,64,512]{2,1,0:T(8,128)(2,1)}, bf16[1,64,512]{2,1,0:T(8,128)(2,1)S(1)}, u32[]{:S(2)}, u32[]{:S(2)}) collective-permute-start(bf16[1,64,512]{2,1,0:T(8,128)(2,1)} %bitcast.290), channel_id=1, source_target_pairs={{0,8},{8,0},{16,24},{24,16},{1,9},{9,1},{17,25},{25,17},{2,10},{10... | collective-permute-start | bytes 196616 | tf_op jit(solution)/shard_map/ppermute | solution.py:491
  16.6 24.9 %collective-permute-start = (bf16[512,1024]{1,0:T(8,128)(2,1)}, bf16[512,1024]{1,0:T(8,128)(2,1)}, u32[]{:S(2)}, u32[]{:S(2)}) collective-permute-start(bf16[512,1024]{1,0:T(8,128)(2,1)} %fusion.7), channel_id=1, source_target_pairs={{0,1},{1,0},{2,3},{3,2},{4,5},{5,4},{6,7},{7,6},{8,9},{9,8},{10,11... | collective-permute-start | bytes 3145736 | tf_op jit(solution)/shard_map/ppermute | solution.py:58
  22.0 42.4 %collective-permute-start.2 = (bf16[2,96,1024]{2,1,0:T(8,128)(2,1)}, bf16[2,96,1024]{2,1,0:T(8,128)(2,1)}, u32[]{:S(2)}, u32[]{:S(2)}) collective-permute-start(bf16[2,96,1024]{2,1,0:T(8,128)(2,1)} %get-tuple-element.228), channel_id=1, source_target_pairs={{0,2},{2,0},{1,3},{3,1},{4,6},{6,4},{5,7},{7,5},{8,10},{10,8},{9,1... | collective-permute-start | bytes 1179656 | tf_op jit(solution)/shard_map/ppermute | solution.py:58
  23.7 48.5 %collective-permute-start.9 = (bf16[2,1,96,1024]{3,2,1,0:T(8,128)(2,1)}, bf16[2,1,96,1024]{3,2,1,0:T(8,128)(2,1)}, u32[]{:S(2)}, u32[]{:S(2)}) collective-permute-start(bf16[2,1,96,1024]{3,2,1,0:T(8,128)(2,1)} %get-tuple-element.221), channel_id=1, source_target_pairs={{0,4},{4,0},{1,5},{5,1},{2,6},{6,2},{3,7},{7,3},{8,12},{12,8},{9,1... | collective-permute-start | bytes 1179656 | tf_op jit(solution)/shard_map/ppermute | solution.py:58
  26.2 32.3 %collective-permute-start.3 = (bf16[2,2,96,1024]{3,2,1,0:T(8,128)(2,1)}, bf16[2,2,96,1024]{3,2,1,0:T(8,128)(2,1)}, u32[]{:S(2)}, u32[]{:S(2)}) collective-permute-start(bf16[2,2,96,1024]{3,2,1,0:T(8,128)(2,1)} %slice.225), channel_id=1, source_target_pairs={{0,4},{4,0},{1,5},{5,1},{2,6},{6,2},{3,7},{7,3},{8,12},{12,8},{9,1... | collective-permute-start | bytes 2359304 | tf_op jit(solution)/shard_map/ppermute | solution.py:58
  44.8 24.1 %collective-permute-start.1 = (bf16[512,1024]{1,0:T(8,128)(2,1)}, bf16[512,1024]{1,0:T(8,128)(2,1)}, u32[]{:S(2)}, u32[]{:S(2)}) collective-permute-start(bf16[512,1024]{1,0:T(8,128)(2,1)} %fusion.6), channel_id=1, source_target_pairs={{0,1},{1,0},{2,3},{3,2},{4,5},{5,4},{6,7},{7,6},{8,9},{9,8},{10,11... | collective-permute-start | bytes 3145736 | tf_op jit(solution)/shard_map/ppermute | solution.py:58
  73.5 199.6 %all-gather.12.cloned.1.call-start = ((), (), s32[]{:S(2)}) async-start(), calls=%async_computation.6 | async-start | bytes 3932160 | tf_op jit(solution)/shard_map/all_gather | solution.py:558
  75.3 24.6 %collective-permute-start.11 = (bf16[4,2,64,512]{3,2,1,0:T(8,128)(2,1)S(1)}, bf16[4,2,64,512]{3,2,1,0:T(8,128)(2,1)}, u32[]{:S(2)}, u32[]{:S(2)}) collective-permute-start(bf16[4,2,64,512]{3,2,1,0:T(8,128)(2,1)S(1)} %pad_maximum_fusion.16), channel_id=1, source_target_pairs={{0,2},{2,0},{1,3},{3,1},{4,6},{6,4},{5,7},{7,5},{8,10},{10,8},{9,1... | collective-permute-start | bytes 1572872 | tf_op jit(solution)/shard_map/ppermute | solution.py:58
  81.9 49.8 %collective-permute-start.13 = (bf16[1024,1024]{1,0:T(8,128)(2,1)}, bf16[1024,1024]{1,0:T(8,128)(2,1)}, u32[]{:S(2)}, u32[]{:S(2)}) collective-permute-start(bf16[1024,1024]{1,0:T(8,128)(2,1)} %pad_maximum_fusion.4), channel_id=1, source_target_pairs={{0,4},{4,0},{1,5},{5,1},{2,6},{6,2},{3,7},{7,3},{8,12},{12,8},{9,1... | collective-permute-start | bytes 6291464 | tf_op jit(solution)/shard_map/ppermute | solution.py:58
  104.0 25.6 %collective-permute-start.12 = (bf16[512,1024]{1,0:T(8,128)(2,1)}, bf16[512,1024]{1,0:T(8,128)(2,1)}, u32[]{:S(2)}, u32[]{:S(2)}) collective-permute-start(bf16[512,1024]{1,0:T(8,128)(2,1)} %dynamic-slice_convert_fusion.1), channel_id=1, source_target_pairs={{0,1},{1,0},{2,3},{3,2},{4,5},{5,4},{6,7},{7,6},{8,9},{9,8},{10,11... | collective-permute-start | bytes 3145736 | tf_op jit(solution)/shard_map/ppermute | solution.py:58
  109.6 25.5 %collective-permute-start.22 = (bf16[1024,1024]{1,0:T(8,128)(2,1)}, bf16[1024,1024]{1,0:T(8,128)(2,1)}, u32[]{:S(2)}, u32[]{:S(2)}) collective-permute-start(bf16[1024,1024]{1,0:T(8,128)(2,1)} %pad_maximum_fusion.4), channel_id=1, source_target_pairs={{0,2},{2,0},{1,3},{3,1},{4,6},{6,4},{5,7},{7,5},{8,10},{10,8},{9,1... | collective-permute-start | bytes 6291464 | tf_op jit(solution)/shard_map/ppermute | solution.py:58
  131.9 183.5 %all-gather.10.cloned.1.call-start = ((), (), s32[]{:S(2)}) async-start(), calls=%async_computation.5 | async-start | bytes 3932160 | tf_op jit(solution)/shard_map/all_gather | solution.py:558
  132.8 25.6 %collective-permute-start.21 = (bf16[512,1024]{1,0:T(8,128)(2,1)S(1)}, bf16[512,1024]{1,0:T(8,128)(2,1)S(1)}, u32[]{:S(2)}, u32[]{:S(2)}) collective-permute-start(bf16[512,1024]{1,0:T(8,128)(2,1)S(1)} %multiply_convert_fusion.1), channel_id=1, source_target_pairs={{0,4},{4,0},{1,5},{5,1},{2,6},{6,2},{3,7},{7,3},{8,12},{12,8},{9,1... | collective-permute-start | bytes 3145736 | tf_op jit(solution)/shard_map/ppermute | solution.py:58
  134.4 25.3 %collective-permute-start.20 = (bf16[512,1024]{1,0:T(8,128)(2,1)S(1)}, bf16[512,1024]{1,0:T(8,128)(2,1)S(1)}, u32[]{:S(2)}, u32[]{:S(2)}) collective-permute-start(bf16[512,1024]{1,0:T(8,128)(2,1)S(1)} %multiply_convert_fusion.1), channel_id=1, source_target_pairs={{0,1},{1,0},{2,3},{3,2},{4,5},{5,4},{6,7},{7,6},{8,9},{9,8},{10,11... | collective-permute-start | bytes 3145736 | tf_op jit(solution)/shard_map/ppermute | solution.py:58
  179.8 269.7 %reduce-scatter.3.cloned.1.call-start = ((), (), s32[]{:S(2)}) async-start(), calls=%async_computation.3 | async-start | bytes 7864320 | tf_op jit(solution)/shard_map/reduce_scatter | solution.py:603
  273.1 267.4 %reduce-scatter.5.cloned.1.call-start = ((), (), s32[]{:S(2)}) async-start(), calls=%async_computation.4 | async-start | bytes 7864320 | tf_op jit(solution)/shard_map/reduce_scatter | solution.py:603
  368.7 42.7 %collective-permute-start.38 = (bf16[2,1024,1024]{2,1,0:T(8,128)(2,1)}, bf16[2,1024,1024]{2,1,0:T(8,128)(2,1)}, u32[]{:S(2)}, u32[]{:S(2)}) collective-permute-start(bf16[2,1024,1024]{2,1,0:T(8,128)(2,1)} %get-tuple-element.151), channel_id=1, source_target_pairs={{0,2},{2,0},{1,3},{3,1},{4,6},{6,4},{5,7},{7,5},{8,10},{10,8},{9,1... | collective-permute-start | bytes 12582920 | tf_op jit(solution)/shard_map/ppermute | solution.py:58
  377.0 21.4 %collective-permute-start.32 = (bf16[256,1024]{1,0:T(8,128)(2,1)S(1)}, bf16[256,1024]{1,0:T(8,128)(2,1)S(1)}, u32[]{:S(2)}, u32[]{:S(2)}) collective-permute-start(bf16[256,1024]{1,0:T(8,128)(2,1)S(1)} %fusion.41), channel_id=1, source_target_pairs={{0,1},{1,0},{2,3},{3,2},{4,5},{5,4},{6,7},{7,6},{8,9},{9,8},{10,11... | collective-permute-start | bytes 1572872 | tf_op jit(solution)/shard_map/ppermute | solution.py:58
  377.8 20.6 %collective-permute-start.33 = (bf16[256,1024]{1,0:T(8,128)(2,1)S(1)}, bf16[256,1024]{1,0:T(8,128)(2,1)S(1)}, u32[]{:S(2)}, u32[]{:S(2)}) collective-permute-start(bf16[256,1024]{1,0:T(8,128)(2,1)S(1)} %fusion.42), channel_id=1, source_target_pairs={{0,4},{4,0},{1,5},{5,1},{2,6},{6,2},{3,7},{7,3},{8,12},{12,8},{9,1... | collective-permute-start | bytes 1572872 | tf_op jit(solution)/shard_map/ppermute | solution.py:58
  387.5 21.4 %collective-permute-start.36 = (bf16[256,1024]{1,0:T(8,128)(2,1)S(1)}, bf16[256,1024]{1,0:T(8,128)(2,1)S(1)}, u32[]{:S(2)}, u32[]{:S(2)}) collective-permute-start(bf16[256,1024]{1,0:T(8,128)(2,1)S(1)} %fusion.31), channel_id=1, source_target_pairs={{0,1},{1,0},{2,3},{3,2},{4,5},{5,4},{6,7},{7,6},{8,9},{9,8},{10,11... | collective-permute-start | bytes 1572872 | tf_op jit(solution)/shard_map/ppermute | solution.py:58
  389.0 19.9 %collective-permute-start.37 = (bf16[256,1024]{1,0:T(8,128)(2,1)S(1)}, bf16[256,1024]{1,0:T(8,128)(2,1)S(1)}, u32[]{:S(2)}, u32[]{:S(2)}) collective-permute-start(bf16[256,1024]{1,0:T(8,128)(2,1)S(1)} %fusion.29), channel_id=1, source_target_pairs={{0,4},{4,0},{1,5},{5,1},{2,6},{6,2},{3,7},{7,3},{8,12},{12,8},{9,1... | collective-permute-start | bytes 1572872 | tf_op jit(solution)/shard_map/ppermute | solution.py:58
  414.7 24.6 %collective-permute-start.39 = (bf16[512,1024]{1,0:T(8,128)(2,1)S(1)}, bf16[512,1024]{1,0:T(8,128)(2,1)}, u32[]{:S(2)}, u32[]{:S(2)}) collective-permute-start(bf16[512,1024]{1,0:T(8,128)(2,1)S(1)} %get-tuple-element.187), channel_id=1, source_target_pairs={{0,1},{1,0},{2,3},{3,2},{4,5},{5,4},{6,7},{7,6},{8,9},{9,8},{10,11... | collective-permute-start | bytes 3145736 | tf_op jit(solution)/shard_map/ppermute | solution.py:58
  419.1 24.6 %collective-permute-start.40 = (bf16[512,1024]{1,0:T(8,128)(2,1)}, bf16[512,1024]{1,0:T(8,128)(2,1)}, u32[]{:S(2)}, u32[]{:S(2)}) collective-permute-start(bf16[512,1024]{1,0:T(8,128)(2,1)} %fusion.25), channel_id=1, source_target_pairs={{0,4},{4,0},{1,5},{5,1},{2,6},{6,2},{3,7},{7,3},{8,12},{12,8},{9,1... | collective-permute-start | bytes 3145736 | tf_op jit(solution)/shard_map/ppermute | solution.py:58
  446.2 78.4 %collective-permute-start.51 = (bf16[512,1024]{1,0:T(8,128)(2,1)S(1)}, bf16[512,1024]{1,0:T(8,128)(2,1)}, u32[]{:S(2)}, u32[]{:S(2)}) collective-permute-start(bf16[512,1024]{1,0:T(8,128)(2,1)S(1)} %fusion.15), channel_id=1, source_target_pairs={{0,1},{1,0},{2,3},{3,2},{4,5},{5,4},{6,7},{7,6},{8,9},{9,8},{10,11... | collective-permute-start | bytes 3145736 | tf_op jit(solution)/shard_map/ppermute | solution.py:58
  446.8 34.7 %collective-permute-start.41 = (bf16[512,1024]{1,0:T(8,128)(2,1)}, bf16[512,1024]{1,0:T(8,128)(2,1)}, u32[]{:S(2)}, u32[]{:S(2)}) collective-permute-start(bf16[512,1024]{1,0:T(8,128)(2,1)} %fusion.26), channel_id=1, source_target_pairs={{0,4},{4,0},{1,5},{5,1},{2,6},{6,2},{3,7},{7,3},{8,12},{12,8},{9,1... | collective-permute-start | bytes 3145736 | tf_op jit(solution)/shard_map/ppermute | solution.py:58
  453.2 26.6 %collective-permute-start.42 = (bf16[2,2,96,1024]{3,2,0,1:T(8,128)(2,1)}, bf16[2,2,96,1024]{3,2,0,1:T(8,128)(2,1)}, u32[]{:S(2)}, u32[]{:S(2)}) collective-permute-start(bf16[2,2,96,1024]{3,2,0,1:T(8,128)(2,1)} %slice_bitcast_fusion.4), channel_id=1, source_target_pairs={{0,2},{2,0},{1,3},{3,1},{4,6},{6,4},{5,7},{7,5},{8,10},{10,8},{9,1... | collective-permute-start | bytes 2359304 | tf_op jit(solution)/shard_map/ppermute | solution.py:58
  481.5 20.0 %collective-permute-start.46 = (bf16[2,2,96,1024]{3,2,1,0:T(8,128)(2,1)S(1)}, bf16[2,2,96,1024]{3,2,1,0:T(8,128)(2,1)S(1)}, u32[]{:S(2)}, u32[]{:S(2)}) collective-permute-start(bf16[2,2,96,1024]{3,2,1,0:T(8,128)(2,1)S(1)} %slice_bitcast_fusion.7), channel_id=1, source_target_pairs={{0,4},{4,0},{1,5},{5,1},{2,6},{6,2},{3,7},{7,3},{8,12},{12,8},{9,1... | collective-permute-start | bytes 2359304 | tf_op jit(solution)/shard_map/ppermute | solution.py:58
  488.5 25.6 %collective-permute-start.43 = (bf16[512,1024]{1,0:T(8,128)(2,1)S(1)}, bf16[512,1024]{1,0:T(8,128)(2,1)S(1)}, u32[]{:S(2)}, u32[]{:S(2)}) collective-permute-start(bf16[512,1024]{1,0:T(8,128)(2,1)S(1)} %dynamic-slice_convert_fusion), channel_id=1, source_target_pairs={{0,1},{1,0},{2,3},{3,2},{4,5},{5,4},{6,7},{7,6},{8,9},{9,8},{10,11... | collective-permute-start | bytes 3145736 | tf_op jit(solution)/shard_map/ppermute | solution.py:58
  490.2 24.4 %collective-permute-start.44 = (bf16[4,2,64,1024]{3,2,0,1:T(8,128)(2,1)S(1)}, bf16[4,2,64,1024]{3,2,0,1:T(8,128)(2,1)S(1)}, u32[]{:S(2)}, u32[]{:S(2)}) collective-permute-start(bf16[4,2,64,1024]{3,2,0,1:T(8,128)(2,1)S(1)} %fusion.27), channel_id=1, source_target_pairs={{0,2},{2,0},{1,3},{3,1},{4,6},{6,4},{5,7},{7,5},{8,10},{10,8},{9,1... | collective-permute-start | bytes 3145736 | tf_op jit(solution)/shard_map/ppermute | solution.py:58
  491.8 22.7 %collective-permute-start.45 = (bf16[4,2,64,512]{3,2,0,1:T(8,128)(2,1)S(1)}, bf16[4,2,64,512]{3,2,0,1:T(8,128)(2,1)S(1)}, u32[]{:S(2)}, u32[]{:S(2)}) collective-permute-start(bf16[4,2,64,512]{3,2,0,1:T(8,128)(2,1)S(1)} %fusion.40), channel_id=1, source_target_pairs={{0,2},{2,0},{1,3},{3,1},{4,6},{6,4},{5,7},{7,5},{8,10},{10,8},{9,1... | collective-permute-start | bytes 1572872 | tf_op jit(solution)/shard_map/ppermute | solution.py:58
  (78 other events, 943.0 us)
Sparse Core Ops, SparseCore 0:
  10.8 49.7 all-gather.7
  73.7 114.9 all-gather.13
  190.2 61.6 all-gather.11
  253.3 62.0 all-gather.9
  317.6 109.4 reduce-scatter.2
  429.2 111.2 reduce-scatter.4
